TPU v7x, 128 devices: a whole 4x4x4 slice. The times are simulated.
128 devices in a mesh: layer: 32 (over x, y, core), rows: 4 (over z).
Axes of the slice: x: 4, y: 4, z: 4, core: 2. Of those that a mesh axis runs over, the one named last changes fastest.
Arguments:
- weights: bfloat16 [256, 32, 288], P('layer'), may hold values from -0.375 to 0.375
- image: float32 [3, 32, 64, 128], P(None, None, 'rows'), may hold values from -6 to 6
- guess: float32 [64, 3, 32, 64, 128], P('layer', None, None, 'rows'), may hold values from -6 to 6
Outputs:
- corrected: float32 [64, 3, 32, 64, 128], P('layer', None, None, 'rows')
All inputs are finite; a program needn't handle non-finite values.
Results may differ from a plain program's by a relative error of at most 0.009.
Values may be sent and summed in bfloat16 or wider, within the bound.
No kernel may reach another device: no remote copies, remote signals or barrier semaphores. Data moves between devices by JAX's collectives and lax.ppermute only.
A program may use at most 64 MiB of HBM per device.

v0:
```python
import functools

import jax
import jax.numpy as jnp
from jax import lax
from jax.experimental import pallas as pl
from jax.experimental.pallas import tpu as pltpu
from jax.sharding import PartitionSpec as P


M = 4
H = 0.125
C = 32
W = 128
BAND = 16
SUB = 8
STEPS = 2 * SUB
IMAGES = 3
WIN = 3 * BAND
REACH = 4
SPAN = BAND + 2 * REACH
EDGE = [BAND - (s + 1) // 2 * 2 for s in range(STEPS)]
OFFSET = [sum(EDGE[:s]) for s in range(STEPS)]
HALO = sum(EDGE)
CHUNK = 2 * BAND + 6
bf16 = jnp.bfloat16
f32 = jnp.float32


FLOW = 4
HALVES = 2
LEAD = sum(EDGE[: STEPS // 2])


def home(b):
    return (0, 2, 6)[b]


def banded(tiles):
    lane = lax.broadcasted_iota(jnp.int32, (C, W), 1)
    keep = lane < 3 * C
    last, columns = jnp.zeros((C, W), bf16), []
    for tile in tiles:
        turned = pltpu.roll(tile, 3 * C, 1)
        columns.append(jnp.concatenate([tile, jnp.where(keep, last, turned)], axis=0))
        last = turned
    return jnp.concatenate(columns, axis=1)


def spread(xs, buf, row, value):
    lane = lax.broadcasted_iota(jnp.int32, (2 * C, W), 1)
    value = value.astype(bf16)
    left = jnp.where(lane == 0, bf16(0), pltpu.roll(value, 1, 1))
    right = jnp.where(lane == W - 1, bf16(0), pltpu.roll(value, W - 1, 1))
    for dc, v in enumerate((left, value, right)):
        xs[buf, row : row + 2, dc] = v.reshape(2, C, W)


def block(xs, buf, matrix, row):
    a = xs[buf, row : row + 4].reshape(12 * C, W)
    b = xs[buf, row + 2 : row + 6].reshape(12 * C, W)
    rhs = jnp.concatenate([a, b], axis=1)
    z = jnp.dot(matrix, rhs, preferred_element_type=f32)
    return jnp.tanh(z[:, :W]), jnp.tanh(z[:, W:])


def clear_rims(xs, rows):
    for buf in range(xs.shape[0]):
        for row in (0, rows + 1):
            xs[buf, row] = jnp.zeros((3, C, W), bf16)


def drain(source, targets, sems):
    copies = [pltpu.make_async_copy(source.at[r], target, sems.at[r]) for r, target in enumerate(targets)]
    for copy in copies:
        copy.start()
    for copy in copies:
        copy.wait()


def relax_kernel(info_ref, own_ref, up_ref, dn_ref, img_ref, here_ref, next_ref, open_ref, *refs):
    outs, (v1_ref, xs, state, base, slots, sems) = refs[:FLOW], refs[FLOW:]
    z, turn, lead = info_ref[0], info_ref[1], info_ref[2]

    def tiles(ref, n):
        tail = jnp.concatenate([ref[n, :, 2 * W :], jnp.zeros((C, 3 * C), bf16)], axis=1)
        return [ref[n, :, :W], ref[n, :, W : 2 * W], tail]

    def tap(point, j):
        return tiles(next_ref, j) if point else tiles(here_ref, M + j)

    clear_rims(xs, SPAN)
    low_ok = jnp.where(z > 0, 1.0, 0.0)
    high_ok = jnp.where(z < 3, 1.0, 0.0)

    def put(buf, pair, value):
        if pair < REACH // 2:
            value = value * low_ok
        elif pair >= (REACH + BAND) // 2:
            value = value * high_ok
        spread(xs, buf, 2 * pair + 1, value)

    def load(lane_set, u):
        for pair in range(SPAN // 2):
            r = 2 * pair
            if r < REACH:
                x = up_ref[u, r : r + 2]
            elif r >= REACH + BAND:
                x = dn_ref[u, r - REACH - BAND : r - REACH - BAND + 2]
            else:
                ref, at = (img_ref, 0) if isinstance(u, int) else (own_ref, u * (C * BAND))
                x = [ref[pl.ds(at + r - REACH + k, C, stride=BAND), :] for k in range(2)]
                x = jnp.concatenate(x, axis=0).astype(bf16)
            x = x.astype(f32).reshape(2 * C, W)
            state[lane_set, r : r + 2] = x.reshape(2, C, W)
            put(2 * lane_set, pair, x)

    def layer(lane_set, j, matrix):
        lo = (j + 1) // 2 * 2
        for row in range(lo, SPAN - lo, 4):
            for i, t in enumerate(block(xs, 2 * lane_set + j % 2, matrix, row)):
                r = row + 2 * i
                x = state[lane_set, r : r + 2].reshape(2 * C, W)
                if j == 0 and REACH <= r < REACH + BAND:
                    base[lane_set, r - REACH : r - REACH + 2] = (x + (M * H) * t).reshape(2, C, W)
                x = x + H * t
                state[lane_set, r : r + 2] = x.reshape(2, C, W)
                if j < M - 1:
                    put(2 * lane_set + (j + 1) % 2, r // 2, x)

    def image(b, carry):
        for point in range(2):
            load(point, point * IMAGES + b)
        for j in range(M):
            for point in range(2):
                layer(point, j, banded(tap(point, j)))
        slot = lax.rem(turn - b + FLOW, FLOW)
        for point in range(2):
            change = state[point, REACH : REACH + BAND] - base[point]
            slots[slot, point * BAND : (point + 1) * BAND] = change.astype(bf16)
            for t, tile in enumerate(tap(point, 0)):
                slots[slot, 2 * BAND + 3 * point + t] = tile
        return carry

    lax.fori_loop(0, IMAGES, image, 0)

    @pl.when(lead == 1)
    def _():
        load(0, 2 * IMAGES)
        for j in range(M):
            layer(0, j, banded(tiles(open_ref, j)))
        for r in range(BAND):
            x = img_ref[pl.ds(r, C, stride=BAND), :]
            v1_ref[r] = x + (state[0, REACH + r] - x.astype(bf16).astype(f32))

    drain(slots, outs, sems)


def rim_kernel(half, b_ref, *refs):
    chunks, rest = refs[:FLOW], refs[FLOW:]
    if half == 0:
        v1_ref, up_ref, dn_ref, d_ref = rest
        v1 = v1_ref[...].astype(bf16)
        up_ref[LEAD:] = v1
        dn_ref[LEAD:] = v1
    else:
        up_ref, dn_ref, d_ref = rest
    for k in range(FLOW):
        at = lax.rem(b_ref[0] + k, FLOW)
        for p in range(2):
            d_ref[2 * at + p] = chunks[k][p * BAND : (p + 1) * BAND]
    for s in range(SUB):
        rows, to = EDGE[SUB * half + s], OFFSET[SUB * half + s] - half * LEAD
        if rows:
            up_ref[to : to + rows] = d_ref[s, BAND - rows :]
            dn_ref[to : to + rows] = d_ref[s, :rows]


def order_kernel(b_ref, *refs):
    chunks, (d_ref, w_ref) = refs[:SUB], refs[SUB:]
    for r in range(SUB):
        at = SUB // 2 * (r // FLOW) + lax.rem(b_ref[0] + r % FLOW, FLOW)
        for p in range(2):
            d_ref[2 * at + p] = chunks[r][p * BAND : (p + 1) * BAND]
            w_ref[2 * at + p] = chunks[r][2 * BAND + 3 * p : 2 * BAND + 3 * p + 3]


def finish_kernel(info_ref, *refs):
    arrived, (out_ref, picked, stage, sems) = refs[:SUB], refs[SUB:]
    turn, half = info_ref[1], info_ref[4]
    for b in range(IMAGES):
        want = lax.rem(turn - b + FLOW, FLOW) + FLOW * half
        for r in range(SUB):

            @pl.when(want == r)
            def _():
                pltpu.make_async_copy(arrived[r], picked.at[b], sems.at[b]).start()

    for b in range(IMAGES):
        pltpu.make_async_copy(arrived[0], picked.at[b], sems.at[b]).wait()
        for p in range(2):
            stage[b, p] = picked[b, p].astype(f32).reshape(BAND * C, W)
            for c in range(C):
                to = ((p * IMAGES + b) * C + c) * BAND
                out_ref[to : to + BAND] = stage[b, p, pl.ds(c, BAND, stride=C), :]


def sweep_kernel(
    opening, closing, info_ref, v1_ref, d_ref, up0_ref, dn0_ref, up1_ref, dn1_ref, w_ref, *refs
):
    if not opening:
        (own_ref, above_ref, below_ref), refs = refs[:3], refs[3:]
    if closing:
        outs, (xs, state, res_ref, sems) = refs[:SUB], refs[SUB:]
    else:
        out_ref, edge_ref, xs, state = refs
    z, first, b = info_ref[0], info_ref[2], info_ref[3]
    clear_rims(xs, WIN)
    low_ok = jnp.where(z > 0, 1.0, 0.0)
    high_ok = jnp.where(z < 3, 1.0, 0.0)

    def put(buf, row, value):
        if row < BAND:
            value = value * low_ok
        elif row >= 2 * BAND:
            value = value * high_ok
        spread(xs, buf, row + 1, value)

    def begin():
        state[:BAND] = up0_ref[LEAD:].astype(f32)
        state[BAND : 2 * BAND] = v1_ref[...]
        state[2 * BAND :] = dn0_ref[LEAD:].astype(f32)

    def resume():
        state[:BAND] = above_ref[...].astype(f32)
        state[BAND : 2 * BAND] = own_ref[...]
        state[2 * BAND :] = below_ref[...].astype(f32)

    if opening:
        begin()
    else:
        pl.when(first == 1)(begin)
        pl.when(first == 0)(resume)

    for row in range(0, WIN, 2):
        put(0, row, state[row : row + 2].reshape(2 * C, W))

    for s, rows in enumerate(EDGE):
        now = s % 2
        half = s // SUB
        if closing:
            res_ref[FLOW * half + lax.rem(s // 2 % FLOW - b + FLOW, FLOW), now] = xs[now, BAND + 1 : 2 * BAND + 1, 1]
            if s == STEPS - 1:
                break
        matrix = banded([w_ref[s, t] for t in range(3)])
        up_ref, dn_ref = (up1_ref, dn1_ref) if half else (up0_ref, dn0_ref)
        for row in range(BAND - rows, 2 * BAND + rows, 4):
            for k, t in enumerate(block(xs, now, matrix, row)):
                r = row + 2 * k
                if r < BAND:
                    at = OFFSET[s] - half * LEAD + r - (BAND - rows)
                    d = up_ref[at : at + 2]
                elif r < 2 * BAND:
                    d = d_ref[s, r - BAND : r - BAND + 2]
                else:
                    at = OFFSET[s] - half * LEAD + r - 2 * BAND
                    d = dn_ref[at : at + 2]
                x = state[r : r + 2].reshape(2 * C, W) + ((M * H) * t + d.astype(f32).reshape(2 * C, W))
                state[r : r + 2] = x.reshape(2, C, W)
                if s < STEPS - 1:
                    put(1 - now, r, x)
    if closing:
        drain(res_ref, outs, sems)
    else:
        out_ref[...] = state[BAND : 2 * BAND]
        edge_ref[...] = state[BAND : 2 * BAND].astype(bf16)


VM = pl.BlockSpec(memory_space=pltpu.VMEM)
SM = pl.BlockSpec(memory_space=pltpu.SMEM)
AN = pl.BlockSpec(memory_space=pl.ANY)


def shape(*dims, dtype=bf16):
    return jax.ShapeDtypeStruct(dims, dtype)


def relax(info, *arrays):
    outs = pl.pallas_call(
        relax_kernel,
        out_shape=(shape(CHUNK, C, W),) * FLOW + (shape(BAND, C, W, dtype=f32),),
        in_specs=[SM] + [VM] * 7,
        out_specs=(AN,) * FLOW + (VM,),
        scratch_shapes=[
            pltpu.VMEM((4, SPAN + 2, 3, C, W), bf16),
            pltpu.VMEM((2, SPAN, C, W), f32),
            pltpu.VMEM((2, BAND, C, W), f32),
            pltpu.VMEM((FLOW, CHUNK, C, W), bf16),
            pltpu.SemaphoreType.DMA((FLOW,)),
        ],
        name="relax",
    )(info, *arrays)
    return outs[:FLOW], outs[FLOW]


def rims(half, b, *arrays):
    total = HALO - LEAD if half else LEAD + BAND
    return pl.pallas_call(
        functools.partial(rim_kernel, half),
        out_shape=(shape(total, C, W),) * 2,
        in_specs=[SM] + [VM] * len(arrays),
        out_specs=(VM, VM),
        scratch_shapes=[pltpu.VMEM((SUB, BAND, C, W), bf16)],
    )(b, *arrays)


def finish(info, arrays):
    return pl.pallas_call(
        finish_kernel,
        out_shape=shape(2 * IMAGES * C * BAND, W, dtype=f32),
        in_specs=[SM] + [AN] * SUB,
        out_specs=VM,
        scratch_shapes=[
            pltpu.VMEM((IMAGES, 2, BAND, C, W), bf16),
            pltpu.VMEM((IMAGES, 2, BAND * C, W), f32),
            pltpu.SemaphoreType.DMA((IMAGES,)),
        ],
        name="finish",
    )(info, *arrays)


def order(sub, chunks):
    return pl.pallas_call(
        order_kernel,
        out_shape=(shape(STEPS, BAND, C, W), shape(STEPS, 3, C, W)),
        in_specs=[SM] + [VM] * SUB,
        out_specs=(VM, VM),
        cost_estimate=pl.CostEstimate(flops=0, bytes_accessed=5_000_000, transcendentals=0),
        name="order",
    )(sub, *chunks)


def sweep(opening, closing, info, *arrays):
    if closing:
        out_shape = (shape(2, BAND, C, W),) * SUB
        extra = [pltpu.VMEM((SUB, 2, BAND, C, W), bf16), pltpu.SemaphoreType.DMA((SUB,))]
    else:
        out_shape = (shape(BAND, C, W, dtype=f32), shape(BAND, C, W))
        extra = []
    return pl.pallas_call(
        functools.partial(sweep_kernel, opening, closing),
        out_shape=out_shape,
        in_specs=[SM] + [VM] * len(arrays),
        out_specs=(AN,) * SUB if closing else (VM, VM),
        scratch_shapes=[pltpu.VMEM((2, WIN + 2, 3, C, W), bf16), pltpu.VMEM((WIN, C, W), f32)] + extra,
        name="sweep",
    )(info, *arrays)


def cycle(weights, image, guess):
    layers, rows = lax.axis_size("layer"), lax.axis_size("rows")
    groups = layers // SUB
    l, z = lax.axis_index("layer"), lax.axis_index("rows")
    sub, group = lax.rem(l, SUB), l // SUB
    mine = jnp.where(sub == home(1), 1, jnp.where(sub == home(2), 2, 0))

    own_image = lax.dynamic_index_in_dim(image, mine, 0, keepdims=False)
    flat = guess.reshape(2 * IMAGES, C, BAND, W)

    def edge_rows(first):
        rim = jnp.concatenate([flat[:, :, first : first + REACH], own_image[None, :, first : first + REACH]], axis=0)
        return rim.transpose(0, 2, 1, 3).astype(bf16)

    small = weights[:M]
    up = lax.ppermute(edge_rows(BAND - REACH), "rows", [(i, i + 1) for i in range(rows - 1)])
    dn = lax.ppermute(edge_rows(0), "rows", [(i + 1, i) for i in range(rows - 1)])
    following = lax.ppermute(small, "layer", [(i + 1, i) for i in range(layers - 1)])
    opening = small
    for b in range(1, IMAGES):
        got = lax.ppermute(small, "layer", [(0, home(b))])
        opening = jnp.where(l == home(b), got, opening)

    lead = jnp.where(group == 0, 1, 0)
    info = jnp.stack([z, lax.rem(sub, FLOW), lead, mine, sub // FLOW]).astype(jnp.int32)
    sends, v1 = relax(
        info, guess.reshape(-1, W), up, dn, own_image.reshape(-1, W), weights, following, opening
    )

    def pairs(half, k):
        return [
            (SUB * g + FLOW * half + (b + k) % FLOW, SUB * g + home(b))
            for g in range(groups)
            for b in range(IMAGES)
        ]

    received = [[lax.ppermute(sends[k], "layer", pairs(h, k)) for k in range(FLOW)] for h in range(HALVES)]

    def among_sweepers(value, ahead, by):
        pairs = []
        for g in range(groups - ahead):
            for b in range(IMAGES):
                for k in range(rows):
                    if 0 <= k + by < rows:
                        source = (SUB * g + home(b)) * rows + k
                        target = (SUB * (g + ahead) + home(b)) * rows + k + by
                        pairs.append((source, target))
        return lax.ppermute(value, ("layer", "rows"), pairs)

    images = mine.astype(jnp.int32).reshape(1)
    up, dn = rims(0, images, *received[0], v1)
    up0, dn0 = among_sweepers(up, 0, 1), among_sweepers(dn, 0, -1)
    up, dn = rims(1, images, *received[1])
    up1, dn1 = among_sweepers(up, 0, 1), among_sweepers(dn, 0, -1)
    d, w = order(images, received[0] + received[1])

    handed = ()
    for stage in range(groups - 1):
        state, edge = sweep(stage == 0, False, info, v1, d, up0, dn0, up1, dn1, w, *handed)
        handed = among_sweepers(state, 1, 0), among_sweepers(edge, 1, 1), among_sweepers(edge, 1, -1)
    results = sweep(False, True, info, v1, d, up0, dn0, up1, dn1, w, *handed)

    back = []
    for h in range(HALVES):
        for k in range(FLOW):
            back.append(lax.ppermute(results[FLOW * h + k], "layer", [(t, s) for s, t in pairs(h, k)]))
    return finish(info, back).reshape(guess.shape)


def solution(mesh):
    return jax.shard_map(
        cycle,
        mesh=mesh,
        in_specs=(
            P("layer", None, None),
            P(None, None, "rows", None),
            P("layer", None, None, "rows", None),
        ),
        out_specs=P("layer", None, None, "rows", None),
        check_vma=False,
    )
```

profile of v0, /device:TPU:59, one launch (start us, length us, event | category | flops | bytes accessed | tf_op | source)
XLA Modules:
  0.0 205.8 jit_solution(15490001137129174904)
XLA Ops:
  0.0 1.0 slice.23
  2.3 2.6 %collective-permute-start.2 = (bf16[4,32,288]{2,1,0:T(8,128)(2,1)S(1)}, bf16[4,32,288]{2,1,0:T(8,128)(2,1)S(1)}, u32[]{:S(2)}, u32[]{:S(2)}) collective-permute-start(bf16[4,32,288]{2,1,0:T(8,128)(2,1)S(1)} %slice.23), channel_id=1, source_target_pairs={{4,0},{8,4},{12,8},{16,12},{20,16},{24,20},{28,24},{32,28},{36,32}... | collective-permute-start | bytes 221192 | tf_op jit(solution)/shard_map/ppermute | solution.py:377
  5.1 1.5 convert.16
  6.9 3.5 %collective-permute-start = (bf16[7,4,32,128]{3,2,1,0:T(8,128)(2,1)S(1)}, bf16[7,4,32,128]{3,2,1,0:T(8,128)(2,1)S(1)}, u32[]{:S(2)}, u32[]{:S(2)}) collective-permute-start(bf16[7,4,32,128]{3,2,1,0:T(8,128)(2,1)S(1)} %maximum_bitcast_fusion), channel_id=1, source_target_pairs={{0,1},{1,2},{2,3},{4,5},{5,6},{6,7},{8,9},{9,10},{10,11},{12,13},{... | collective-permute-start | bytes 688136 | tf_op jit(solution)/shard_map/ppermute | solution.py:375
  10.5 1.9 collective-permute-start.1
  12.5 0.7 stack.23.info_ref
  13.8 2.0 collective-permute-done.up_ref
  15.8 3.3 %collective-permute-done.1.dn_ref = bf16[7,4,32,128]{3,2,1,0:T(8,128)(2,1)S(1)} collective-permute-done((bf16[7,4,32,128]{3,2,1,0:T(8,128)(2,1)S(1)}, bf16[7,4,32,128]{3,2,1,0:T(8,128)(2,1)S(1)}, u32[]{:S(2)}, u32[]{:S(2)}) %collective-permute-start.1) | collective-permute-done | bytes 229408 | tf_op jit(solution)/shard_map/ppermute | solution.py:376
  19.1 0.7 copy-done.25
  19.8 8.2 %relax.1 = (bf16[38,32,128]{2,1,0:T(8,128)(2,1)}, bf16[38,32,128]{2,1,0:T(8,128)(2,1)}, bf16[38,32,128]{2,1,0:T(8,128)(2,1)}, bf16[38,32,128]{2,1,0:T(8,128)(2,1)}, f32[16,32,128]{2,1,0:T(8,128)}) custom-call(s32[5]{0:T(128)} %stack.23.info_ref, f32[3072,128]{1,0:T(8,128)} %bitcast.20, bf16[7,4,32,128]{3,2,1,0:T(8,128)(2,1)} %copy-done.24, ...), custom_call_target="tpu_custom_call" | custom-call | tf_op jit(solution)/shard_map/relax/pallas_call | solution.py:289
  28.0 0.7 collective-permute-start.5
  28.7 0.7 collective-permute-start.6
  29.4 0.7 collective-permute-start.7
  30.1 0.7 collective-permute-start.8
  31.8 2.8 %shard_map.37 = (bf16[112,32,128]{2,1,0:T(8,128)(2,1)}, bf16[112,32,128]{2,1,0:T(8,128)(2,1)}) custom-call(s32[1]{0:T(128)} %bitcast.3.b_ref, bf16[38,32,128]{2,1,0:T(8,128)(2,1)} %copy-done.6, bf16[38,32,128]{2,1,0:T(8,128)(2,1)} %copy-done.7, bf16[38,32,128]{2,1,0:T(8,128)(2,1)} %copy-done.8, bf16[38,32,128]{2,1,0:T(8,128)(2,1)} %copy-done.9, ...), custom_call_target="tpu_custom_call" | custom-call | tf_op jit(solution)/shard_map/pallas_call | solution.py:308
  34.7 0.7 collective-permute-start.13
  35.4 0.7 collective-permute-start.14
  36.1 0.7 collective-permute-start.9
  36.8 26.1 %collective-permute-start.10 = (bf16[38,32,128]{2,1,0:T(8,128)(2,1)}, bf16[38,32,128]{2,1,0:T(8,128)(2,1)S(1)}, u32[]{:S(2)}, u32[]{:S(2)}) collective-permute-start(bf16[38,32,128]{2,1,0:T(8,128)(2,1)} %get-tuple-element.32), channel_id=1, source_target_pairs={{20,0},{24,8},{28,24},{52,32},{56,40},{60,56},{84,64},{88,72},{92,... | collective-permute-start | bytes 933896 | tf_op jit(solution)/shard_map/ppermute | solution.py:396
  62.9 2.0 collective-permute-start.11
  64.9 10.4 %collective-permute-start.12 = (bf16[38,32,128]{2,1,0:T(8,128)(2,1)}, bf16[38,32,128]{2,1,0:T(8,128)(2,1)}, u32[]{:S(2)}, u32[]{:S(2)}) collective-permute-start(bf16[38,32,128]{2,1,0:T(8,128)(2,1)} %get-tuple-element.34), channel_id=1, source_target_pairs={{28,0},{16,8},{20,24},{60,32},{48,40},{52,56},{92,64},{80,72},{84,... | collective-permute-start | bytes 933896 | tf_op jit(solution)/shard_map/ppermute | solution.py:396
  75.3 3.4 %collective-permute-done.12.refs_7_.refs_3_ = bf16[38,32,128]{2,1,0:T(8,128)(2,1)} collective-permute-done((bf16[38,32,128]{2,1,0:T(8,128)(2,1)}, bf16[38,32,128]{2,1,0:T(8,128)(2,1)}, u32[]{:S(2)}, u32[]{:S(2)}) %collective-permute-start.12) | collective-permute-done | bytes 311328 | tf_op jit(solution)/shard_map/ppermute | solution.py:396
  78.8 2.1 %shard_map.38 = (bf16[32,32,128]{2,1,0:T(8,128)(2,1)}, bf16[32,32,128]{2,1,0:T(8,128)(2,1)}) custom-call(s32[1]{0:T(128)} %bitcast.3.b_ref, bf16[38,32,128]{2,1,0:T(8,128)(2,1)} %copy-done.10, bf16[38,32,128]{2,1,0:T(8,128)(2,1)} %copy-done.11, bf16[38,32,128]{2,1,0:T(8,128)(2,1)} %collective-permute-done.11.refs_6_.refs_2_, ...), custom_call_target="tpu_custom_call" | custom-call | tf_op jit(solution)/shard_map/pallas_call | solution.py:308
  81.6 0.7 collective-permute-start.16
  82.3 3.3 %order.1 = (bf16[16,16,32,128]{3,2,1,0:T(8,128)(2,1)}, bf16[16,3,32,128]{3,2,1,0:T(8,128)(2,1)}) custom-call(s32[1]{0:T(128)} %bitcast.3.b_ref, bf16[38,32,128]{2,1,0:T(8,128)(2,1)} %copy-done.6, bf16[38,32,128]{2,1,0:T(8,128)(2,1)} %copy-done.7, bf16[38,32,128]{2,1,0:T(8,128)(2,1)} %copy-done.8, bf16[38,32,128]{2,1,0:T(8,128)(2,1)} %copy-done.9, ...), custom_call_target="tpu_custom_call" | custom-call | bytes 5000000 | tf_op jit(solution)/shard_map/order/pallas_call | solution.py:333
  87.0 8.4 %sweep.4 = (f32[16,32,128]{2,1,0:T(8,128)}, bf16[16,32,128]{2,1,0:T(8,128)(2,1)}) custom-call(s32[5]{0:T(128)} %stack.23.info_ref, f32[16,32,128]{2,1,0:T(8,128)} %get-tuple-element.30.refs_4_.v1_ref, bf16[16,16,32,128]{3,2,1,0:T(8,128)(2,1)} %get-tuple-element.35.d_ref, bf16[112,32,128]{2,1,0:T(8,128)(2,1)} %copy-done.1, bf16[112,32,128]{2,1,0:T(8,128)(2,1)} %copy-done.2, ...), custom_call_target="tpu_custom_call" | custom-call | tf_op jit(solution)/shard_map/sweep/pallas_call | solution.py:350
  96.0 0.7 collective-permute-start.19
  96.7 0.7 collective-permute-start.18
  98.1 0.7 copy-done.14
  98.8 8.8 %sweep.5 = (f32[16,32,128]{2,1,0:T(8,128)}, bf16[16,32,128]{2,1,0:T(8,128)(2,1)}) custom-call(s32[5]{0:T(128)} %stack.23.info_ref, f32[16,32,128]{2,1,0:T(8,128)} %get-tuple-element.30.refs_4_.v1_ref, bf16[16,16,32,128]{3,2,1,0:T(8,128)(2,1)} %get-tuple-element.35.d_ref, bf16[112,32,128]{2,1,0:T(8,128)(2,1)} %copy-done.1, bf16[112,32,128]{2,1,0:T(8,128)(2,1)} %copy-done.2, ...), custom_call_target="tpu_custom_call" | custom-call | tf_op jit(solution)/shard_map/sweep/pallas_call | solution.py:350
  108.2 0.7 collective-permute-start.22
  110.3 0.7 copy-done.15
  111.0 8.6 %sweep.6 = (f32[16,32,128]{2,1,0:T(8,128)}, bf16[16,32,128]{2,1,0:T(8,128)(2,1)}) custom-call(s32[5]{0:T(128)} %stack.23.info_ref, f32[16,32,128]{2,1,0:T(8,128)} %get-tuple-element.30.refs_4_.v1_ref, bf16[16,16,32,128]{3,2,1,0:T(8,128)(2,1)} %get-tuple-element.35.d_ref, bf16[112,32,128]{2,1,0:T(8,128)(2,1)} %copy-done.1, bf16[112,32,128]{2,1,0:T(8,128)(2,1)} %copy-done.2, ...), custom_call_target="tpu_custom_call" | custom-call | tf_op jit(solution)/shard_map/sweep/pallas_call | solution.py:350
  122.4 0.7 copy-done.13
  123.1 9.3 %sweep.7 = (bf16[2,16,32,128]{3,2,1,0:T(8,128)(2,1)}, bf16[2,16,32,128]{3,2,1,0:T(8,128)(2,1)}, bf16[2,16,32,128]{3,2,1,0:T(8,128)(2,1)}, bf16[2,16,32,128]{3,2,...) custom-call(s32[5]{0:T(128)} %stack.23.info_ref, ...), custom_call_target="tpu_custom_call" | custom-call | tf_op jit(solution)/shard_map/sweep/pallas_call | solution.py:350
  132.4 0.7 collective-permute-start.26
  133.1 0.7 collective-permute-start.27
  133.8 0.7 collective-permute-start.28
  134.5 0.7 collective-permute-start.29
  135.2 0.7 collective-permute-start.30
  135.9 1.3 collective-permute-start.31
  137.2 1.3 collective-permute-start.32
  138.5 1.3 collective-permute-start.33
  139.9 46.6 %collective-permute-done.31.refs_5_ = bf16[2,16,32,128]{3,2,1,0:T(8,128)(2,1)S(1)} collective-permute-done((bf16[2,16,32,128]{3,2,1,0:T(8,128)(2,1)}, bf16[2,16,32,128]{3,2,1,0:T(8,128)(2,1)S(1)}, u32[]{:S(2)}, u32[]{:S(2)}) %collective-permute-start.31) | collective-permute-done | bytes 262176 | tf_op jit(solution)/shard_map/ppermute | solution.py:425
  186.5 9.1 %collective-permute-done.32.refs_6_ = bf16[2,16,32,128]{3,2,1,0:T(8,128)(2,1)S(1)} collective-permute-done((bf16[2,16,32,128]{3,2,1,0:T(8,128)(2,1)}, bf16[2,16,32,128]{3,2,1,0:T(8,128)(2,1)S(1)}, u32[]{:S(2)}, u32[]{:S(2)}) %collective-permute-start.32) | collective-permute-done | bytes 262176 | tf_op jit(solution)/shard_map/ppermute | solution.py:425
  195.5 5.5 %collective-permute-done.33.refs_7_ = bf16[2,16,32,128]{3,2,1,0:T(8,128)(2,1)S(1)} collective-permute-done((bf16[2,16,32,128]{3,2,1,0:T(8,128)(2,1)}, bf16[2,16,32,128]{3,2,1,0:T(8,128)(2,1)S(1)}, u32[]{:S(2)}, u32[]{:S(2)}) %collective-permute-start.33) | collective-permute-done | bytes 262176 | tf_op jit(solution)/shard_map/ppermute | solution.py:425
  201.1 0.7 copy-done.23
  201.8 3.8 %finish.1 = f32[3072,128]{1,0:T(8,128)} custom-call(s32[5]{0:T(128)} %stack.23.info_ref, bf16[2,16,32,128]{3,2,1,0:T(8,128)(2,1)} %copy-done.16, bf16[2,16,32,128]{3,2,1,0:T(8,128)(2,1)} %copy-done.17, bf16[2,16,32,128]{3,2,1,0:T(8,128)(2,1)} %copy-done.18, bf16[2,16,32,128]{3,2,1,0:T(8,128)(2,1)} %copy-done.19, bf16[2,16,32,128]{3,2,1,0:T(8,128)(2,1)} %copy-done.20, ...), custom_call_target="tpu_custom_call" | custom-call | tf_op jit(solution)/shard_map/finish/pallas_call | solution.py:318
  (106 shorter events, 11.6 us)
Async XLA Ops:
  0.0 4.9 %copy-start = (f32[3,32,16,128]{3,2,1,0:T(8,128)S(1)}, f32[3,32,16,128]{3,2,1,0:T(8,128)}, u32[]{:S(2)}) copy-start(f32[3,32,16,128]{3,2,1,0:T(8,128)} %param.4) | copy-start | bytes 2359300
  1.0 12.2 %collective-permute-start.4 = (bf16[4,32,288]{2,1,0:T(8,128)(2,1)S(1)}, bf16[4,32,288]{2,1,0:T(8,128)(2,1)S(1)}, u32[]{:S(2)}, u32[]{:S(2)}) collective-permute-start(bf16[4,32,288]{2,1,0:T(8,128)(2,1)S(1)} %slice.23), channel_id=1, source_target_pairs={{0,8},{1,9},{2,10},{3,11}} | collective-permute-start | bytes 221192 | tf_op jit(solution)/shard_map/ppermute | solution.py:380
  1.7 11.5 %collective-permute-start.3 = (bf16[4,32,288]{2,1,0:T(8,128)(2,1)S(1)}, bf16[4,32,288]{2,1,0:T(8,128)(2,1)S(1)}, u32[]{:S(2)}, u32[]{:S(2)}) collective-permute-start(bf16[4,32,288]{2,1,0:T(8,128)(2,1)S(1)} %slice.23), channel_id=1, source_target_pairs={{0,24},{1,25},{2,26},{3,27}} | collective-permute-start | bytes 221192 | tf_op jit(solution)/shard_map/ppermute | solution.py:380
  2.3 11.5 %collective-permute-start.2 = (bf16[4,32,288]{2,1,0:T(8,128)(2,1)S(1)}, bf16[4,32,288]{2,1,0:T(8,128)(2,1)S(1)}, u32[]{:S(2)}, u32[]{:S(2)}) collective-permute-start(bf16[4,32,288]{2,1,0:T(8,128)(2,1)S(1)} %slice.23), channel_id=1, source_target_pairs={{4,0},{8,4},{12,8},{16,12},{20,16},{24,20},{28,24},{32,28},{36,32}... | collective-permute-start | bytes 221192 | tf_op jit(solution)/shard_map/ppermute | solution.py:377
  5.0 1.9 copy-start.5
  6.6 6.6 %copy-start.12 = (bf16[8,32,288]{2,1,0:T(8,128)(2,1)S(1)}, bf16[8,32,288]{2,1,0:T(8,128)(2,1)}, u32[]{:S(2)}) copy-start(bf16[8,32,288]{2,1,0:T(8,128)(2,1)} %here_ref.1) | copy-start | bytes 442372
  6.9 8.9 %collective-permute-start = (bf16[7,4,32,128]{3,2,1,0:T(8,128)(2,1)S(1)}, bf16[7,4,32,128]{3,2,1,0:T(8,128)(2,1)S(1)}, u32[]{:S(2)}, u32[]{:S(2)}) collective-permute-start(bf16[7,4,32,128]{3,2,1,0:T(8,128)(2,1)S(1)} %maximum_bitcast_fusion), channel_id=1, source_target_pairs={{0,1},{1,2},{2,3},{4,5},{5,6},{6,7},{8,9},{9,10},{10,11},{12,13},{... | collective-permute-start | bytes 688136 | tf_op jit(solution)/shard_map/ppermute | solution.py:375
  10.5 8.6 %collective-permute-start.1 = (bf16[7,4,32,128]{3,2,1,0:T(8,128)(2,1)S(1)}, bf16[7,4,32,128]{3,2,1,0:T(8,128)(2,1)S(1)}, u32[]{:S(2)}, u32[]{:S(2)}) collective-permute-start(bf16[7,4,32,128]{3,2,1,0:T(8,128)(2,1)S(1)} %maximum_bitcast_fusion.1), channel_id=1, source_target_pairs={{1,0},{2,1},{3,2},{5,4},{6,5},{7,6},{9,8},{10,9},{11,10},{13,12},{... | collective-permute-start | bytes 688136 | tf_op jit(solution)/shard_map/ppermute | solution.py:376
  13.8 5.3 %copy-start.32 = (bf16[4,32,288]{2,1,0:T(8,128)(2,1)}, bf16[4,32,288]{2,1,0:T(8,128)(2,1)S(1)}, u32[]{:S(2)}) copy-start(bf16[4,32,288]{2,1,0:T(8,128)(2,1)S(1)} %collective-permute-done.2.next_ref) | copy-start | bytes 221188
  15.8 3.3 %copy-start.24 = (bf16[7,4,32,128]{3,2,1,0:T(8,128)(2,1)}, bf16[7,4,32,128]{3,2,1,0:T(8,128)(2,1)S(1)}, u32[]{:S(2)}) copy-start(bf16[7,4,32,128]{3,2,1,0:T(8,128)(2,1)S(1)} %collective-permute-done.up_ref) | copy-start | bytes 688132
  28.0 2.8 %collective-permute-start.5 = (bf16[38,32,128]{2,1,0:T(8,128)(2,1)}, bf16[38,32,128]{2,1,0:T(8,128)(2,1)S(1)}, u32[]{:S(2)}, u32[]{:S(2)}) collective-permute-start(bf16[38,32,128]{2,1,0:T(8,128)(2,1)} %get-tuple-element.31), channel_id=1, source_target_pairs={{0,0},{4,8},{8,24},{32,32},{36,40},{40,56},{64,64},{68,72},{72,88}... | collective-permute-start | bytes 933896 | tf_op jit(solution)/shard_map/ppermute | solution.py:396
  28.7 2.1 %collective-permute-start.6 = (bf16[38,32,128]{2,1,0:T(8,128)(2,1)}, bf16[38,32,128]{2,1,0:T(8,128)(2,1)S(1)}, u32[]{:S(2)}, u32[]{:S(2)}) collective-permute-start(bf16[38,32,128]{2,1,0:T(8,128)(2,1)} %get-tuple-element.32), channel_id=1, source_target_pairs={{4,0},{8,8},{12,24},{36,32},{40,40},{44,56},{68,64},{72,72},{76,88... | collective-permute-start | bytes 933896 | tf_op jit(solution)/shard_map/ppermute | solution.py:396
  29.4 1.4 collective-permute-start.7
  30.1 0.8 collective-permute-start.8
  34.7 50.9 %collective-permute-start.13 = (bf16[112,32,128]{2,1,0:T(8,128)(2,1)}, bf16[112,32,128]{2,1,0:T(8,128)(2,1)S(1)}, u32[]{:S(2)}, u32[]{:S(2)}) collective-permute-start(bf16[112,32,128]{2,1,0:T(8,128)(2,1)} %get-tuple-element.36), channel_id=1, source_target_pairs={{0,1},{1,2},{2,3},{8,9},{9,10},{10,11},{24,25},{25,26},{26,27},{32... | collective-permute-start | bytes 2752520 | tf_op jit(solution)/shard_map/ppermute | solution.py:407
  35.4 50.2 %collective-permute-start.14 = (bf16[112,32,128]{2,1,0:T(8,128)(2,1)}, bf16[112,32,128]{2,1,0:T(8,128)(2,1)S(1)}, u32[]{:S(2)}, u32[]{:S(2)}) collective-permute-start(bf16[112,32,128]{2,1,0:T(8,128)(2,1)} %get-tuple-element.37), channel_id=1, source_target_pairs={{1,0},{2,1},{3,2},{9,8},{10,9},{11,10},{25,24},{26,25},{27,26},{33... | collective-permute-start | bytes 2752520 | tf_op jit(solution)/shard_map/ppermute | solution.py:407
  36.1 28.8 %collective-permute-start.9 = (bf16[38,32,128]{2,1,0:T(8,128)(2,1)}, bf16[38,32,128]{2,1,0:T(8,128)(2,1)S(1)}, u32[]{:S(2)}, u32[]{:S(2)}) collective-permute-start(bf16[38,32,128]{2,1,0:T(8,128)(2,1)} %get-tuple-element.31), channel_id=1, source_target_pairs={{16,0},{20,8},{24,24},{48,32},{52,40},{56,56},{80,64},{84,72},{88,... | collective-permute-start | bytes 933896 | tf_op jit(solution)/shard_map/ppermute | solution.py:396
  36.8 38.5 %collective-permute-start.10 = (bf16[38,32,128]{2,1,0:T(8,128)(2,1)}, bf16[38,32,128]{2,1,0:T(8,128)(2,1)S(1)}, u32[]{:S(2)}, u32[]{:S(2)}) collective-permute-start(bf16[38,32,128]{2,1,0:T(8,128)(2,1)} %get-tuple-element.32), channel_id=1, source_target_pairs={{20,0},{24,8},{28,24},{52,32},{56,40},{60,56},{84,64},{88,72},{92,... | collective-permute-start | bytes 933896 | tf_op jit(solution)/shard_map/ppermute | solution.py:396
  62.9 12.4 %collective-permute-start.11 = (bf16[38,32,128]{2,1,0:T(8,128)(2,1)}, bf16[38,32,128]{2,1,0:T(8,128)(2,1)}, u32[]{:S(2)}, u32[]{:S(2)}) collective-permute-start(bf16[38,32,128]{2,1,0:T(8,128)(2,1)} %get-tuple-element.33), channel_id=1, source_target_pairs={{24,0},{28,8},{16,24},{56,32},{60,40},{48,56},{88,64},{92,72},{80,... | collective-permute-start | bytes 933896 | tf_op jit(solution)/shard_map/ppermute | solution.py:396
  64.9 13.8 %copy-start.10 = (bf16[38,32,128]{2,1,0:T(8,128)(2,1)}, bf16[38,32,128]{2,1,0:T(8,128)(2,1)S(1)}, u32[]{:S(2)}) copy-start(bf16[38,32,128]{2,1,0:T(8,128)(2,1)S(1)} %collective-permute-done.9.refs_4_.refs_0_) | copy-start | bytes 933892
  64.9 13.8 %collective-permute-start.12 = (bf16[38,32,128]{2,1,0:T(8,128)(2,1)}, bf16[38,32,128]{2,1,0:T(8,128)(2,1)}, u32[]{:S(2)}, u32[]{:S(2)}) collective-permute-start(bf16[38,32,128]{2,1,0:T(8,128)(2,1)} %get-tuple-element.34), channel_id=1, source_target_pairs={{28,0},{16,8},{20,24},{60,32},{48,40},{52,56},{92,64},{80,72},{84,... | collective-permute-start | bytes 933896 | tf_op jit(solution)/shard_map/ppermute | solution.py:396
  75.3 3.4 %copy-start.11 = (bf16[38,32,128]{2,1,0:T(8,128)(2,1)}, bf16[38,32,128]{2,1,0:T(8,128)(2,1)S(1)}, u32[]{:S(2)}) copy-start(bf16[38,32,128]{2,1,0:T(8,128)(2,1)S(1)} %collective-permute-done.10.refs_5_.refs_1_) | copy-start | bytes 933892
  80.9 4.6 %collective-permute-start.15 = (bf16[32,32,128]{2,1,0:T(8,128)(2,1)}, bf16[32,32,128]{2,1,0:T(8,128)(2,1)S(1)}, u32[]{:S(2)}, u32[]{:S(2)}) collective-permute-start(bf16[32,32,128]{2,1,0:T(8,128)(2,1)} %get-tuple-element.38), channel_id=1, source_target_pairs={{0,1},{1,2},{2,3},{8,9},{9,10},{10,11},{24,25},{25,26},{26,27},{32... | collective-permute-start | bytes 786440 | tf_op jit(solution)/shard_map/ppermute | solution.py:407
  81.6 4.0 %collective-permute-start.16 = (bf16[32,32,128]{2,1,0:T(8,128)(2,1)}, bf16[32,32,128]{2,1,0:T(8,128)(2,1)S(1)}, u32[]{:S(2)}, u32[]{:S(2)}) collective-permute-start(bf16[32,32,128]{2,1,0:T(8,128)(2,1)} %get-tuple-element.39), channel_id=1, source_target_pairs={{1,0},{2,1},{3,2},{9,8},{10,9},{11,10},{25,24},{26,25},{27,26},{33... | collective-permute-start | bytes 786440 | tf_op jit(solution)/shard_map/ppermute | solution.py:407
  95.3 2.1 %collective-permute-start.17 = (f32[16,32,128]{2,1,0:T(8,128)}, f32[16,32,128]{2,1,0:T(8,128)S(1)}, u32[]{:S(2)}, u32[]{:S(2)}) collective-permute-start(f32[16,32,128]{2,1,0:T(8,128)} %get-tuple-element.41), channel_id=1, source_target_pairs={{0,32},{1,33},{2,34},{3,35},{8,40},{9,41},{10,42},{11,43},{24,56},... | collective-permute-start | bytes 786440 | tf_op jit(solution)/shard_map/ppermute | solution.py:407
  96.0 1.4 collective-permute-start.19
  96.7 0.7 collective-permute-start.18
  107.6 2.1 %collective-permute-start.20 = (f32[16,32,128]{2,1,0:T(8,128)}, f32[16,32,128]{2,1,0:T(8,128)S(1)}, u32[]{:S(2)}, u32[]{:S(2)}) collective-permute-start(f32[16,32,128]{2,1,0:T(8,128)} %get-tuple-element.43), channel_id=1, source_target_pairs={{0,32},{1,33},{2,34},{3,35},{8,40},{9,41},{10,42},{11,43},{24,56},... | collective-permute-start | bytes 786440 | tf_op jit(solution)/shard_map/ppermute | solution.py:407
  108.2 1.4 collective-permute-start.22
  108.9 0.7 collective-permute-start.21
  119.6 2.1 %collective-permute-start.23 = (f32[16,32,128]{2,1,0:T(8,128)}, f32[16,32,128]{2,1,0:T(8,128)S(1)}, u32[]{:S(2)}, u32[]{:S(2)}) collective-permute-start(f32[16,32,128]{2,1,0:T(8,128)} %get-tuple-element.45), channel_id=1, source_target_pairs={{0,32},{1,33},{2,34},{3,35},{8,40},{9,41},{10,42},{11,43},{24,56},... | collective-permute-start | bytes 786440 | tf_op jit(solution)/shard_map/ppermute | solution.py:407
  120.3 1.4 collective-permute-start.25
  121.0 0.7 collective-permute-start.24
  132.4 3.4 %collective-permute-start.26 = (bf16[2,16,32,128]{3,2,1,0:T(8,128)(2,1)}, bf16[2,16,32,128]{3,2,1,0:T(8,128)(2,1)S(1)}, u32[]{:S(2)}, u32[]{:S(2)}) collective-permute-start(bf16[2,16,32,128]{3,2,1,0:T(8,128)(2,1)} %get-tuple-element.47), channel_id=1, source_target_pairs={{0,0},{8,4},{24,8},{32,32},{40,36},{56,40},{64,64},{72,68},{88,72}... | collective-permute-start | bytes 786440 | tf_op jit(solution)/shard_map/ppermute | solution.py:425
  133.1 4.1 %collective-permute-start.27 = (bf16[2,16,32,128]{3,2,1,0:T(8,128)(2,1)}, bf16[2,16,32,128]{3,2,1,0:T(8,128)(2,1)S(1)}, u32[]{:S(2)}, u32[]{:S(2)}) collective-permute-start(bf16[2,16,32,128]{3,2,1,0:T(8,128)(2,1)} %get-tuple-element.48), channel_id=1, source_target_pairs={{0,4},{8,8},{24,12},{32,36},{40,40},{56,44},{64,68},{72,72},{88,76... | collective-permute-start | bytes 786440 | tf_op jit(solution)/shard_map/ppermute | solution.py:425
  133.8 4.7 %collective-permute-start.28 = (bf16[2,16,32,128]{3,2,1,0:T(8,128)(2,1)}, bf16[2,16,32,128]{3,2,1,0:T(8,128)(2,1)S(1)}, u32[]{:S(2)}, u32[]{:S(2)}) collective-permute-start(bf16[2,16,32,128]{3,2,1,0:T(8,128)(2,1)} %get-tuple-element.49), channel_id=1, source_target_pairs={{0,8},{8,12},{24,0},{32,40},{40,44},{56,32},{64,72},{72,76},{88,64... | collective-permute-start | bytes 786440 | tf_op jit(solution)/shard_map/ppermute | solution.py:425
  134.5 5.3 %collective-permute-start.29 = (bf16[2,16,32,128]{3,2,1,0:T(8,128)(2,1)}, bf16[2,16,32,128]{3,2,1,0:T(8,128)(2,1)S(1)}, u32[]{:S(2)}, u32[]{:S(2)}) collective-permute-start(bf16[2,16,32,128]{3,2,1,0:T(8,128)(2,1)} %get-tuple-element.50), channel_id=1, source_target_pairs={{0,12},{8,0},{24,4},{32,44},{40,32},{56,36},{64,76},{72,64},{88,68... | collective-permute-start | bytes 786440 | tf_op jit(solution)/shard_map/ppermute | solution.py:425
  135.2 4.7 %collective-permute-start.30 = (bf16[2,16,32,128]{3,2,1,0:T(8,128)(2,1)}, bf16[2,16,32,128]{3,2,1,0:T(8,128)(2,1)S(1)}, u32[]{:S(2)}, u32[]{:S(2)}) collective-permute-start(bf16[2,16,32,128]{3,2,1,0:T(8,128)(2,1)} %get-tuple-element.51), channel_id=1, source_target_pairs={{0,16},{8,20},{24,24},{32,48},{40,52},{56,56},{64,80},{72,84},{88,... | collective-permute-start | bytes 786440 | tf_op jit(solution)/shard_map/ppermute | solution.py:425
  135.9 65.2 %copy-start.16 = (bf16[2,16,32,128]{3,2,1,0:T(8,128)(2,1)}, bf16[2,16,32,128]{3,2,1,0:T(8,128)(2,1)S(1)}, u32[]{:S(2)}) copy-start(bf16[2,16,32,128]{3,2,1,0:T(8,128)(2,1)S(1)} %collective-permute-done.26.refs_0_) | copy-start | bytes 786436
  135.9 50.6 %collective-permute-start.31 = (bf16[2,16,32,128]{3,2,1,0:T(8,128)(2,1)}, bf16[2,16,32,128]{3,2,1,0:T(8,128)(2,1)S(1)}, u32[]{:S(2)}, u32[]{:S(2)}) collective-permute-start(bf16[2,16,32,128]{3,2,1,0:T(8,128)(2,1)} %get-tuple-element.52), channel_id=1, source_target_pairs={{0,20},{8,24},{24,28},{32,52},{40,56},{56,60},{64,84},{72,88},{88,... | collective-permute-start | bytes 786440 | tf_op jit(solution)/shard_map/ppermute | solution.py:425
  137.2 63.9 %copy-start.17 = (bf16[2,16,32,128]{3,2,1,0:T(8,128)(2,1)}, bf16[2,16,32,128]{3,2,1,0:T(8,128)(2,1)S(1)}, u32[]{:S(2)}) copy-start(bf16[2,16,32,128]{3,2,1,0:T(8,128)(2,1)S(1)} %collective-permute-done.27.refs_1_) | copy-start | bytes 786436
  137.2 58.3 %collective-permute-start.32 = (bf16[2,16,32,128]{3,2,1,0:T(8,128)(2,1)}, bf16[2,16,32,128]{3,2,1,0:T(8,128)(2,1)S(1)}, u32[]{:S(2)}, u32[]{:S(2)}) collective-permute-start(bf16[2,16,32,128]{3,2,1,0:T(8,128)(2,1)} %get-tuple-element.53), channel_id=1, source_target_pairs={{0,24},{8,28},{24,16},{32,56},{40,60},{56,48},{64,88},{72,92},{88,... | collective-permute-start | bytes 786440 | tf_op jit(solution)/shard_map/ppermute | solution.py:425
  138.5 62.5 %copy-start.18 = (bf16[2,16,32,128]{3,2,1,0:T(8,128)(2,1)}, bf16[2,16,32,128]{3,2,1,0:T(8,128)(2,1)S(1)}, u32[]{:S(2)}) copy-start(bf16[2,16,32,128]{3,2,1,0:T(8,128)(2,1)S(1)} %collective-permute-done.28.refs_2_) | copy-start | bytes 786436
  138.5 62.5 %collective-permute-start.33 = (bf16[2,16,32,128]{3,2,1,0:T(8,128)(2,1)}, bf16[2,16,32,128]{3,2,1,0:T(8,128)(2,1)S(1)}, u32[]{:S(2)}, u32[]{:S(2)}) collective-permute-start(bf16[2,16,32,128]{3,2,1,0:T(8,128)(2,1)} %get-tuple-element.54), channel_id=1, source_target_pairs={{0,28},{8,16},{24,20},{32,60},{40,48},{56,52},{64,92},{72,80},{88,... | collective-permute-start | bytes 786440 | tf_op jit(solution)/shard_map/ppermute | solution.py:425
  139.8 61.2 %copy-start.19 = (bf16[2,16,32,128]{3,2,1,0:T(8,128)(2,1)}, bf16[2,16,32,128]{3,2,1,0:T(8,128)(2,1)S(1)}, u32[]{:S(2)}) copy-start(bf16[2,16,32,128]{3,2,1,0:T(8,128)(2,1)S(1)} %collective-permute-done.29.refs_3_) | copy-start | bytes 786436
  139.8 61.2 %copy-start.20 = (bf16[2,16,32,128]{3,2,1,0:T(8,128)(2,1)}, bf16[2,16,32,128]{3,2,1,0:T(8,128)(2,1)S(1)}, u32[]{:S(2)}) copy-start(bf16[2,16,32,128]{3,2,1,0:T(8,128)(2,1)S(1)} %collective-permute-done.30.refs_4_) | copy-start | bytes 786436
  186.5 14.6 %copy-start.21 = (bf16[2,16,32,128]{3,2,1,0:T(8,128)(2,1)}, bf16[2,16,32,128]{3,2,1,0:T(8,128)(2,1)S(1)}, u32[]{:S(2)}) copy-start(bf16[2,16,32,128]{3,2,1,0:T(8,128)(2,1)S(1)} %collective-permute-done.31.refs_5_) | copy-start | bytes 786436
  195.5 5.6 %copy-start.22 = (bf16[2,16,32,128]{3,2,1,0:T(8,128)(2,1)}, bf16[2,16,32,128]{3,2,1,0:T(8,128)(2,1)S(1)}, u32[]{:S(2)}) copy-start(bf16[2,16,32,128]{3,2,1,0:T(8,128)(2,1)S(1)} %collective-permute-done.32.refs_6_) | copy-start | bytes 786436
  (19 other events, 15.0 us)
where the time goes:
time: 207 us; the launch traced here: 206 us
  waiting for transfers between devices  69.9 us (34%)
  starting transfers between devices  67.4 us (33%)
  Pallas kernels  55.3 us (27%)
  local copies, waits for them, and re-layouts  10 us (5%)
  other arithmetic  2.22 us (1%)
    ppermute x8, waiting for transfers between devices, cycle(): lax.ppermute(results[FLOW * h + k], 'layer', [(t, s) for s, t in pairs(h,...  61.2 us
    ppermute x8, starting transfers between devices, cycle(): lax.ppermute(sends[k], 'layer', pairs(h, k))  41.9 us
    pallas_call x4, Pallas kernels, sweep(): pl.pallas_call(functools.partial(sweep_kernel, opening, closing), out_sha...  35 us
    ppermute x13, starting transfers between devices, among_sweepers(): return lax.ppermute(value, ('layer', 'rows'), pairs)  8.78 us
    pallas_call x1, Pallas kernels, relax(): pl.pallas_call(relax_kernel, out_shape=(shape(CHUNK, C, W),) * FLOW + (sh...  8.2 us
    unnamed x67, local copies, waits for them, and re-layouts  8.12 us
    ppermute x8, starting transfers between devices, cycle(): lax.ppermute(results[FLOW * h + k], 'layer', [(t, s) for s, t in pairs(h,...  7.26 us
    pallas_call x2, Pallas kernels, rims(): pl.pallas_call(functools.partial(rim_kernel, half), out_shape=(shape(tota...  4.97 us
  transfers between devices with their start and end apart: 34, of which 6 were waited for; matrix products, arithmetic and copies ran while one was open for 2% of the time, Pallas kernels for 3%

commit v1 on v0

--- a/solution.py
+++ b/solution.py
@@ -70,6 +70,51 @@
             xs[buf, row] = jnp.zeros((3, C, W), bf16)
 
 
+def relaxer(info_ref, xs, state):
+    low_ok = jnp.where(info_ref[0] > 0, 1.0, 0.0)
+    high_ok = jnp.where(info_ref[0] < 3, 1.0, 0.0)
+
+    def put(buf, row, value):
+        if row < REACH:
+            value = value * low_ok
+        elif row >= REACH + BAND:
+            value = value * high_ok
+        spread(xs, buf, row + 1, value)
+
+    def load(point, u, up_ref, own_ref, dn_ref, at):
+        for r in range(0, SPAN, 2):
+            if r < REACH:
+                x = up_ref[u, r : r + 2]
+            elif r >= REACH + BAND:
+                x = dn_ref[u, r - REACH - BAND : r - REACH - BAND + 2]
+            else:
+                x = [own_ref[pl.ds(at + r - REACH + k, C, stride=BAND), :] for k in range(2)]
+                x = jnp.concatenate(x, axis=0).astype(bf16)
+            x = x.astype(f32).reshape(2 * C, W)
+            state[point, r : r + 2] = x.reshape(2, C, W)
+            put(2 * point, r, x)
+
+    def layer(point, j, matrix, base=None):
+        lo = (j + 1) // 2 * 2
+        for row in range(lo, SPAN - lo, 4):
+            for i, t in enumerate(block(xs, 2 * point + j % 2, matrix, row)):
+                r = row + 2 * i
+                x = state[point, r : r + 2].reshape(2 * C, W)
+                if j == 0 and base is not None and REACH <= r < REACH + BAND:
+                    base[point, r - REACH : r - REACH + 2] = (x + (M * H) * t).reshape(2, C, W)
+                x = x + H * t
+                state[point, r : r + 2] = x.reshape(2, C, W)
+                if j < M - 1:
+                    put(2 * point + (j + 1) % 2, r, x)
+
+    return load, layer
+
+
+def tiles(ref, n):
+    tail = jnp.concatenate([ref[n, :, 2 * W :], jnp.zeros((C, 3 * C), bf16)], axis=1)
+    return [ref[n, :, :W], ref[n, :, W : 2 * W], tail]
+
+
 def drain(source, targets, sems):
     copies = [pltpu.make_async_copy(source.at[r], target, sems.at[r]) for r, target in enumerate(targets)]
     for copy in copies:
@@ -78,82 +123,41 @@
         copy.wait()
 
 
-def relax_kernel(info_ref, own_ref, up_ref, dn_ref, img_ref, here_ref, next_ref, open_ref, *refs):
-    outs, (v1_ref, xs, state, base, slots, sems) = refs[:FLOW], refs[FLOW:]
-    z, turn, lead = info_ref[0], info_ref[1], info_ref[2]
-
-    def tiles(ref, n):
-        tail = jnp.concatenate([ref[n, :, 2 * W :], jnp.zeros((C, 3 * C), bf16)], axis=1)
-        return [ref[n, :, :W], ref[n, :, W : 2 * W], tail]
+def relax_kernel(k, info_ref, own_ref, up_ref, dn_ref, here_ref, next_ref, out_ref, xs, state, base):
+    b = lax.rem(info_ref[1] - k + FLOW, FLOW)
+    load, layer = relaxer(info_ref, xs, state)
 
     def tap(point, j):
         return tiles(next_ref, j) if point else tiles(here_ref, M + j)
 
-    clear_rims(xs, SPAN)
-    low_ok = jnp.where(z > 0, 1.0, 0.0)
-    high_ok = jnp.where(z < 3, 1.0, 0.0)
-
-    def put(buf, pair, value):
-        if pair < REACH // 2:
-            value = value * low_ok
-        elif pair >= (REACH + BAND) // 2:
-            value = value * high_ok
-        spread(xs, buf, 2 * pair + 1, value)
-
-    def load(lane_set, u):
-        for pair in range(SPAN // 2):
-            r = 2 * pair
-            if r < REACH:
-                x = up_ref[u, r : r + 2]
-            elif r >= REACH + BAND:
-                x = dn_ref[u, r - REACH - BAND : r - REACH - BAND + 2]
-            else:
-                ref, at = (img_ref, 0) if isinstance(u, int) else (own_ref, u * (C * BAND))
-                x = [ref[pl.ds(at + r - REACH + k, C, stride=BAND), :] for k in range(2)]
-                x = jnp.concatenate(x, axis=0).astype(bf16)
-            x = x.astype(f32).reshape(2 * C, W)
-            state[lane_set, r : r + 2] = x.reshape(2, C, W)
-            put(2 * lane_set, pair, x)
-
-    def layer(lane_set, j, matrix):
-        lo = (j + 1) // 2 * 2
-        for row in range(lo, SPAN - lo, 4):
-            for i, t in enumerate(block(xs, 2 * lane_set + j % 2, matrix, row)):
-                r = row + 2 * i
-                x = state[lane_set, r : r + 2].reshape(2 * C, W)
-                if j == 0 and REACH <= r < REACH + BAND:
-                    base[lane_set, r - REACH : r - REACH + 2] = (x + (M * H) * t).reshape(2, C, W)
-                x = x + H * t
-                state[lane_set, r : r + 2] = x.reshape(2, C, W)
-                if j < M - 1:
-                    put(2 * lane_set + (j + 1) % 2, r // 2, x)
-
-    def image(b, carry):
+    @pl.when(b < IMAGES)
+    def _():
+        clear_rims(xs, SPAN)
         for point in range(2):
-            load(point, point * IMAGES + b)
+            u = point * IMAGES + b
+            load(point, u, up_ref, own_ref, dn_ref, u * (C * BAND))
         for j in range(M):
             for point in range(2):
-                layer(point, j, banded(tap(point, j)))
-        slot = lax.rem(turn - b + FLOW, FLOW)
+                layer(point, j, banded(tap(point, j)), base)
         for point in range(2):
             change = state[point, REACH : REACH + BAND] - base[point]
-            slots[slot, point * BAND : (point + 1) * BAND] = change.astype(bf16)
+            out_ref[point * BAND : (point + 1) * BAND] = change.astype(bf16)
             for t, tile in enumerate(tap(point, 0)):
-                slots[slot, 2 * BAND + 3 * point + t] = tile
-        return carry
-
-    lax.fori_loop(0, IMAGES, image, 0)
-
-    @pl.when(lead == 1)
+                out_ref[2 * BAND + 3 * point + t] = tile
+
+
+def opening_kernel(info_ref, img_ref, up_ref, dn_ref, open_ref, v1_ref, xs, state):
+    load, layer = relaxer(info_ref, xs, state)
+
+    @pl.when(info_ref[2] == 1)
     def _():
-        load(0, 2 * IMAGES)
+        clear_rims(xs, SPAN)
+        load(0, 2 * IMAGES, up_ref, img_ref, dn_ref, 0)
         for j in range(M):
             layer(0, j, banded(tiles(open_ref, j)))
         for r in range(BAND):
             x = img_ref[pl.ds(r, C, stride=BAND), :]
             v1_ref[r] = x + (state[0, REACH + r] - x.astype(bf16).astype(f32))
-
-    drain(slots, outs, sems)
 
 
 def rim_kernel(half, b_ref, *refs):
@@ -285,22 +289,32 @@
     return jax.ShapeDtypeStruct(dims, dtype)
 
 
-def relax(info, *arrays):
-    outs = pl.pallas_call(
-        relax_kernel,
-        out_shape=(shape(CHUNK, C, W),) * FLOW + (shape(BAND, C, W, dtype=f32),),
-        in_specs=[SM] + [VM] * 7,
-        out_specs=(AN,) * FLOW + (VM,),
+def relax(k, info, *arrays):
+    return pl.pallas_call(
+        functools.partial(relax_kernel, k),
+        out_shape=shape(CHUNK, C, W),
+        in_specs=[SM] + [VM] * len(arrays),
+        out_specs=VM,
         scratch_shapes=[
             pltpu.VMEM((4, SPAN + 2, 3, C, W), bf16),
             pltpu.VMEM((2, SPAN, C, W), f32),
             pltpu.VMEM((2, BAND, C, W), f32),
-            pltpu.VMEM((FLOW, CHUNK, C, W), bf16),
-            pltpu.SemaphoreType.DMA((FLOW,)),
         ],
-        name="relax",
     )(info, *arrays)
-    return outs[:FLOW], outs[FLOW]
+
+
+def opened(info, *arrays):
+    return pl.pallas_call(
+        opening_kernel,
+        out_shape=shape(BAND, C, W, dtype=f32),
+        in_specs=[SM] + [VM] * len(arrays),
+        out_specs=VM,
+        scratch_shapes=[
+            pltpu.VMEM((2, SPAN + 2, 3, C, W), bf16),
+            pltpu.VMEM((1, SPAN, C, W), f32),
+        ],
+        name="opening",
+    )(info, *arrays)
 
 
 def rims(half, b, *arrays):
@@ -382,9 +396,6 @@
 
     lead = jnp.where(group == 0, 1, 0)
     info = jnp.stack([z, lax.rem(sub, FLOW), lead, mine, sub // FLOW]).astype(jnp.int32)
-    sends, v1 = relax(
-        info, guess.reshape(-1, W), up, dn, own_image.reshape(-1, W), weights, following, opening
-    )
 
     def pairs(half, k):
         return [
@@ -393,7 +404,12 @@
             for b in range(IMAGES)
         ]
 
-    received = [[lax.ppermute(sends[k], "layer", pairs(h, k)) for k in range(FLOW)] for h in range(HALVES)]
+    received = [[], []]
+    for k in range(FLOW):
+        chunk = relax(k, info, guess.reshape(-1, W), up, dn, weights, following)
+        for h in range(HALVES):
+            received[h].append(lax.ppermute(chunk, "layer", pairs(h, k)))
+    v1 = opened(info, own_image.reshape(-1, W), up, dn, opening)
 
     def among_sweepers(value, ahead, by):
         pairs = []

time: 207 us -> 207 us (level)
  starting transfers between devices: 67.4 us -> 59.5 us
  Pallas kernels: 55.3 us -> 62.9 us
    ppermute x8, starting transfers between devices: 41.9 us -> 33.5 us  [cycle(): received[h].append(lax.ppermute(chunk, 'layer', pairs(h, k)))]
    pallas_call x1 -> x5, Pallas kernels: 8.2 us -> 16.1 us  [the longest x4 14.2 us: relax(): pl.pallas_call(functools.partial(relax_kernel, k), out_shape=shape(CHUNK,...]
    ppermute x1, waiting for transfers between devices: 0.01 us -> 3.74 us  [cycle(): lax.ppermute(small, 'layer', [(i + 1, i) for i in range(layers - 1)])]
    ppermute x1, waiting for transfers between devices: 3.3 us -> 0.01 us  [cycle(): lax.ppermute(edge_rows(0), 'rows', [(i + 1, i) for i in range(rows - 1)])]
    unnamed x67 -> x71, local copies, waits for them, and re-layouts: 8.12 us -> 9.93 us
  transfers between devices with their start and end apart: 34 -> 34, of which waited for: 6 -> 5; matrix products, arithmetic and copies ran while one was open for 2% -> 1% of each run, Pallas kernels for 3% -> 10%
where the time goes in v1:
time: 207 us; the launch traced here: 206 us
  waiting for transfers between devices  69.3 us (33%)
  Pallas kernels  62.9 us (30%)
  starting transfers between devices  59.5 us (29%)
  local copies, waits for them, and re-layouts  10.8 us (5%)
  other arithmetic  2.22 us (1%)
    ppermute x8, waiting for transfers between devices, cycle(): lax.ppermute(results[FLOW * h + k], 'layer', [(t, s) for s, t in pairs(h,...  62.1 us
    pallas_call x4, Pallas kernels, sweep(): pl.pallas_call(functools.partial(sweep_kernel, opening, closing), out_sha...  34.8 us
    ppermute x8, starting transfers between devices, cycle(): received[h].append(lax.ppermute(chunk, 'layer', pairs(h, k)))  33.5 us
    pallas_call x4, Pallas kernels, relax(): pl.pallas_call(functools.partial(relax_kernel, k), out_shape=shape(CHUNK,...  14.2 us
    unnamed x71, local copies, waits for them, and re-layouts  9.93 us
    ppermute x13, starting transfers between devices, among_sweepers(): return lax.ppermute(value, ('layer', 'rows'), pairs)  8.96 us
    ppermute x8, starting transfers between devices, cycle(): lax.ppermute(results[FLOW * h + k], 'layer', [(t, s) for s, t in pairs(h,...  7.26 us
    pallas_call x2, Pallas kernels, rims(): pl.pallas_call(functools.partial(rim_kernel, half), out_shape=(shape(tota...  4.96 us
  transfers between devices with their start and end apart: 34, of which 5 were waited for; matrix products, arithmetic and copies ran while one was open for 1% of the time, Pallas kernels for 10%

profile of v1, /device:TPU:59, one launch (start us, length us, event | category | flops | bytes accessed | tf_op | source)
XLA Modules:
  0.0 205.7 jit_solution(2998547216180132149)
XLA Ops:
  0.0 1.1 copy-done
  1.3 1.5 convert.16
  3.1 3.5 %collective-permute-start = (bf16[7,4,32,128]{3,2,1,0:T(8,128)(2,1)S(1)}, bf16[7,4,32,128]{3,2,1,0:T(8,128)(2,1)S(1)}, u32[]{:S(2)}, u32[]{:S(2)}) collective-permute-start(bf16[7,4,32,128]{3,2,1,0:T(8,128)(2,1)S(1)} %maximum_bitcast_fusion), channel_id=1, source_target_pairs={{0,1},{1,2},{2,3},{4,5},{5,6},{6,7},{8,9},{9,10},{10,11},{12,13},{... | collective-permute-start | bytes 688136 | tf_op jit(solution)/shard_map/ppermute | solution.py:389
  6.7 1.9 collective-permute-start.1
  8.6 3.0 %collective-permute-start.4 = (bf16[4,32,288]{2,1,0:T(8,128)(2,1)S(1)}, bf16[4,32,288]{2,1,0:T(8,128)(2,1)S(1)}, u32[]{:S(2)}, u32[]{:S(2)}) collective-permute-start(bf16[4,32,288]{2,1,0:T(8,128)(2,1)S(1)} %slice.23), channel_id=1, source_target_pairs={{4,0},{8,4},{12,8},{16,12},{20,16},{24,20},{28,24},{32,28},{36,32}... | collective-permute-start | bytes 221192 | tf_op jit(solution)/shard_map/ppermute | solution.py:391
  12.9 3.7 %collective-permute-done.4.next_ref = bf16[4,32,288]{2,1,0:T(8,128)(2,1)S(1)} collective-permute-done((bf16[4,32,288]{2,1,0:T(8,128)(2,1)S(1)}, bf16[4,32,288]{2,1,0:T(8,128)(2,1)S(1)}, u32[]{:S(2)}, u32[]{:S(2)}) %collective-permute-start.4) | collective-permute-done | bytes 73760 | tf_op jit(solution)/shard_map/ppermute | solution.py:391
  17.5 2.4 %shard_map.37 = bf16[38,32,128]{2,1,0:T(8,128)(2,1)} custom-call(s32[5]{0:T(128)} %stack.23.info_ref, f32[3072,128]{1,0:T(8,128)} %bitcast.20, bf16[7,4,32,128]{3,2,1,0:T(8,128)(2,1)} %copy-done.3, bf16[7,4,32,128]{3,2,1,0:T(8,128)(2,1)} %copy-done.4, bf16[8,32,288]{2,1,0:T(8,128)(2,1)} %here_ref.7, bf16[4,32,288]{2,1,0:T(8,128)(2,1)} %copy-done.10), custom_call_target="tpu_custom_call" | custom-call | tf_op jit(solution)/shard_map/pallas_call | solution.py:293
  20.6 3.9 %shard_map.38 = bf16[38,32,128]{2,1,0:T(8,128)(2,1)} custom-call(s32[5]{0:T(128)} %stack.23.info_ref, f32[3072,128]{1,0:T(8,128)} %bitcast.21, bf16[7,4,32,128]{3,2,1,0:T(8,128)(2,1)} %copy-done.3, bf16[7,4,32,128]{3,2,1,0:T(8,128)(2,1)} %copy-done.4, bf16[8,32,288]{2,1,0:T(8,128)(2,1)} %here_ref.7, bf16[4,32,288]{2,1,0:T(8,128)(2,1)} %copy-done.10), custom_call_target="tpu_custom_call" | custom-call | tf_op jit(solution)/shard_map/pallas_call | solution.py:293
  25.2 3.9 %shard_map.39 = bf16[38,32,128]{2,1,0:T(8,128)(2,1)} custom-call(s32[5]{0:T(128)} %stack.23.info_ref, f32[3072,128]{1,0:T(8,128)} %bitcast.22, bf16[7,4,32,128]{3,2,1,0:T(8,128)(2,1)} %copy-done.3, bf16[7,4,32,128]{3,2,1,0:T(8,128)(2,1)} %copy-done.4, bf16[8,32,288]{2,1,0:T(8,128)(2,1)} %here_ref.7, bf16[4,32,288]{2,1,0:T(8,128)(2,1)} %copy-done.10), custom_call_target="tpu_custom_call" | custom-call | tf_op jit(solution)/shard_map/pallas_call | solution.py:293
  29.1 0.8 collective-permute-start.7
  29.9 3.9 %shard_map.40 = bf16[38,32,128]{2,1,0:T(8,128)(2,1)} custom-call(s32[5]{0:T(128)} %stack.23.info_ref, f32[3072,128]{1,0:T(8,128)} %bitcast.23, bf16[7,4,32,128]{3,2,1,0:T(8,128)(2,1)} %copy-done.3, bf16[7,4,32,128]{3,2,1,0:T(8,128)(2,1)} %copy-done.4, bf16[8,32,288]{2,1,0:T(8,128)(2,1)} %here_ref.7, bf16[4,32,288]{2,1,0:T(8,128)(2,1)} %copy-done.10), custom_call_target="tpu_custom_call" | custom-call | tf_op jit(solution)/shard_map/pallas_call | solution.py:293
  33.8 0.8 collective-permute-start.8
  36.0 1.9 opening.1.refs_4_.v1_ref
  38.0 0.7 copy-done.11
  38.9 0.7 copy-done.14
  39.6 2.8 %shard_map.41 = (bf16[112,32,128]{2,1,0:T(8,128)(2,1)}, bf16[112,32,128]{2,1,0:T(8,128)(2,1)}) custom-call(s32[1]{0:T(128)} %bitcast.3.b_ref, bf16[38,32,128]{2,1,0:T(8,128)(2,1)} %copy-done.11, bf16[38,32,128]{2,1,0:T(8,128)(2,1)} %copy-done.12, bf16[38,32,128]{2,1,0:T(8,128)(2,1)} %copy-done.13, bf16[38,32,128]{2,1,0:T(8,128)(2,1)} %copy-done.14, ...), custom_call_target="tpu_custom_call" | custom-call | tf_op jit(solution)/shard_map/pallas_call | solution.py:322
  42.5 0.7 collective-permute-start.13
  43.2 0.7 collective-permute-start.14
  43.9 0.7 collective-permute-start.9
  44.6 13.7 %collective-permute-start.10 = (bf16[38,32,128]{2,1,0:T(8,128)(2,1)S(1)}, bf16[38,32,128]{2,1,0:T(8,128)(2,1)S(1)}, u32[]{:S(2)}, u32[]{:S(2)}) collective-permute-start(bf16[38,32,128]{2,1,0:T(8,128)(2,1)S(1)} %copy-done.17), channel_id=1, source_target_pairs={{20,0},{24,8},{28,24},{52,32},{56,40},{60,56},{84,64},{88,72},{92,... | collective-permute-start | bytes 933896 | tf_op jit(solution)/shard_map/ppermute | solution.py:411
  58.3 5.7 %collective-permute-start.11 = (bf16[38,32,128]{2,1,0:T(8,128)(2,1)}, bf16[38,32,128]{2,1,0:T(8,128)(2,1)}, u32[]{:S(2)}, u32[]{:S(2)}) collective-permute-start(bf16[38,32,128]{2,1,0:T(8,128)(2,1)} %shard_map.39), channel_id=1, source_target_pairs={{24,0},{28,8},{16,24},{56,32},{60,40},{48,56},{88,64},{92,72},{80,... | collective-permute-start | bytes 933896 | tf_op jit(solution)/shard_map/ppermute | solution.py:411
  64.0 10.5 %collective-permute-start.12 = (bf16[38,32,128]{2,1,0:T(8,128)(2,1)}, bf16[38,32,128]{2,1,0:T(8,128)(2,1)}, u32[]{:S(2)}, u32[]{:S(2)}) collective-permute-start(bf16[38,32,128]{2,1,0:T(8,128)(2,1)} %shard_map.40), channel_id=1, source_target_pairs={{28,0},{16,8},{20,24},{60,32},{48,40},{52,56},{92,64},{80,72},{84,... | collective-permute-start | bytes 933896 | tf_op jit(solution)/shard_map/ppermute | solution.py:411
  74.5 3.4 %collective-permute-done.12.refs_7_.refs_3_ = bf16[38,32,128]{2,1,0:T(8,128)(2,1)} collective-permute-done((bf16[38,32,128]{2,1,0:T(8,128)(2,1)}, bf16[38,32,128]{2,1,0:T(8,128)(2,1)}, u32[]{:S(2)}, u32[]{:S(2)}) %collective-permute-start.12) | collective-permute-done | bytes 311328 | tf_op jit(solution)/shard_map/ppermute | solution.py:411
  77.9 2.1 %shard_map.42 = (bf16[32,32,128]{2,1,0:T(8,128)(2,1)}, bf16[32,32,128]{2,1,0:T(8,128)(2,1)}) custom-call(s32[1]{0:T(128)} %bitcast.3.b_ref, bf16[38,32,128]{2,1,0:T(8,128)(2,1)} %copy-done.15, bf16[38,32,128]{2,1,0:T(8,128)(2,1)} %copy-done.16, bf16[38,32,128]{2,1,0:T(8,128)(2,1)} %collective-permute-done.11.refs_6_.refs_2_, ...), custom_call_target="tpu_custom_call" | custom-call | tf_op jit(solution)/shard_map/pallas_call | solution.py:322
  80.7 0.9 collective-permute-start.16
  81.6 3.2 %order.1 = (bf16[16,16,32,128]{3,2,1,0:T(8,128)(2,1)}, bf16[16,3,32,128]{3,2,1,0:T(8,128)(2,1)}) custom-call(s32[1]{0:T(128)} %bitcast.3.b_ref, bf16[38,32,128]{2,1,0:T(8,128)(2,1)} %copy-done.11, bf16[38,32,128]{2,1,0:T(8,128)(2,1)} %copy-done.12, bf16[38,32,128]{2,1,0:T(8,128)(2,1)} %copy-done.13, bf16[38,32,128]{2,1,0:T(8,128)(2,1)} %copy-done.14, ...), custom_call_target="tpu_custom_call" | custom-call | bytes 5000000 | tf_op jit(solution)/shard_map/order/pallas_call | solution.py:347
  86.3 8.3 %sweep.4 = (f32[16,32,128]{2,1,0:T(8,128)}, bf16[16,32,128]{2,1,0:T(8,128)(2,1)}) custom-call(s32[5]{0:T(128)} %stack.23.info_ref, f32[16,32,128]{2,1,0:T(8,128)} %opening.1.refs_4_.v1_ref, bf16[16,16,32,128]{3,2,1,0:T(8,128)(2,1)} %get-tuple-element.25.d_ref, bf16[112,32,128]{2,1,0:T(8,128)(2,1)} %copy-done.1, bf16[112,32,128]{2,1,0:T(8,128)(2,1)} %copy-done.2, ...), custom_call_target="tpu_custom_call" | custom-call | tf_op jit(solution)/shard_map/sweep/pallas_call | solution.py:364
  95.3 0.7 collective-permute-start.19
  95.9 0.7 collective-permute-start.18
  97.3 0.7 copy-done.19
  98.1 8.6 %sweep.5 = (f32[16,32,128]{2,1,0:T(8,128)}, bf16[16,32,128]{2,1,0:T(8,128)(2,1)}) custom-call(s32[5]{0:T(128)} %stack.23.info_ref, f32[16,32,128]{2,1,0:T(8,128)} %opening.1.refs_4_.v1_ref, bf16[16,16,32,128]{3,2,1,0:T(8,128)(2,1)} %get-tuple-element.25.d_ref, bf16[112,32,128]{2,1,0:T(8,128)(2,1)} %copy-done.1, bf16[112,32,128]{2,1,0:T(8,128)(2,1)} %copy-done.2, ...), custom_call_target="tpu_custom_call" | custom-call | tf_op jit(solution)/shard_map/sweep/pallas_call | solution.py:364
  109.4 0.7 copy-done.20
  110.1 8.8 %sweep.6 = (f32[16,32,128]{2,1,0:T(8,128)}, bf16[16,32,128]{2,1,0:T(8,128)(2,1)}) custom-call(s32[5]{0:T(128)} %stack.23.info_ref, f32[16,32,128]{2,1,0:T(8,128)} %opening.1.refs_4_.v1_ref, bf16[16,16,32,128]{3,2,1,0:T(8,128)(2,1)} %get-tuple-element.25.d_ref, bf16[112,32,128]{2,1,0:T(8,128)(2,1)} %copy-done.1, bf16[112,32,128]{2,1,0:T(8,128)(2,1)} %copy-done.2, ...), custom_call_target="tpu_custom_call" | custom-call | tf_op jit(solution)/shard_map/sweep/pallas_call | solution.py:364
  121.6 0.7 copy-done.18
  122.3 9.1 %sweep.7 = (bf16[2,16,32,128]{3,2,1,0:T(8,128)(2,1)}, bf16[2,16,32,128]{3,2,1,0:T(8,128)(2,1)}, bf16[2,16,32,128]{3,2,1,0:T(8,128)(2,1)}, bf16[2,16,32,128]{3,2,...) custom-call(s32[5]{0:T(128)} %stack.23.info_ref, ...), custom_call_target="tpu_custom_call" | custom-call | tf_op jit(solution)/shard_map/sweep/pallas_call | solution.py:364
  131.5 0.7 collective-permute-start.26
  132.1 0.7 collective-permute-start.27
  132.8 0.7 collective-permute-start.28
  133.5 0.7 collective-permute-start.29
  134.2 0.7 collective-permute-start.30
  134.9 1.3 collective-permute-start.31
  136.2 1.3 collective-permute-start.32
  137.5 1.3 collective-permute-start.33
  138.9 47.5 %collective-permute-done.31.refs_5_ = bf16[2,16,32,128]{3,2,1,0:T(8,128)(2,1)S(1)} collective-permute-done((bf16[2,16,32,128]{3,2,1,0:T(8,128)(2,1)}, bf16[2,16,32,128]{3,2,1,0:T(8,128)(2,1)S(1)}, u32[]{:S(2)}, u32[]{:S(2)}) %collective-permute-start.31) | collective-permute-done | bytes 262176 | tf_op jit(solution)/shard_map/ppermute | solution.py:441
  186.4 9.1 %collective-permute-done.32.refs_6_ = bf16[2,16,32,128]{3,2,1,0:T(8,128)(2,1)S(1)} collective-permute-done((bf16[2,16,32,128]{3,2,1,0:T(8,128)(2,1)}, bf16[2,16,32,128]{3,2,1,0:T(8,128)(2,1)S(1)}, u32[]{:S(2)}, u32[]{:S(2)}) %collective-permute-start.32) | collective-permute-done | bytes 262176 | tf_op jit(solution)/shard_map/ppermute | solution.py:441
  195.4 5.5 %collective-permute-done.33.refs_7_ = bf16[2,16,32,128]{3,2,1,0:T(8,128)(2,1)S(1)} collective-permute-done((bf16[2,16,32,128]{3,2,1,0:T(8,128)(2,1)}, bf16[2,16,32,128]{3,2,1,0:T(8,128)(2,1)S(1)}, u32[]{:S(2)}, u32[]{:S(2)}) %collective-permute-start.33) | collective-permute-done | bytes 262176 | tf_op jit(solution)/shard_map/ppermute | solution.py:441
  201.0 0.7 copy-done.28
  201.7 3.8 %finish.1 = f32[3072,128]{1,0:T(8,128)} custom-call(s32[5]{0:T(128)} %stack.23.info_ref, bf16[2,16,32,128]{3,2,1,0:T(8,128)(2,1)} %copy-done.21, bf16[2,16,32,128]{3,2,1,0:T(8,128)(2,1)} %copy-done.22, bf16[2,16,32,128]{3,2,1,0:T(8,128)(2,1)} %copy-done.23, bf16[2,16,32,128]{3,2,1,0:T(8,128)(2,1)} %copy-done.24, bf16[2,16,32,128]{3,2,1,0:T(8,128)(2,1)} %copy-done.25, ...), custom_call_target="tpu_custom_call" | custom-call | tf_op jit(solution)/shard_map/finish/pallas_call | solution.py:332
  (114 shorter events, 14.2 us)
Async XLA Ops:
  1.2 1.9 copy-start.9
  2.8 5.8 %copy-start.5 = (bf16[8,32,288]{2,1,0:T(8,128)(2,1)S(1)}, bf16[8,32,288]{2,1,0:T(8,128)(2,1)}, u32[]{:S(2)}) copy-start(bf16[8,32,288]{2,1,0:T(8,128)(2,1)} %here_ref.7) | copy-start | bytes 442372
  3.1 13.6 %collective-permute-start = (bf16[7,4,32,128]{3,2,1,0:T(8,128)(2,1)S(1)}, bf16[7,4,32,128]{3,2,1,0:T(8,128)(2,1)S(1)}, u32[]{:S(2)}, u32[]{:S(2)}) collective-permute-start(bf16[7,4,32,128]{3,2,1,0:T(8,128)(2,1)S(1)} %maximum_bitcast_fusion), channel_id=1, source_target_pairs={{0,1},{1,2},{2,3},{4,5},{5,6},{6,7},{8,9},{9,10},{10,11},{12,13},{... | collective-permute-start | bytes 688136 | tf_op jit(solution)/shard_map/ppermute | solution.py:389
  6.7 10.0 %collective-permute-start.1 = (bf16[7,4,32,128]{3,2,1,0:T(8,128)(2,1)S(1)}, bf16[7,4,32,128]{3,2,1,0:T(8,128)(2,1)S(1)}, u32[]{:S(2)}, u32[]{:S(2)}) collective-permute-start(bf16[7,4,32,128]{3,2,1,0:T(8,128)(2,1)S(1)} %maximum_bitcast_fusion.1), channel_id=1, source_target_pairs={{1,0},{2,1},{3,2},{5,4},{6,5},{7,6},{9,8},{10,9},{11,10},{13,12},{... | collective-permute-start | bytes 688136 | tf_op jit(solution)/shard_map/ppermute | solution.py:390
  8.6 8.0 %collective-permute-start.4 = (bf16[4,32,288]{2,1,0:T(8,128)(2,1)S(1)}, bf16[4,32,288]{2,1,0:T(8,128)(2,1)S(1)}, u32[]{:S(2)}, u32[]{:S(2)}) collective-permute-start(bf16[4,32,288]{2,1,0:T(8,128)(2,1)S(1)} %slice.23), channel_id=1, source_target_pairs={{4,0},{8,4},{12,8},{16,12},{20,16},{24,20},{28,24},{32,28},{36,32}... | collective-permute-start | bytes 221192 | tf_op jit(solution)/shard_map/ppermute | solution.py:391
  11.6 23.0 %collective-permute-start.3 = (bf16[4,32,288]{2,1,0:T(8,128)(2,1)S(1)}, bf16[4,32,288]{2,1,0:T(8,128)(2,1)S(1)}, u32[]{:S(2)}, u32[]{:S(2)}) collective-permute-start(bf16[4,32,288]{2,1,0:T(8,128)(2,1)S(1)} %slice.23), channel_id=1, source_target_pairs={{0,8},{1,9},{2,10},{3,11}} | collective-permute-start | bytes 221192 | tf_op jit(solution)/shard_map/ppermute | solution.py:394
  19.9 18.1 %collective-permute-start.5 = (bf16[38,32,128]{2,1,0:T(8,128)(2,1)}, bf16[38,32,128]{2,1,0:T(8,128)(2,1)S(1)}, u32[]{:S(2)}, u32[]{:S(2)}) collective-permute-start(bf16[38,32,128]{2,1,0:T(8,128)(2,1)} %shard_map.37), channel_id=1, source_target_pairs={{0,0},{4,8},{8,24},{32,32},{36,40},{40,56},{64,64},{68,72},{72,88}... | collective-permute-start | bytes 933896 | tf_op jit(solution)/shard_map/ppermute | solution.py:411
  24.5 13.5 %collective-permute-start.6 = (bf16[38,32,128]{2,1,0:T(8,128)(2,1)}, bf16[38,32,128]{2,1,0:T(8,128)(2,1)S(1)}, u32[]{:S(2)}, u32[]{:S(2)}) collective-permute-start(bf16[38,32,128]{2,1,0:T(8,128)(2,1)} %shard_map.38), channel_id=1, source_target_pairs={{4,0},{8,8},{12,24},{36,32},{40,40},{44,56},{68,64},{72,72},{76,88... | collective-permute-start | bytes 933896 | tf_op jit(solution)/shard_map/ppermute | solution.py:411
  29.1 6.2 %copy-start.6 = (bf16[8,32,288]{2,1,0:T(8,128)(2,1)S(1)}, bf16[8,32,288]{2,1,0:T(8,128)(2,1)}, u32[]{:S(2)}) copy-start(bf16[8,32,288]{2,1,0:T(8,128)(2,1)} %here_ref.7) | copy-start | bytes 442372
  29.1 8.9 %collective-permute-start.7 = (bf16[38,32,128]{2,1,0:T(8,128)(2,1)}, bf16[38,32,128]{2,1,0:T(8,128)(2,1)S(1)}, u32[]{:S(2)}, u32[]{:S(2)}) collective-permute-start(bf16[38,32,128]{2,1,0:T(8,128)(2,1)} %shard_map.39), channel_id=1, source_target_pairs={{8,0},{12,8},{0,24},{40,32},{44,40},{32,56},{72,64},{76,72},{64,88... | collective-permute-start | bytes 933896 | tf_op jit(solution)/shard_map/ppermute | solution.py:411
  33.8 10.8 %copy-start.17 = (bf16[38,32,128]{2,1,0:T(8,128)(2,1)S(1)}, bf16[38,32,128]{2,1,0:T(8,128)(2,1)}, u32[]{:S(2)}) copy-start(bf16[38,32,128]{2,1,0:T(8,128)(2,1)} %shard_map.38) | copy-start | bytes 933892
  33.8 4.1 %collective-permute-start.8 = (bf16[38,32,128]{2,1,0:T(8,128)(2,1)}, bf16[38,32,128]{2,1,0:T(8,128)(2,1)S(1)}, u32[]{:S(2)}, u32[]{:S(2)}) collective-permute-start(bf16[38,32,128]{2,1,0:T(8,128)(2,1)} %shard_map.40), channel_id=1, source_target_pairs={{12,0},{0,8},{4,24},{44,32},{32,40},{36,56},{76,64},{64,72},{68,88... | collective-permute-start | bytes 933896 | tf_op jit(solution)/shard_map/ppermute | solution.py:411
  34.7 0.7 collective-permute-start.2
  42.5 42.4 %collective-permute-start.13 = (bf16[112,32,128]{2,1,0:T(8,128)(2,1)}, bf16[112,32,128]{2,1,0:T(8,128)(2,1)S(1)}, u32[]{:S(2)}, u32[]{:S(2)}) collective-permute-start(bf16[112,32,128]{2,1,0:T(8,128)(2,1)} %get-tuple-element.26), channel_id=1, source_target_pairs={{0,1},{1,2},{2,3},{8,9},{9,10},{10,11},{24,25},{25,26},{26,27},{32... | collective-permute-start | bytes 2752520 | tf_op jit(solution)/shard_map/ppermute | solution.py:423
  43.2 41.7 %collective-permute-start.14 = (bf16[112,32,128]{2,1,0:T(8,128)(2,1)}, bf16[112,32,128]{2,1,0:T(8,128)(2,1)S(1)}, u32[]{:S(2)}, u32[]{:S(2)}) collective-permute-start(bf16[112,32,128]{2,1,0:T(8,128)(2,1)} %get-tuple-element.27), channel_id=1, source_target_pairs={{1,0},{2,1},{3,2},{9,8},{10,9},{11,10},{25,24},{26,25},{27,26},{33... | collective-permute-start | bytes 2752520 | tf_op jit(solution)/shard_map/ppermute | solution.py:423
  43.9 20.1 %collective-permute-start.9 = (bf16[38,32,128]{2,1,0:T(8,128)(2,1)}, bf16[38,32,128]{2,1,0:T(8,128)(2,1)S(1)}, u32[]{:S(2)}, u32[]{:S(2)}) collective-permute-start(bf16[38,32,128]{2,1,0:T(8,128)(2,1)} %shard_map.37), channel_id=1, source_target_pairs={{16,0},{20,8},{24,24},{48,32},{52,40},{56,56},{80,64},{84,72},{88,... | collective-permute-start | bytes 933896 | tf_op jit(solution)/shard_map/ppermute | solution.py:411
  44.6 29.9 %collective-permute-start.10 = (bf16[38,32,128]{2,1,0:T(8,128)(2,1)S(1)}, bf16[38,32,128]{2,1,0:T(8,128)(2,1)S(1)}, u32[]{:S(2)}, u32[]{:S(2)}) collective-permute-start(bf16[38,32,128]{2,1,0:T(8,128)(2,1)S(1)} %copy-done.17), channel_id=1, source_target_pairs={{20,0},{24,8},{28,24},{52,32},{56,40},{60,56},{84,64},{88,72},{92,... | collective-permute-start | bytes 933896 | tf_op jit(solution)/shard_map/ppermute | solution.py:411
  58.3 16.2 %collective-permute-start.11 = (bf16[38,32,128]{2,1,0:T(8,128)(2,1)}, bf16[38,32,128]{2,1,0:T(8,128)(2,1)}, u32[]{:S(2)}, u32[]{:S(2)}) collective-permute-start(bf16[38,32,128]{2,1,0:T(8,128)(2,1)} %shard_map.39), channel_id=1, source_target_pairs={{24,0},{28,8},{16,24},{56,32},{60,40},{48,56},{88,64},{92,72},{80,... | collective-permute-start | bytes 933896 | tf_op jit(solution)/shard_map/ppermute | solution.py:411
  64.0 13.9 %copy-start.15 = (bf16[38,32,128]{2,1,0:T(8,128)(2,1)}, bf16[38,32,128]{2,1,0:T(8,128)(2,1)S(1)}, u32[]{:S(2)}) copy-start(bf16[38,32,128]{2,1,0:T(8,128)(2,1)S(1)} %collective-permute-done.9.refs_4_.refs_0_) | copy-start | bytes 933892
  64.0 13.9 %collective-permute-start.12 = (bf16[38,32,128]{2,1,0:T(8,128)(2,1)}, bf16[38,32,128]{2,1,0:T(8,128)(2,1)}, u32[]{:S(2)}, u32[]{:S(2)}) collective-permute-start(bf16[38,32,128]{2,1,0:T(8,128)(2,1)} %shard_map.40), channel_id=1, source_target_pairs={{28,0},{16,8},{20,24},{60,32},{48,40},{52,56},{92,64},{80,72},{84,... | collective-permute-start | bytes 933896 | tf_op jit(solution)/shard_map/ppermute | solution.py:411
  74.5 3.4 %copy-start.16 = (bf16[38,32,128]{2,1,0:T(8,128)(2,1)}, bf16[38,32,128]{2,1,0:T(8,128)(2,1)S(1)}, u32[]{:S(2)}) copy-start(bf16[38,32,128]{2,1,0:T(8,128)(2,1)S(1)} %collective-permute-done.10.refs_5_.refs_1_) | copy-start | bytes 933892
  80.1 4.8 %collective-permute-start.15 = (bf16[32,32,128]{2,1,0:T(8,128)(2,1)}, bf16[32,32,128]{2,1,0:T(8,128)(2,1)S(1)}, u32[]{:S(2)}, u32[]{:S(2)}) collective-permute-start(bf16[32,32,128]{2,1,0:T(8,128)(2,1)} %get-tuple-element.28), channel_id=1, source_target_pairs={{0,1},{1,2},{2,3},{8,9},{9,10},{10,11},{24,25},{25,26},{26,27},{32... | collective-permute-start | bytes 786440 | tf_op jit(solution)/shard_map/ppermute | solution.py:423
  80.7 4.1 %collective-permute-start.16 = (bf16[32,32,128]{2,1,0:T(8,128)(2,1)}, bf16[32,32,128]{2,1,0:T(8,128)(2,1)S(1)}, u32[]{:S(2)}, u32[]{:S(2)}) collective-permute-start(bf16[32,32,128]{2,1,0:T(8,128)(2,1)} %get-tuple-element.29), channel_id=1, source_target_pairs={{1,0},{2,1},{3,2},{9,8},{10,9},{11,10},{25,24},{26,25},{27,26},{33... | collective-permute-start | bytes 786440 | tf_op jit(solution)/shard_map/ppermute | solution.py:423
  84.9 1.4 copy-start.2
  94.6 2.1 %collective-permute-start.17 = (f32[16,32,128]{2,1,0:T(8,128)}, f32[16,32,128]{2,1,0:T(8,128)S(1)}, u32[]{:S(2)}, u32[]{:S(2)}) collective-permute-start(f32[16,32,128]{2,1,0:T(8,128)} %get-tuple-element.31), channel_id=1, source_target_pairs={{0,32},{1,33},{2,34},{3,35},{8,40},{9,41},{10,42},{11,43},{24,56},... | collective-permute-start | bytes 786440 | tf_op jit(solution)/shard_map/ppermute | solution.py:423
  95.3 1.4 collective-permute-start.19
  95.9 0.7 collective-permute-start.18
  106.6 2.1 %collective-permute-start.20 = (f32[16,32,128]{2,1,0:T(8,128)}, f32[16,32,128]{2,1,0:T(8,128)S(1)}, u32[]{:S(2)}, u32[]{:S(2)}) collective-permute-start(f32[16,32,128]{2,1,0:T(8,128)} %get-tuple-element.33), channel_id=1, source_target_pairs={{0,32},{1,33},{2,34},{3,35},{8,40},{9,41},{10,42},{11,43},{24,56},... | collective-permute-start | bytes 786440 | tf_op jit(solution)/shard_map/ppermute | solution.py:423
  107.3 1.4 collective-permute-start.22
  108.0 0.7 collective-permute-start.21
  118.9 2.1 %collective-permute-start.23 = (f32[16,32,128]{2,1,0:T(8,128)}, f32[16,32,128]{2,1,0:T(8,128)S(1)}, u32[]{:S(2)}, u32[]{:S(2)}) collective-permute-start(f32[16,32,128]{2,1,0:T(8,128)} %get-tuple-element.35), channel_id=1, source_target_pairs={{0,32},{1,33},{2,34},{3,35},{8,40},{9,41},{10,42},{11,43},{24,56},... | collective-permute-start | bytes 786440 | tf_op jit(solution)/shard_map/ppermute | solution.py:423
  119.6 1.4 collective-permute-start.25
  120.2 0.7 collective-permute-start.24
  131.5 3.4 %collective-permute-start.26 = (bf16[2,16,32,128]{3,2,1,0:T(8,128)(2,1)}, bf16[2,16,32,128]{3,2,1,0:T(8,128)(2,1)S(1)}, u32[]{:S(2)}, u32[]{:S(2)}) collective-permute-start(bf16[2,16,32,128]{3,2,1,0:T(8,128)(2,1)} %get-tuple-element.37), channel_id=1, source_target_pairs={{0,0},{8,4},{24,8},{32,32},{40,36},{56,40},{64,64},{72,68},{88,72}... | collective-permute-start | bytes 786440 | tf_op jit(solution)/shard_map/ppermute | solution.py:441
  132.1 4.1 %collective-permute-start.27 = (bf16[2,16,32,128]{3,2,1,0:T(8,128)(2,1)}, bf16[2,16,32,128]{3,2,1,0:T(8,128)(2,1)S(1)}, u32[]{:S(2)}, u32[]{:S(2)}) collective-permute-start(bf16[2,16,32,128]{3,2,1,0:T(8,128)(2,1)} %get-tuple-element.38), channel_id=1, source_target_pairs={{0,4},{8,8},{24,12},{32,36},{40,40},{56,44},{64,68},{72,72},{88,76... | collective-permute-start | bytes 786440 | tf_op jit(solution)/shard_map/ppermute | solution.py:441
  132.8 4.7 %collective-permute-start.28 = (bf16[2,16,32,128]{3,2,1,0:T(8,128)(2,1)}, bf16[2,16,32,128]{3,2,1,0:T(8,128)(2,1)S(1)}, u32[]{:S(2)}, u32[]{:S(2)}) collective-permute-start(bf16[2,16,32,128]{3,2,1,0:T(8,128)(2,1)} %get-tuple-element.39), channel_id=1, source_target_pairs={{0,8},{8,12},{24,0},{32,40},{40,44},{56,32},{64,72},{72,76},{88,64... | collective-permute-start | bytes 786440 | tf_op jit(solution)/shard_map/ppermute | solution.py:441
  133.5 5.3 %collective-permute-start.29 = (bf16[2,16,32,128]{3,2,1,0:T(8,128)(2,1)}, bf16[2,16,32,128]{3,2,1,0:T(8,128)(2,1)S(1)}, u32[]{:S(2)}, u32[]{:S(2)}) collective-permute-start(bf16[2,16,32,128]{3,2,1,0:T(8,128)(2,1)} %get-tuple-element.40), channel_id=1, source_target_pairs={{0,12},{8,0},{24,4},{32,44},{40,32},{56,36},{64,76},{72,64},{88,68... | collective-permute-start | bytes 786440 | tf_op jit(solution)/shard_map/ppermute | solution.py:441
  134.2 4.7 %collective-permute-start.30 = (bf16[2,16,32,128]{3,2,1,0:T(8,128)(2,1)}, bf16[2,16,32,128]{3,2,1,0:T(8,128)(2,1)S(1)}, u32[]{:S(2)}, u32[]{:S(2)}) collective-permute-start(bf16[2,16,32,128]{3,2,1,0:T(8,128)(2,1)} %get-tuple-element.41), channel_id=1, source_target_pairs={{0,16},{8,20},{24,24},{32,48},{40,52},{56,56},{64,80},{72,84},{88,... | collective-permute-start | bytes 786440 | tf_op jit(solution)/shard_map/ppermute | solution.py:441
  134.9 66.1 %copy-start.21 = (bf16[2,16,32,128]{3,2,1,0:T(8,128)(2,1)}, bf16[2,16,32,128]{3,2,1,0:T(8,128)(2,1)S(1)}, u32[]{:S(2)}) copy-start(bf16[2,16,32,128]{3,2,1,0:T(8,128)(2,1)S(1)} %collective-permute-done.26.refs_0_) | copy-start | bytes 786436
  134.9 51.5 %collective-permute-start.31 = (bf16[2,16,32,128]{3,2,1,0:T(8,128)(2,1)}, bf16[2,16,32,128]{3,2,1,0:T(8,128)(2,1)S(1)}, u32[]{:S(2)}, u32[]{:S(2)}) collective-permute-start(bf16[2,16,32,128]{3,2,1,0:T(8,128)(2,1)} %get-tuple-element.42), channel_id=1, source_target_pairs={{0,20},{8,24},{24,28},{32,52},{40,56},{56,60},{64,84},{72,88},{88,... | collective-permute-start | bytes 786440 | tf_op jit(solution)/shard_map/ppermute | solution.py:441
  136.2 64.8 %copy-start.22 = (bf16[2,16,32,128]{3,2,1,0:T(8,128)(2,1)}, bf16[2,16,32,128]{3,2,1,0:T(8,128)(2,1)S(1)}, u32[]{:S(2)}) copy-start(bf16[2,16,32,128]{3,2,1,0:T(8,128)(2,1)S(1)} %collective-permute-done.27.refs_1_) | copy-start | bytes 786436
  136.2 59.2 %collective-permute-start.32 = (bf16[2,16,32,128]{3,2,1,0:T(8,128)(2,1)}, bf16[2,16,32,128]{3,2,1,0:T(8,128)(2,1)S(1)}, u32[]{:S(2)}, u32[]{:S(2)}) collective-permute-start(bf16[2,16,32,128]{3,2,1,0:T(8,128)(2,1)} %get-tuple-element.43), channel_id=1, source_target_pairs={{0,24},{8,28},{24,16},{32,56},{40,60},{56,48},{64,88},{72,92},{88,... | collective-permute-start | bytes 786440 | tf_op jit(solution)/shard_map/ppermute | solution.py:441
  137.5 63.4 %copy-start.23 = (bf16[2,16,32,128]{3,2,1,0:T(8,128)(2,1)}, bf16[2,16,32,128]{3,2,1,0:T(8,128)(2,1)S(1)}, u32[]{:S(2)}) copy-start(bf16[2,16,32,128]{3,2,1,0:T(8,128)(2,1)S(1)} %collective-permute-done.28.refs_2_) | copy-start | bytes 786436
  137.5 63.4 %collective-permute-start.33 = (bf16[2,16,32,128]{3,2,1,0:T(8,128)(2,1)}, bf16[2,16,32,128]{3,2,1,0:T(8,128)(2,1)S(1)}, u32[]{:S(2)}, u32[]{:S(2)}) collective-permute-start(bf16[2,16,32,128]{3,2,1,0:T(8,128)(2,1)} %get-tuple-element.44), channel_id=1, source_target_pairs={{0,28},{8,16},{24,20},{32,60},{40,48},{56,52},{64,92},{72,80},{88,... | collective-permute-start | bytes 786440 | tf_op jit(solution)/shard_map/ppermute | solution.py:441
  138.9 62.1 %copy-start.24 = (bf16[2,16,32,128]{3,2,1,0:T(8,128)(2,1)}, bf16[2,16,32,128]{3,2,1,0:T(8,128)(2,1)S(1)}, u32[]{:S(2)}) copy-start(bf16[2,16,32,128]{3,2,1,0:T(8,128)(2,1)S(1)} %collective-permute-done.29.refs_3_) | copy-start | bytes 786436
  138.9 62.1 %copy-start.25 = (bf16[2,16,32,128]{3,2,1,0:T(8,128)(2,1)}, bf16[2,16,32,128]{3,2,1,0:T(8,128)(2,1)S(1)}, u32[]{:S(2)}) copy-start(bf16[2,16,32,128]{3,2,1,0:T(8,128)(2,1)S(1)} %collective-permute-done.30.refs_4_) | copy-start | bytes 786436
  186.4 14.6 %copy-start.26 = (bf16[2,16,32,128]{3,2,1,0:T(8,128)(2,1)}, bf16[2,16,32,128]{3,2,1,0:T(8,128)(2,1)S(1)}, u32[]{:S(2)}) copy-start(bf16[2,16,32,128]{3,2,1,0:T(8,128)(2,1)S(1)} %collective-permute-done.31.refs_5_) | copy-start | bytes 786436
  195.4 5.6 %copy-start.27 = (bf16[2,16,32,128]{3,2,1,0:T(8,128)(2,1)}, bf16[2,16,32,128]{3,2,1,0:T(8,128)(2,1)S(1)}, u32[]{:S(2)}) copy-start(bf16[2,16,32,128]{3,2,1,0:T(8,128)(2,1)S(1)} %collective-permute-done.32.refs_6_) | copy-start | bytes 786436
  (21 other events, 15.9 us)

commit v2 on v0

--- a/solution.py
+++ b/solution.py
@@ -277,6 +277,7 @@
 
 
 VM = pl.BlockSpec(memory_space=pltpu.VMEM)
+GRANT = pltpu.CompilerParams(vmem_limit_bytes=18 * 1024 * 1024)
 SM = pl.BlockSpec(memory_space=pltpu.SMEM)
 AN = pl.BlockSpec(memory_space=pl.ANY)
 
@@ -298,6 +299,7 @@
             pltpu.VMEM((FLOW, CHUNK, C, W), bf16),
             pltpu.SemaphoreType.DMA((FLOW,)),
         ],
+        compiler_params=GRANT,
         name="relax",
     )(info, *arrays)
     return outs[:FLOW], outs[FLOW]
@@ -311,6 +313,7 @@
         in_specs=[SM] + [VM] * len(arrays),
         out_specs=(VM, VM),
         scratch_shapes=[pltpu.VMEM((SUB, BAND, C, W), bf16)],
+        compiler_params=GRANT,
     )(b, *arrays)
 
 
@@ -325,6 +328,7 @@
             pltpu.VMEM((IMAGES, 2, BAND * C, W), f32),
             pltpu.SemaphoreType.DMA((IMAGES,)),
         ],
+        compiler_params=GRANT,
         name="finish",
     )(info, *arrays)
 
@@ -336,6 +340,7 @@
         in_specs=[SM] + [VM] * SUB,
         out_specs=(VM, VM),
         cost_estimate=pl.CostEstimate(flops=0, bytes_accessed=5_000_000, transcendentals=0),
+        compiler_params=GRANT,
         name="order",
     )(sub, *chunks)
 
@@ -353,6 +358,7 @@
         in_specs=[SM] + [VM] * len(arrays),
         out_specs=(AN,) * SUB if closing else (VM, VM),
         scratch_shapes=[pltpu.VMEM((2, WIN + 2, 3, C, W), bf16), pltpu.VMEM((WIN, C, W), f32)] + extra,
+        compiler_params=GRANT,
         name="sweep",
     )(info, *arrays)
 

time: 207 us -> 179 us (0.86)
  Pallas kernels: 55.3 us -> 33 us
  local copies, waits for them, and re-layouts: 10 us -> 1.43 us
  waiting for transfers between devices: 69.9 us -> 72.1 us
    pallas_call x4, Pallas kernels: 35 us -> 24 us  [sweep(): pl.pallas_call(functools.partial(sweep_kernel, opening, closing), out_sha...]
    unnamed x67 -> x7, local copies, waits for them, and re-layouts: 8.12 us -> 0.11 us
    pallas_call x2, Pallas kernels: 4.97 us -> 0.37 us  [rims(): pl.pallas_call(functools.partial(rim_kernel, half), out_shape=(shape(tota...]
    pallas_call x1, Pallas kernels: 3.26 us -> 0.17 us  [order(): pl.pallas_call(order_kernel, out_shape=(shape(STEPS, BAND, C, W), shape(S...]
    pallas_call x1, Pallas kernels: 8.2 us -> 5.53 us  [relax(): pl.pallas_call(relax_kernel, out_shape=(shape(CHUNK, C, W),) * FLOW + (sh...]
  transfers between devices with their start and end apart: 34 -> 34, of which waited for: 6 -> 6; matrix products, arithmetic and copies ran while one was open for 2% -> 2% of each run, Pallas kernels for 3% -> 0%
where the time goes in v2:
time: 179 us; the launch traced here: 178 us
  waiting for transfers between devices  72.1 us (40%)
  starting transfers between devices  67.8 us (38%)
  Pallas kernels  33 us (18%)
  other arithmetic  2.97 us (2%)
    ppermute x8, waiting for transfers between devices, cycle(): lax.ppermute(results[FLOW * h + k], 'layer', [(t, s) for s, t in pairs(h,...  61.6 us
    ppermute x8, starting transfers between devices, cycle(): lax.ppermute(sends[k], 'layer', pairs(h, k))  41.1 us
    pallas_call x4, Pallas kernels, sweep(): pl.pallas_call(functools.partial(sweep_kernel, opening, closing), out_sha...  24 us
    ppermute x13, starting transfers between devices, among_sweepers(): return lax.ppermute(value, ('layer', 'rows'), pairs)  8.84 us
    ppermute x8, starting transfers between devices, cycle(): lax.ppermute(results[FLOW * h + k], 'layer', [(t, s) for s, t in pairs(h,...  7.26 us
    pallas_call x1, Pallas kernels, relax(): pl.pallas_call(relax_kernel, out_shape=(shape(CHUNK, C, W),) * FLOW + (sh...  5.53 us
    ppermute x1, waiting for transfers between devices, cycle(): lax.ppermute(edge_rows(0), 'rows', [(i + 1, i) for i in range(rows - 1)])  3.96 us
    ppermute x8, waiting for transfers between devices, cycle(): lax.ppermute(sends[k], 'layer', pairs(h, k))  3.8 us
  transfers between devices with their start and end apart: 34, of which 6 were waited for; matrix products, arithmetic and copies ran while one was open for 2% of the time, Pallas kernels for 0%

profile of v2, /device:TPU:59, one launch (start us, length us, event | category | flops | bytes accessed | tf_op | source)
XLA Modules:
  0.0 178.2 jit_solution(8504860219227509027)
XLA Ops:
  0.0 1.0 slice.23
  1.0 1.3 collective-permute-start.4
  2.3 1.3 collective-permute-start.3
  3.6 2.6 %collective-permute-start.2 = (bf16[4,32,288]{2,1,0:T(8,128)(2,1)S(1)}, bf16[4,32,288]{2,1,0:T(8,128)(2,1)S(1)}, u32[]{:S(2)}, u32[]{:S(2)}) collective-permute-start(bf16[4,32,288]{2,1,0:T(8,128)(2,1)S(1)} %slice.23), channel_id=1, source_target_pairs={{4,0},{8,4},{12,8},{16,12},{20,16},{24,20},{28,24},{32,28},{36,32}... | collective-permute-start | bytes 221192 | tf_op jit(solution)/shard_map/ppermute | solution.py:383
  6.3 1.5 convert.16
  8.1 0.7 maximum_bitcast_fusion
  8.8 3.5 %collective-permute-start = (bf16[7,4,32,128]{3,2,1,0:T(8,128)(2,1)}, bf16[7,4,32,128]{3,2,1,0:T(8,128)(2,1)S(1)}, u32[]{:S(2)}, u32[]{:S(2)}) collective-permute-start(bf16[7,4,32,128]{3,2,1,0:T(8,128)(2,1)} %maximum_bitcast_fusion), channel_id=1, source_target_pairs={{0,1},{1,2},{2,3},{4,5},{5,6},{6,7},{8,9},{9,10},{10,11},{12,13},{... | collective-permute-start | bytes 688136 | tf_op jit(solution)/shard_map/ppermute | solution.py:381
  12.4 0.7 maximum_bitcast_fusion.1
  13.1 1.9 %collective-permute-start.1 = (bf16[7,4,32,128]{3,2,1,0:T(8,128)(2,1)}, bf16[7,4,32,128]{3,2,1,0:T(8,128)(2,1)S(1)}, u32[]{:S(2)}, u32[]{:S(2)}) collective-permute-start(bf16[7,4,32,128]{3,2,1,0:T(8,128)(2,1)} %maximum_bitcast_fusion.1), channel_id=1, source_target_pairs={{1,0},{2,1},{3,2},{5,4},{6,5},{7,6},{9,8},{10,9},{11,10},{13,12},{... | collective-permute-start | bytes 688136 | tf_op jit(solution)/shard_map/ppermute | solution.py:382
  15.2 2.7 %collective-permute-done.up_ref = bf16[7,4,32,128]{3,2,1,0:T(8,128)(2,1)S(1)} collective-permute-done((bf16[7,4,32,128]{3,2,1,0:T(8,128)(2,1)}, bf16[7,4,32,128]{3,2,1,0:T(8,128)(2,1)S(1)}, u32[]{:S(2)}, u32[]{:S(2)}) %collective-permute-start) | collective-permute-done | bytes 229408 | tf_op jit(solution)/shard_map/ppermute | solution.py:381
  17.9 4.0 %collective-permute-done.1.dn_ref = bf16[7,4,32,128]{3,2,1,0:T(8,128)(2,1)S(1)} collective-permute-done((bf16[7,4,32,128]{3,2,1,0:T(8,128)(2,1)}, bf16[7,4,32,128]{3,2,1,0:T(8,128)(2,1)S(1)}, u32[]{:S(2)}, u32[]{:S(2)}) %collective-permute-start.1) | collective-permute-done | bytes 229408 | tf_op jit(solution)/shard_map/ppermute | solution.py:382
  21.9 5.5 %relax.1 = (bf16[38,32,128]{2,1,0:T(8,128)(2,1)S(1)}, bf16[38,32,128]{2,1,0:T(8,128)(2,1)S(1)}, bf16[38,32,128]{2,1,0:T(8,128)(2,1)S(1)}, bf16[38,32,128]{2,1,0:T(8,128)(2,1)S(1)}, f32[16,32,128]{2,1,0:T(8,128)S(1)}) custom-call(s32[5]{0:T(128)S(1)} %stack.23.info_ref, f32[3072,128]{1,0:T(8,128)S(1)} %bitcast.20, ...), custom_call_target="tpu_custom_call" | custom-call | tf_op jit(solution)/shard_map/relax/pallas_call | solution.py:290
  27.4 0.7 collective-permute-start.5
  28.1 0.7 collective-permute-start.6
  28.8 0.7 collective-permute-start.7
  29.5 0.7 collective-permute-start.8
  30.5 0.7 collective-permute-start.13
  31.2 0.7 collective-permute-start.14
  31.9 0.7 collective-permute-start.9
  32.6 25.2 %collective-permute-start.10 = (bf16[38,32,128]{2,1,0:T(8,128)(2,1)S(1)}, bf16[38,32,128]{2,1,0:T(8,128)(2,1)S(1)}, u32[]{:S(2)}, u32[]{:S(2)}) collective-permute-start(bf16[38,32,128]{2,1,0:T(8,128)(2,1)S(1)} %get-tuple-element.32), channel_id=1, source_target_pairs={{20,0},{24,8},{28,24},{52,32},{56,40},{60,56},{84,64},{88,72},{92,... | collective-permute-start | bytes 933896 | tf_op jit(solution)/shard_map/ppermute | solution.py:402
  57.8 1.3 collective-permute-start.11
  59.1 11.2 %collective-permute-start.12 = (bf16[38,32,128]{2,1,0:T(8,128)(2,1)S(1)}, bf16[38,32,128]{2,1,0:T(8,128)(2,1)S(1)}, u32[]{:S(2)}, u32[]{:S(2)}) collective-permute-start(bf16[38,32,128]{2,1,0:T(8,128)(2,1)S(1)} %get-tuple-element.34), channel_id=1, source_target_pairs={{28,0},{16,8},{20,24},{60,32},{48,40},{52,56},{92,64},{80,72},{84,... | collective-permute-start | bytes 933896 | tf_op jit(solution)/shard_map/ppermute | solution.py:402
  70.3 3.8 %collective-permute-done.12.refs_7_.refs_3_ = bf16[38,32,128]{2,1,0:T(8,128)(2,1)S(1)} collective-permute-done((bf16[38,32,128]{2,1,0:T(8,128)(2,1)S(1)}, bf16[38,32,128]{2,1,0:T(8,128)(2,1)S(1)}, u32[]{:S(2)}, u32[]{:S(2)}) %collective-permute-start.12) | collective-permute-done | bytes 311328 | tf_op jit(solution)/shard_map/ppermute | solution.py:402
  74.2 0.7 collective-permute-start.15
  74.9 0.7 collective-permute-start.16
  75.8 5.8 %sweep.4 = (f32[16,32,128]{2,1,0:T(8,128)S(1)}, bf16[16,32,128]{2,1,0:T(8,128)(2,1)S(1)}) custom-call(s32[5]{0:T(128)S(1)} %stack.23.info_ref, f32[16,32,128]{2,1,0:T(8,128)S(1)} %get-tuple-element.30.refs_4_.v1_ref, bf16[16,16,32,128]{3,2,1,0:T(8,128)(2,1)S(1)} %get-tuple-element.35.d_ref, bf16[112,32,128]{2,1,0:T(8,128)(2,1)S(1)} %collective-permute-done.13.up0_ref, ...), custom_call_target="tpu_custom_call" | custom-call | tf_op jit(solution)/shard_map/sweep/pallas_call | solution.py:355
  81.6 0.7 collective-permute-start.17
  82.3 0.7 collective-permute-start.19
  83.0 0.7 collective-permute-start.18
  83.7 6.1 %sweep.5 = (f32[16,32,128]{2,1,0:T(8,128)S(1)}, bf16[16,32,128]{2,1,0:T(8,128)(2,1)S(1)}) custom-call(s32[5]{0:T(128)S(1)} %stack.23.info_ref, f32[16,32,128]{2,1,0:T(8,128)S(1)} %get-tuple-element.30.refs_4_.v1_ref, bf16[16,16,32,128]{3,2,1,0:T(8,128)(2,1)S(1)} %get-tuple-element.35.d_ref, bf16[112,32,128]{2,1,0:T(8,128)(2,1)S(1)} %collective-permute-done.13.up0_ref, ...), custom_call_target="tpu_custom_call" | custom-call | tf_op jit(solution)/shard_map/sweep/pallas_call | solution.py:355
  89.8 0.7 collective-permute-start.20
  90.4 0.7 collective-permute-start.22
  91.1 0.7 collective-permute-start.21
  91.8 5.9 %sweep.6 = (f32[16,32,128]{2,1,0:T(8,128)S(1)}, bf16[16,32,128]{2,1,0:T(8,128)(2,1)S(1)}) custom-call(s32[5]{0:T(128)S(1)} %stack.23.info_ref, f32[16,32,128]{2,1,0:T(8,128)S(1)} %get-tuple-element.30.refs_4_.v1_ref, bf16[16,16,32,128]{3,2,1,0:T(8,128)(2,1)S(1)} %get-tuple-element.35.d_ref, bf16[112,32,128]{2,1,0:T(8,128)(2,1)S(1)} %collective-permute-done.13.up0_ref, ...), custom_call_target="tpu_custom_call" | custom-call | tf_op jit(solution)/shard_map/sweep/pallas_call | solution.py:355
  97.7 0.7 collective-permute-start.23
  99.8 6.3 %sweep.7 = (bf16[2,16,32,128]{3,2,1,0:T(8,128)(2,1)S(1)}, bf16[2,16,32,128]{3,2,1,0:T(8,128)(2,1)S(1)}, bf16[2,16,32,128]{3,2,1,0:T(8,128)(2,1)S(1)}, bf16[2,16,...) custom-call(s32[5]{0:T(128)S(1)} %stack.23.info_ref, ...), custom_call_target="tpu_custom_call" | custom-call | tf_op jit(solution)/shard_map/sweep/pallas_call | solution.py:355
  106.1 0.7 collective-permute-start.26
  106.7 0.7 collective-permute-start.27
  107.4 0.7 collective-permute-start.28
  108.1 0.7 collective-permute-start.29
  108.8 0.7 collective-permute-start.30
  109.5 1.3 collective-permute-start.31
  110.8 1.3 collective-permute-start.32
  112.1 1.3 collective-permute-start.33
  113.4 47.0 %collective-permute-done.31.refs_5_ = bf16[2,16,32,128]{3,2,1,0:T(8,128)(2,1)S(1)} collective-permute-done((bf16[2,16,32,128]{3,2,1,0:T(8,128)(2,1)S(1)}, bf16[2,16,32,128]{3,2,1,0:T(8,128)(2,1)S(1)}, u32[]{:S(2)}, u32[]{:S(2)}) %collective-permute-start.31) | collective-permute-done | bytes 262176 | tf_op jit(solution)/shard_map/ppermute | solution.py:431
  160.5 9.1 %collective-permute-done.32.refs_6_ = bf16[2,16,32,128]{3,2,1,0:T(8,128)(2,1)S(1)} collective-permute-done((bf16[2,16,32,128]{3,2,1,0:T(8,128)(2,1)S(1)}, bf16[2,16,32,128]{3,2,1,0:T(8,128)(2,1)S(1)}, u32[]{:S(2)}, u32[]{:S(2)}) %collective-permute-start.32) | collective-permute-done | bytes 262176 | tf_op jit(solution)/shard_map/ppermute | solution.py:431
  169.5 5.5 %collective-permute-done.33.refs_7_ = bf16[2,16,32,128]{3,2,1,0:T(8,128)(2,1)S(1)} collective-permute-done((bf16[2,16,32,128]{3,2,1,0:T(8,128)(2,1)S(1)}, bf16[2,16,32,128]{3,2,1,0:T(8,128)(2,1)S(1)}, u32[]{:S(2)}, u32[]{:S(2)}) %collective-permute-start.33) | collective-permute-done | bytes 262176 | tf_op jit(solution)/shard_map/ppermute | solution.py:431
  175.1 2.9 %finish.1 = f32[3072,128]{1,0:T(8,128)} custom-call(s32[5]{0:T(128)S(1)} %stack.23.info_ref, bf16[2,16,32,128]{3,2,1,0:T(8,128)(2,1)S(1)} %collective-permute-done.26.refs_0_, bf16[2,16,32,128]{3,2,1,0:T(8,128)(2,1)S(1)} %collective-permute-done.27.refs_1_, bf16[2,16,32,128]{3,2,1,0:T(8,128)(2,1)S(1)} %collective-permute-done.28.refs_2_, ...), custom_call_target="tpu_custom_call" | custom-call | tf_op jit(solution)/shard_map/finish/pallas_call | solution.py:321
  (46 shorter events, 2.4 us)
Async XLA Ops:
  0.0 6.2 %copy-start = (f32[3,32,16,128]{3,2,1,0:T(8,128)S(1)}, f32[3,32,16,128]{3,2,1,0:T(8,128)}, u32[]{:S(2)}) copy-start(f32[3,32,16,128]{3,2,1,0:T(8,128)} %param.4) | copy-start | bytes 2359300
  1.0 14.1 %collective-permute-start.4 = (bf16[4,32,288]{2,1,0:T(8,128)(2,1)S(1)}, bf16[4,32,288]{2,1,0:T(8,128)(2,1)}, u32[]{:S(2)}, u32[]{:S(2)}) collective-permute-start(bf16[4,32,288]{2,1,0:T(8,128)(2,1)S(1)} %slice.23), channel_id=1, source_target_pairs={{0,8},{1,9},{2,10},{3,11}} | collective-permute-start | bytes 221192 | tf_op jit(solution)/shard_map/ppermute | solution.py:386
  2.3 12.8 %collective-permute-start.3 = (bf16[4,32,288]{2,1,0:T(8,128)(2,1)S(1)}, bf16[4,32,288]{2,1,0:T(8,128)(2,1)}, u32[]{:S(2)}, u32[]{:S(2)}) collective-permute-start(bf16[4,32,288]{2,1,0:T(8,128)(2,1)S(1)} %slice.23), channel_id=1, source_target_pairs={{0,24},{1,25},{2,26},{3,27}} | collective-permute-start | bytes 221192 | tf_op jit(solution)/shard_map/ppermute | solution.py:386
  3.6 11.6 %collective-permute-start.2 = (bf16[4,32,288]{2,1,0:T(8,128)(2,1)S(1)}, bf16[4,32,288]{2,1,0:T(8,128)(2,1)S(1)}, u32[]{:S(2)}, u32[]{:S(2)}) collective-permute-start(bf16[4,32,288]{2,1,0:T(8,128)(2,1)S(1)} %slice.23), channel_id=1, source_target_pairs={{4,0},{8,4},{12,8},{16,12},{20,16},{24,20},{28,24},{32,28},{36,32}... | collective-permute-start | bytes 221192 | tf_op jit(solution)/shard_map/ppermute | solution.py:383
  7.8 7.3 %copy-start.2 = (bf16[8,32,288]{2,1,0:T(8,128)(2,1)S(1)}, bf16[8,32,288]{2,1,0:T(8,128)(2,1)}, u32[]{:S(2)}) copy-start(bf16[8,32,288]{2,1,0:T(8,128)(2,1)} %here_ref.1) | copy-start | bytes 442372
  7.9 14.0 %copy-start.1 = (f32[2,3,32,16,128]{4,3,2,1,0:T(8,128)S(1)}, f32[2,3,32,16,128]{4,3,2,1,0:T(8,128)}, u32[]{:S(2)}) copy-start(f32[2,3,32,16,128]{4,3,2,1,0:T(8,128)} %param.5) | copy-start | bytes 4718596
  8.8 9.1 %collective-permute-start = (bf16[7,4,32,128]{3,2,1,0:T(8,128)(2,1)}, bf16[7,4,32,128]{3,2,1,0:T(8,128)(2,1)S(1)}, u32[]{:S(2)}, u32[]{:S(2)}) collective-permute-start(bf16[7,4,32,128]{3,2,1,0:T(8,128)(2,1)} %maximum_bitcast_fusion), channel_id=1, source_target_pairs={{0,1},{1,2},{2,3},{4,5},{5,6},{6,7},{8,9},{9,10},{10,11},{12,13},{... | collective-permute-start | bytes 688136 | tf_op jit(solution)/shard_map/ppermute | solution.py:381
  13.1 8.8 %collective-permute-start.1 = (bf16[7,4,32,128]{3,2,1,0:T(8,128)(2,1)}, bf16[7,4,32,128]{3,2,1,0:T(8,128)(2,1)S(1)}, u32[]{:S(2)}, u32[]{:S(2)}) collective-permute-start(bf16[7,4,32,128]{3,2,1,0:T(8,128)(2,1)} %maximum_bitcast_fusion.1), channel_id=1, source_target_pairs={{1,0},{2,1},{3,2},{5,4},{6,5},{7,6},{9,8},{10,9},{11,10},{13,12},{... | collective-permute-start | bytes 688136 | tf_op jit(solution)/shard_map/ppermute | solution.py:382
  27.4 2.8 %collective-permute-start.5 = (bf16[38,32,128]{2,1,0:T(8,128)(2,1)S(1)}, bf16[38,32,128]{2,1,0:T(8,128)(2,1)S(1)}, u32[]{:S(2)}, u32[]{:S(2)}) collective-permute-start(bf16[38,32,128]{2,1,0:T(8,128)(2,1)S(1)} %get-tuple-element.31), channel_id=1, source_target_pairs={{0,0},{4,8},{8,24},{32,32},{36,40},{40,56},{64,64},{68,72},{72,88}... | collective-permute-start | bytes 933896 | tf_op jit(solution)/shard_map/ppermute | solution.py:402
  28.1 2.1 %collective-permute-start.6 = (bf16[38,32,128]{2,1,0:T(8,128)(2,1)S(1)}, bf16[38,32,128]{2,1,0:T(8,128)(2,1)S(1)}, u32[]{:S(2)}, u32[]{:S(2)}) collective-permute-start(bf16[38,32,128]{2,1,0:T(8,128)(2,1)S(1)} %get-tuple-element.32), channel_id=1, source_target_pairs={{4,0},{8,8},{12,24},{36,32},{40,40},{44,56},{68,64},{72,72},{76,88... | collective-permute-start | bytes 933896 | tf_op jit(solution)/shard_map/ppermute | solution.py:402
  28.8 1.4 collective-permute-start.7
  29.5 0.7 collective-permute-start.8
  30.5 45.4 %collective-permute-start.13 = (bf16[112,32,128]{2,1,0:T(8,128)(2,1)S(1)}, bf16[112,32,128]{2,1,0:T(8,128)(2,1)S(1)}, u32[]{:S(2)}, u32[]{:S(2)}) collective-permute-start(bf16[112,32,128]{2,1,0:T(8,128)(2,1)S(1)} %get-tuple-element.36), channel_id=1, source_target_pairs={{0,1},{1,2},{2,3},{8,9},{9,10},{10,11},{24,25},{25,26},{26,27},{32... | collective-permute-start | bytes 2752520 | tf_op jit(solution)/shard_map/ppermute | solution.py:413
  31.2 44.6 %collective-permute-start.14 = (bf16[112,32,128]{2,1,0:T(8,128)(2,1)S(1)}, bf16[112,32,128]{2,1,0:T(8,128)(2,1)S(1)}, u32[]{:S(2)}, u32[]{:S(2)}) collective-permute-start(bf16[112,32,128]{2,1,0:T(8,128)(2,1)S(1)} %get-tuple-element.37), channel_id=1, source_target_pairs={{1,0},{2,1},{3,2},{9,8},{10,9},{11,10},{25,24},{26,25},{27,26},{33... | collective-permute-start | bytes 2752520 | tf_op jit(solution)/shard_map/ppermute | solution.py:413
  31.9 27.2 %collective-permute-start.9 = (bf16[38,32,128]{2,1,0:T(8,128)(2,1)S(1)}, bf16[38,32,128]{2,1,0:T(8,128)(2,1)S(1)}, u32[]{:S(2)}, u32[]{:S(2)}) collective-permute-start(bf16[38,32,128]{2,1,0:T(8,128)(2,1)S(1)} %get-tuple-element.31), channel_id=1, source_target_pairs={{16,0},{20,8},{24,24},{48,32},{52,40},{56,56},{80,64},{84,72},{88,... | collective-permute-start | bytes 933896 | tf_op jit(solution)/shard_map/ppermute | solution.py:402
  32.6 37.7 %collective-permute-start.10 = (bf16[38,32,128]{2,1,0:T(8,128)(2,1)S(1)}, bf16[38,32,128]{2,1,0:T(8,128)(2,1)S(1)}, u32[]{:S(2)}, u32[]{:S(2)}) collective-permute-start(bf16[38,32,128]{2,1,0:T(8,128)(2,1)S(1)} %get-tuple-element.32), channel_id=1, source_target_pairs={{20,0},{24,8},{28,24},{52,32},{56,40},{60,56},{84,64},{88,72},{92,... | collective-permute-start | bytes 933896 | tf_op jit(solution)/shard_map/ppermute | solution.py:402
  57.8 12.5 %collective-permute-start.11 = (bf16[38,32,128]{2,1,0:T(8,128)(2,1)S(1)}, bf16[38,32,128]{2,1,0:T(8,128)(2,1)S(1)}, u32[]{:S(2)}, u32[]{:S(2)}) collective-permute-start(bf16[38,32,128]{2,1,0:T(8,128)(2,1)S(1)} %get-tuple-element.33), channel_id=1, source_target_pairs={{24,0},{28,8},{16,24},{56,32},{60,40},{48,56},{88,64},{92,72},{80,... | collective-permute-start | bytes 933896 | tf_op jit(solution)/shard_map/ppermute | solution.py:402
  59.1 15.0 %collective-permute-start.12 = (bf16[38,32,128]{2,1,0:T(8,128)(2,1)S(1)}, bf16[38,32,128]{2,1,0:T(8,128)(2,1)S(1)}, u32[]{:S(2)}, u32[]{:S(2)}) collective-permute-start(bf16[38,32,128]{2,1,0:T(8,128)(2,1)S(1)} %get-tuple-element.34), channel_id=1, source_target_pairs={{28,0},{16,8},{20,24},{60,32},{48,40},{52,56},{92,64},{80,72},{84,... | collective-permute-start | bytes 933896 | tf_op jit(solution)/shard_map/ppermute | solution.py:402
  74.2 1.6 collective-permute-start.15
  74.9 0.9 collective-permute-start.16
  81.6 2.1 %collective-permute-start.17 = (f32[16,32,128]{2,1,0:T(8,128)S(1)}, f32[16,32,128]{2,1,0:T(8,128)S(1)}, u32[]{:S(2)}, u32[]{:S(2)}) collective-permute-start(f32[16,32,128]{2,1,0:T(8,128)S(1)} %get-tuple-element.41), channel_id=1, source_target_pairs={{0,32},{1,33},{2,34},{3,35},{8,40},{9,41},{10,42},{11,43},{24,56},... | collective-permute-start | bytes 786440 | tf_op jit(solution)/shard_map/ppermute | solution.py:413
  82.3 1.4 collective-permute-start.19
  83.0 0.7 collective-permute-start.18
  89.8 2.1 %collective-permute-start.20 = (f32[16,32,128]{2,1,0:T(8,128)S(1)}, f32[16,32,128]{2,1,0:T(8,128)S(1)}, u32[]{:S(2)}, u32[]{:S(2)}) collective-permute-start(f32[16,32,128]{2,1,0:T(8,128)S(1)} %get-tuple-element.43), channel_id=1, source_target_pairs={{0,32},{1,33},{2,34},{3,35},{8,40},{9,41},{10,42},{11,43},{24,56},... | collective-permute-start | bytes 786440 | tf_op jit(solution)/shard_map/ppermute | solution.py:413
  90.4 1.4 collective-permute-start.22
  91.1 0.7 collective-permute-start.21
  97.7 2.1 %collective-permute-start.23 = (f32[16,32,128]{2,1,0:T(8,128)S(1)}, f32[16,32,128]{2,1,0:T(8,128)S(1)}, u32[]{:S(2)}, u32[]{:S(2)}) collective-permute-start(f32[16,32,128]{2,1,0:T(8,128)S(1)} %get-tuple-element.45), channel_id=1, source_target_pairs={{0,32},{1,33},{2,34},{3,35},{8,40},{9,41},{10,42},{11,43},{24,56},... | collective-permute-start | bytes 786440 | tf_op jit(solution)/shard_map/ppermute | solution.py:413
  98.4 1.4 collective-permute-start.25
  99.1 0.7 collective-permute-start.24
  106.1 3.4 %collective-permute-start.26 = (bf16[2,16,32,128]{3,2,1,0:T(8,128)(2,1)S(1)}, bf16[2,16,32,128]{3,2,1,0:T(8,128)(2,1)S(1)}, u32[]{:S(2)}, u32[]{:S(2)}) collective-permute-start(bf16[2,16,32,128]{3,2,1,0:T(8,128)(2,1)S(1)} %get-tuple-element.47), channel_id=1, source_target_pairs={{0,0},{8,4},{24,8},{32,32},{40,36},{56,40},{64,64},{72,68},{88,72}... | collective-permute-start | bytes 786440 | tf_op jit(solution)/shard_map/ppermute | solution.py:431
  106.7 4.1 %collective-permute-start.27 = (bf16[2,16,32,128]{3,2,1,0:T(8,128)(2,1)S(1)}, bf16[2,16,32,128]{3,2,1,0:T(8,128)(2,1)S(1)}, u32[]{:S(2)}, u32[]{:S(2)}) collective-permute-start(bf16[2,16,32,128]{3,2,1,0:T(8,128)(2,1)S(1)} %get-tuple-element.48), channel_id=1, source_target_pairs={{0,4},{8,8},{24,12},{32,36},{40,40},{56,44},{64,68},{72,72},{88,76... | collective-permute-start | bytes 786440 | tf_op jit(solution)/shard_map/ppermute | solution.py:431
  107.4 4.7 %collective-permute-start.28 = (bf16[2,16,32,128]{3,2,1,0:T(8,128)(2,1)S(1)}, bf16[2,16,32,128]{3,2,1,0:T(8,128)(2,1)S(1)}, u32[]{:S(2)}, u32[]{:S(2)}) collective-permute-start(bf16[2,16,32,128]{3,2,1,0:T(8,128)(2,1)S(1)} %get-tuple-element.49), channel_id=1, source_target_pairs={{0,8},{8,12},{24,0},{32,40},{40,44},{56,32},{64,72},{72,76},{88,64... | collective-permute-start | bytes 786440 | tf_op jit(solution)/shard_map/ppermute | solution.py:431
  108.1 5.3 %collective-permute-start.29 = (bf16[2,16,32,128]{3,2,1,0:T(8,128)(2,1)S(1)}, bf16[2,16,32,128]{3,2,1,0:T(8,128)(2,1)S(1)}, u32[]{:S(2)}, u32[]{:S(2)}) collective-permute-start(bf16[2,16,32,128]{3,2,1,0:T(8,128)(2,1)S(1)} %get-tuple-element.50), channel_id=1, source_target_pairs={{0,12},{8,0},{24,4},{32,44},{40,32},{56,36},{64,76},{72,64},{88,68... | collective-permute-start | bytes 786440 | tf_op jit(solution)/shard_map/ppermute | solution.py:431
  108.8 4.6 %collective-permute-start.30 = (bf16[2,16,32,128]{3,2,1,0:T(8,128)(2,1)S(1)}, bf16[2,16,32,128]{3,2,1,0:T(8,128)(2,1)S(1)}, u32[]{:S(2)}, u32[]{:S(2)}) collective-permute-start(bf16[2,16,32,128]{3,2,1,0:T(8,128)(2,1)S(1)} %get-tuple-element.51), channel_id=1, source_target_pairs={{0,16},{8,20},{24,24},{32,48},{40,52},{56,56},{64,80},{72,84},{88,... | collective-permute-start | bytes 786440 | tf_op jit(solution)/shard_map/ppermute | solution.py:431
  109.5 51.0 %collective-permute-start.31 = (bf16[2,16,32,128]{3,2,1,0:T(8,128)(2,1)S(1)}, bf16[2,16,32,128]{3,2,1,0:T(8,128)(2,1)S(1)}, u32[]{:S(2)}, u32[]{:S(2)}) collective-permute-start(bf16[2,16,32,128]{3,2,1,0:T(8,128)(2,1)S(1)} %get-tuple-element.52), channel_id=1, source_target_pairs={{0,20},{8,24},{24,28},{32,52},{40,56},{56,60},{64,84},{72,88},{88,... | collective-permute-start | bytes 786440 | tf_op jit(solution)/shard_map/ppermute | solution.py:431
  110.8 58.7 %collective-permute-start.32 = (bf16[2,16,32,128]{3,2,1,0:T(8,128)(2,1)S(1)}, bf16[2,16,32,128]{3,2,1,0:T(8,128)(2,1)S(1)}, u32[]{:S(2)}, u32[]{:S(2)}) collective-permute-start(bf16[2,16,32,128]{3,2,1,0:T(8,128)(2,1)S(1)} %get-tuple-element.53), channel_id=1, source_target_pairs={{0,24},{8,28},{24,16},{32,56},{40,60},{56,48},{64,88},{72,92},{88,... | collective-permute-start | bytes 786440 | tf_op jit(solution)/shard_map/ppermute | solution.py:431
  112.1 62.9 %collective-permute-start.33 = (bf16[2,16,32,128]{3,2,1,0:T(8,128)(2,1)S(1)}, bf16[2,16,32,128]{3,2,1,0:T(8,128)(2,1)S(1)}, u32[]{:S(2)}, u32[]{:S(2)}) collective-permute-start(bf16[2,16,32,128]{3,2,1,0:T(8,128)(2,1)S(1)} %get-tuple-element.54), channel_id=1, source_target_pairs={{0,28},{8,16},{24,20},{32,60},{40,48},{56,52},{64,92},{72,80},{88,... | collective-permute-start | bytes 786440 | tf_op jit(solution)/shard_map/ppermute | solution.py:431

commit v3 on v1

--- a/solution.py
+++ b/solution.py
@@ -123,27 +123,31 @@
         copy.wait()
 
 
-def relax_kernel(k, info_ref, own_ref, up_ref, dn_ref, here_ref, next_ref, out_ref, xs, state, base):
-    b = lax.rem(info_ref[1] - k + FLOW, FLOW)
+def relax_kernel(info_ref, own_ref, up_ref, dn_ref, here_ref, next_ref, *refs):
+    outs, (xs, state, base, slots, sems) = refs[:FLOW], refs[FLOW:]
     load, layer = relaxer(info_ref, xs, state)
+    clear_rims(xs, SPAN)
 
     def tap(point, j):
         return tiles(next_ref, j) if point else tiles(here_ref, M + j)
 
-    @pl.when(b < IMAGES)
-    def _():
-        clear_rims(xs, SPAN)
+    def image(b, carry):
         for point in range(2):
             u = point * IMAGES + b
             load(point, u, up_ref, own_ref, dn_ref, u * (C * BAND))
         for j in range(M):
             for point in range(2):
                 layer(point, j, banded(tap(point, j)), base)
+        slot = lax.rem(info_ref[1] - b + FLOW, FLOW)
         for point in range(2):
             change = state[point, REACH : REACH + BAND] - base[point]
-            out_ref[point * BAND : (point + 1) * BAND] = change.astype(bf16)
+            slots[slot, point * BAND : (point + 1) * BAND] = change.astype(bf16)
             for t, tile in enumerate(tap(point, 0)):
-                out_ref[2 * BAND + 3 * point + t] = tile
+                slots[slot, 2 * BAND + 3 * point + t] = tile
+        return carry
+
+    lax.fori_loop(0, IMAGES, image, 0)
+    drain(slots, outs, sems)
 
 
 def opening_kernel(info_ref, img_ref, up_ref, dn_ref, open_ref, v1_ref, xs, state):
@@ -210,16 +214,15 @@
 
 
 def sweep_kernel(
-    opening, closing, info_ref, v1_ref, d_ref, up0_ref, dn0_ref, up1_ref, dn1_ref, w_ref, *refs
+    stage, closing, info_ref, v1_ref, d_ref, up0_ref, dn0_ref, up1_ref, dn1_ref, w_ref, *refs
 ):
-    if not opening:
-        (own_ref, above_ref, below_ref), refs = refs[:3], refs[3:]
+    inputs = 3 * (stage if closing else min(stage, 1))
+    handed, refs = refs[:inputs], refs[inputs:]
     if closing:
         outs, (xs, state, res_ref, sems) = refs[:SUB], refs[SUB:]
     else:
         out_ref, edge_ref, xs, state = refs
-    z, first, b = info_ref[0], info_ref[2], info_ref[3]
-    clear_rims(xs, WIN)
+    z, b, group = info_ref[0], info_ref[3], info_ref[5]
     low_ok = jnp.where(z > 0, 1.0, 0.0)
     high_ok = jnp.where(z < 3, 1.0, 0.0)
 
@@ -235,52 +238,63 @@
         state[BAND : 2 * BAND] = v1_ref[...]
         state[2 * BAND :] = dn0_ref[LEAD:].astype(f32)
 
-    def resume():
+    def resume(own_ref, above_ref, below_ref):
         state[:BAND] = above_ref[...].astype(f32)
         state[BAND : 2 * BAND] = own_ref[...]
         state[2 * BAND :] = below_ref[...].astype(f32)
 
-    if opening:
-        begin()
+    def run():
+        clear_rims(xs, WIN)
+        if closing:
+            pl.when(group == 0)(begin)
+            for g in range(stage):
+                pl.when(group == g + 1)(functools.partial(resume, *handed[3 * g : 3 * g + 3]))
+        elif stage == 0:
+            begin()
+        else:
+            resume(*handed)
+
+        for row in range(0, WIN, 2):
+            put(0, row, state[row : row + 2].reshape(2 * C, W))
+
+        for s, rows in enumerate(EDGE):
+            now = s % 2
+            half = s // SUB
+            if closing:
+                res_ref[FLOW * half + lax.rem(s // 2 % FLOW - b + FLOW, FLOW), now] = xs[now, BAND + 1 : 2 * BAND + 1, 1]
+                if s == STEPS - 1:
+                    break
+            matrix = banded([w_ref[s, t] for t in range(3)])
+            up_ref, dn_ref = (up1_ref, dn1_ref) if half else (up0_ref, dn0_ref)
+            for row in range(BAND - rows, 2 * BAND + rows, 4):
+                for k, t in enumerate(block(xs, now, matrix, row)):
+                    r = row + 2 * k
+                    if r < BAND:
+                        at = OFFSET[s] - half * LEAD + r - (BAND - rows)
+                        d = up_ref[at : at + 2]
+                    elif r < 2 * BAND:
+                        d = d_ref[s, r - BAND : r - BAND + 2]
+                    else:
+                        at = OFFSET[s] - half * LEAD + r - 2 * BAND
+                        d = dn_ref[at : at + 2]
+                    x = state[r : r + 2].reshape(2 * C, W) + ((M * H) * t + d.astype(f32).reshape(2 * C, W))
+                    state[r : r + 2] = x.reshape(2, C, W)
+                    if s < STEPS - 1:
+                        put(1 - now, r, x)
+        if closing:
+            drain(res_ref, outs, sems)
+        else:
+            out_ref[...] = state[BAND : 2 * BAND]
+            edge_ref[...] = state[BAND : 2 * BAND].astype(bf16)
+
+    if closing:
+        run()
     else:
-        pl.when(first == 1)(begin)
-        pl.when(first == 0)(resume)
-
-    for row in range(0, WIN, 2):
-        put(0, row, state[row : row + 2].reshape(2 * C, W))
-
-    for s, rows in enumerate(EDGE):
-        now = s % 2
-        half = s // SUB
-        if closing:
-            res_ref[FLOW * half + lax.rem(s // 2 % FLOW - b + FLOW, FLOW), now] = xs[now, BAND + 1 : 2 * BAND + 1, 1]
-            if s == STEPS - 1:
-                break
-        matrix = banded([w_ref[s, t] for t in range(3)])
-        up_ref, dn_ref = (up1_ref, dn1_ref) if half else (up0_ref, dn0_ref)
-        for row in range(BAND - rows, 2 * BAND + rows, 4):
-            for k, t in enumerate(block(xs, now, matrix, row)):
-                r = row + 2 * k
-                if r < BAND:
-                    at = OFFSET[s] - half * LEAD + r - (BAND - rows)
-                    d = up_ref[at : at + 2]
-                elif r < 2 * BAND:
-                    d = d_ref[s, r - BAND : r - BAND + 2]
-                else:
-                    at = OFFSET[s] - half * LEAD + r - 2 * BAND
-                    d = dn_ref[at : at + 2]
-                x = state[r : r + 2].reshape(2 * C, W) + ((M * H) * t + d.astype(f32).reshape(2 * C, W))
-                state[r : r + 2] = x.reshape(2, C, W)
-                if s < STEPS - 1:
-                    put(1 - now, r, x)
-    if closing:
-        drain(res_ref, outs, sems)
-    else:
-        out_ref[...] = state[BAND : 2 * BAND]
-        edge_ref[...] = state[BAND : 2 * BAND].astype(bf16)
+        pl.when(group == stage)(run)
 
 
 VM = pl.BlockSpec(memory_space=pltpu.VMEM)
+GRANT = pltpu.CompilerParams(vmem_limit_bytes=18 * 1024 * 1024)
 SM = pl.BlockSpec(memory_space=pltpu.SMEM)
 AN = pl.BlockSpec(memory_space=pl.ANY)
 
@@ -289,17 +303,21 @@
     return jax.ShapeDtypeStruct(dims, dtype)
 
 
-def relax(k, info, *arrays):
-    return pl.pallas_call(
-        functools.partial(relax_kernel, k),
-        out_shape=shape(CHUNK, C, W),
+def relax(info, *arrays):
+    return pl.pallas_call(
+        relax_kernel,
+        out_shape=(shape(CHUNK, C, W),) * FLOW,
         in_specs=[SM] + [VM] * len(arrays),
-        out_specs=VM,
+        out_specs=(AN,) * FLOW,
         scratch_shapes=[
             pltpu.VMEM((4, SPAN + 2, 3, C, W), bf16),
             pltpu.VMEM((2, SPAN, C, W), f32),
             pltpu.VMEM((2, BAND, C, W), f32),
+            pltpu.VMEM((FLOW, CHUNK, C, W), bf16),
+            pltpu.SemaphoreType.DMA((FLOW,)),
         ],
+        compiler_params=GRANT,
+        name="relax",
     )(info, *arrays)
 
 
@@ -313,6 +331,7 @@
             pltpu.VMEM((2, SPAN + 2, 3, C, W), bf16),
             pltpu.VMEM((1, SPAN, C, W), f32),
         ],
+        compiler_params=GRANT,
         name="opening",
     )(info, *arrays)
 
@@ -325,6 +344,7 @@
         in_specs=[SM] + [VM] * len(arrays),
         out_specs=(VM, VM),
         scratch_shapes=[pltpu.VMEM((SUB, BAND, C, W), bf16)],
+        compiler_params=GRANT,
     )(b, *arrays)
 
 
@@ -339,6 +359,7 @@
             pltpu.VMEM((IMAGES, 2, BAND * C, W), f32),
             pltpu.SemaphoreType.DMA((IMAGES,)),
         ],
+        compiler_params=GRANT,
         name="finish",
     )(info, *arrays)
 
@@ -350,11 +371,12 @@
         in_specs=[SM] + [VM] * SUB,
         out_specs=(VM, VM),
         cost_estimate=pl.CostEstimate(flops=0, bytes_accessed=5_000_000, transcendentals=0),
+        compiler_params=GRANT,
         name="order",
     )(sub, *chunks)
 
 
-def sweep(opening, closing, info, *arrays):
+def sweep(stage, closing, info, *arrays):
     if closing:
         out_shape = (shape(2, BAND, C, W),) * SUB
         extra = [pltpu.VMEM((SUB, 2, BAND, C, W), bf16), pltpu.SemaphoreType.DMA((SUB,))]
@@ -362,11 +384,12 @@
         out_shape = (shape(BAND, C, W, dtype=f32), shape(BAND, C, W))
         extra = []
     return pl.pallas_call(
-        functools.partial(sweep_kernel, opening, closing),
+        functools.partial(sweep_kernel, stage, closing),
         out_shape=out_shape,
         in_specs=[SM] + [VM] * len(arrays),
         out_specs=(AN,) * SUB if closing else (VM, VM),
         scratch_shapes=[pltpu.VMEM((2, WIN + 2, 3, C, W), bf16), pltpu.VMEM((WIN, C, W), f32)] + extra,
+        compiler_params=GRANT,
         name="sweep",
     )(info, *arrays)
 
@@ -395,7 +418,8 @@
         opening = jnp.where(l == home(b), got, opening)
 
     lead = jnp.where(group == 0, 1, 0)
-    info = jnp.stack([z, lax.rem(sub, FLOW), lead, mine, sub // FLOW]).astype(jnp.int32)
+    info = jnp.stack([z, lax.rem(sub, FLOW), lead, mine, sub // FLOW, group]).astype(jnp.int32)
+    sends = relax(info, guess.reshape(-1, W), up, dn, weights, following)
 
     def pairs(half, k):
         return [
@@ -404,16 +428,15 @@
             for b in range(IMAGES)
         ]
 
-    received = [[], []]
-    for k in range(FLOW):
-        chunk = relax(k, info, guess.reshape(-1, W), up, dn, weights, following)
-        for h in range(HALVES):
-            received[h].append(lax.ppermute(chunk, "layer", pairs(h, k)))
+    received = [
+        [lax.ppermute(sends[k], "layer", pairs(h, k)) for k in range(FLOW)] for h in range(HALVES)
+    ]
+
     v1 = opened(info, own_image.reshape(-1, W), up, dn, opening)
 
-    def among_sweepers(value, ahead, by):
+    def among_sweepers(value, ahead, by, live):
         pairs = []
-        for g in range(groups - ahead):
+        for g in live:
             for b in range(IMAGES):
                 for k in range(rows):
                     if 0 <= k + by < rows:
@@ -424,16 +447,17 @@
 
     images = mine.astype(jnp.int32).reshape(1)
     up, dn = rims(0, images, *received[0], v1)
-    up0, dn0 = among_sweepers(up, 0, 1), among_sweepers(dn, 0, -1)
+    up0, dn0 = among_sweepers(up, 0, 1, range(groups)), among_sweepers(dn, 0, -1, range(groups))
     up, dn = rims(1, images, *received[1])
-    up1, dn1 = among_sweepers(up, 0, 1), among_sweepers(dn, 0, -1)
+    up1, dn1 = among_sweepers(up, 0, 1, range(groups)), among_sweepers(dn, 0, -1, range(groups))
     d, w = order(images, received[0] + received[1])
 
-    handed = ()
+    handed = []
     for stage in range(groups - 1):
-        state, edge = sweep(stage == 0, False, info, v1, d, up0, dn0, up1, dn1, w, *handed)
-        handed = among_sweepers(state, 1, 0), among_sweepers(edge, 1, 1), among_sweepers(edge, 1, -1)
-    results = sweep(False, True, info, v1, d, up0, dn0, up1, dn1, w, *handed)
+        state, edge = sweep(stage, False, info, v1, d, up0, dn0, up1, dn1, w, *handed[-3:])
+        for value, by in ((state, 0), (edge, 1), (edge, -1)):
+            handed.append(among_sweepers(value, 1, by, [stage]))
+    results = sweep(groups - 1, True, info, v1, d, up0, dn0, up1, dn1, w, *handed)
 
     back = []
     for h in range(HALVES):

time: 207 us -> 166 us (0.80)
  the two profiles are of different devices: /device:TPU:59 before, /device:TPU:31 now
where the time goes in v3:
time: 166 us; the launch traced here: 165 us
  waiting for transfers between devices  76.1 us (46%)
  starting transfers between devices  65.4 us (39%)
  Pallas kernels  18.3 us (11%)
  other arithmetic  2.96 us (2%)
    ppermute x8, waiting for transfers between devices, cycle(): lax.ppermute(results[FLOW * h + k], 'layer', [(t, s) for s, t in pairs(h,...  68.9 us
    ppermute x8, starting transfers between devices, cycle(): lax.ppermute(sends[k], 'layer', pairs(h, k))  39.6 us
    ppermute x13, starting transfers between devices, among_sweepers(): return lax.ppermute(value, ('layer', 'rows'), pairs)  8.84 us
    pallas_call x4, Pallas kernels, sweep(): pl.pallas_call(functools.partial(sweep_kernel, stage, closing), out_shape...  8.13 us
    ppermute x8, starting transfers between devices, cycle(): lax.ppermute(results[FLOW * h + k], 'layer', [(t, s) for s, t in pairs(h,...  7.26 us
    pallas_call x1, Pallas kernels, relax(): pl.pallas_call(relax_kernel, out_shape=(shape(CHUNK, C, W),) * FLOW, in_s...  6.19 us
    ppermute x8, waiting for transfers between devices, cycle(): lax.ppermute(sends[k], 'layer', pairs(h, k))  4.12 us
    ppermute x1, starting transfers between devices, cycle(): lax.ppermute(edge_rows(BAND - REACH), 'rows', [(i, i + 1) for i in range(...  3.54 us
  transfers between devices with their start and end apart: 34, of which 5 were waited for; matrix products, arithmetic and copies ran while one was open for 0% of the time, Pallas kernels for 4%

profile of v3, /device:TPU:31, one launch (start us, length us, event | category | flops | bytes accessed | tf_op | source)
XLA Modules:
  0.0 165.2 jit_solution(4583464048293235063)
XLA Ops:
  0.0 1.1 copy-done
  1.3 1.5 convert.16
  3.1 0.7 maximum_bitcast_fusion
  3.8 3.5 %collective-permute-start = (bf16[7,4,32,128]{3,2,1,0:T(8,128)(2,1)}, bf16[7,4,32,128]{3,2,1,0:T(8,128)(2,1)S(1)}, u32[]{:S(2)}, u32[]{:S(2)}) collective-permute-start(bf16[7,4,32,128]{3,2,1,0:T(8,128)(2,1)} %maximum_bitcast_fusion), channel_id=1, source_target_pairs={{0,1},{1,2},{2,3},{4,5},{5,6},{6,7},{8,9},{9,10},{10,11},{12,13},{... | collective-permute-start | bytes 688136 | tf_op jit(solution)/shard_map/ppermute | solution.py:412
  7.3 0.7 maximum_bitcast_fusion.1
  8.0 1.3 collective-permute-start.1
  9.3 2.9 %collective-permute-start.4 = (bf16[4,32,288]{2,1,0:T(8,128)(2,1)S(1)}, bf16[4,32,288]{2,1,0:T(8,128)(2,1)S(1)}, u32[]{:S(2)}, u32[]{:S(2)}) collective-permute-start(bf16[4,32,288]{2,1,0:T(8,128)(2,1)S(1)} %slice.23), channel_id=1, source_target_pairs={{4,0},{8,4},{12,8},{16,12},{20,16},{24,20},{28,24},{32,28},{36,32}... | collective-permute-start | bytes 221192 | tf_op jit(solution)/shard_map/ppermute | solution.py:414
  12.2 1.3 collective-permute-start.3
  13.6 3.1 %collective-permute-done.1.dn_ref = bf16[7,4,32,128]{3,2,1,0:T(8,128)(2,1)S(1)} collective-permute-done((bf16[7,4,32,128]{3,2,1,0:T(8,128)(2,1)}, bf16[7,4,32,128]{3,2,1,0:T(8,128)(2,1)S(1)}, u32[]{:S(2)}, u32[]{:S(2)}) %collective-permute-start.1) | collective-permute-done | bytes 229408 | tf_op jit(solution)/shard_map/ppermute | solution.py:413
  16.7 6.2 %relax.1 = (bf16[38,32,128]{2,1,0:T(8,128)(2,1)}, bf16[38,32,128]{2,1,0:T(8,128)(2,1)}, bf16[38,32,128]{2,1,0:T(8,128)(2,1)}, bf16[38,32,128]{2,1,0:T(8,128)(2,1)}) custom-call(s32[6]{0:T(128)S(1)} %stack.27.info_ref, f32[3072,128]{1,0:T(8,128)S(1)} %bitcast.21, bf16[7,4,32,128]{3,2,1,0:T(8,128)(2,1)S(1)} %collective-permute-done.up_ref, ...), custom_call_target="tpu_custom_call" | custom-call | tf_op jit(solution)/shard_map/relax/pallas_call | solution.py:307
  22.9 0.7 collective-permute-start.5
  23.6 0.7 collective-permute-start.6
  24.3 0.7 collective-permute-start.7
  24.9 0.7 collective-permute-start.8
  25.6 0.7 collective-permute-start.2
  27.2 0.7 collective-permute-start.13
  28.0 0.7 collective-permute-start.14
  28.7 0.7 collective-permute-start.9
  29.4 24.5 %collective-permute-start.10 = (bf16[38,32,128]{2,1,0:T(8,128)(2,1)}, bf16[38,32,128]{2,1,0:T(8,128)(2,1)S(1)}, u32[]{:S(2)}, u32[]{:S(2)}) collective-permute-start(bf16[38,32,128]{2,1,0:T(8,128)(2,1)} %get-tuple-element.30), channel_id=1, source_target_pairs={{20,0},{24,8},{28,24},{52,32},{56,40},{60,56},{84,64},{88,72},{92,... | collective-permute-start | bytes 933896 | tf_op jit(solution)/shard_map/ppermute | solution.py:432
  53.8 1.3 collective-permute-start.11
  55.2 10.5 %collective-permute-start.12 = (bf16[38,32,128]{2,1,0:T(8,128)(2,1)}, bf16[38,32,128]{2,1,0:T(8,128)(2,1)S(1)}, u32[]{:S(2)}, u32[]{:S(2)}) collective-permute-start(bf16[38,32,128]{2,1,0:T(8,128)(2,1)} %get-tuple-element.32), channel_id=1, source_target_pairs={{28,0},{16,8},{20,24},{60,32},{48,40},{52,56},{92,64},{80,72},{84,... | collective-permute-start | bytes 933896 | tf_op jit(solution)/shard_map/ppermute | solution.py:432
  65.7 4.1 %collective-permute-done.12.refs_7_.refs_3_ = bf16[38,32,128]{2,1,0:T(8,128)(2,1)S(1)} collective-permute-done((bf16[38,32,128]{2,1,0:T(8,128)(2,1)}, bf16[38,32,128]{2,1,0:T(8,128)(2,1)S(1)}, u32[]{:S(2)}, u32[]{:S(2)}) %collective-permute-start.12) | collective-permute-done | bytes 311328 | tf_op jit(solution)/shard_map/ppermute | solution.py:432
  69.9 0.7 collective-permute-start.15
  70.6 0.7 collective-permute-start.16
  72.0 0.7 collective-permute-start.17
  72.7 0.7 collective-permute-start.19
  73.4 0.7 collective-permute-start.18
  74.1 0.7 sweep.5
  74.8 0.7 collective-permute-start.20
  75.5 0.7 collective-permute-start.22
  76.2 0.7 collective-permute-start.21
  76.9 0.6 sweep.6
  77.5 0.7 collective-permute-start.23
  78.2 0.7 collective-permute-start.25
  78.8 0.7 collective-permute-start.24
  79.5 6.3 %sweep.7 = (bf16[2,16,32,128]{3,2,1,0:T(8,128)(2,1)S(1)}, bf16[2,16,32,128]{3,2,1,0:T(8,128)(2,1)S(1)}, bf16[2,16,32,128]{3,2,1,0:T(8,128)(2,1)S(1)}, bf16[2,16,...) custom-call(s32[6]{0:T(128)S(1)} %stack.27.info_ref, ...), custom_call_target="tpu_custom_call" | custom-call | tf_op jit(solution)/shard_map/sweep/pallas_call | solution.py:386
  85.8 0.7 collective-permute-start.26
  86.5 0.7 collective-permute-start.27
  87.2 0.7 collective-permute-start.28
  87.9 0.7 collective-permute-start.29
  88.6 0.7 collective-permute-start.30
  89.3 1.3 collective-permute-start.31
  90.6 1.3 collective-permute-start.32
  91.9 1.3 collective-permute-start.33
  93.2 54.3 %collective-permute-done.31.refs_5_ = bf16[2,16,32,128]{3,2,1,0:T(8,128)(2,1)S(1)} collective-permute-done((bf16[2,16,32,128]{3,2,1,0:T(8,128)(2,1)S(1)}, bf16[2,16,32,128]{3,2,1,0:T(8,128)(2,1)S(1)}, u32[]{:S(2)}, u32[]{:S(2)}) %collective-permute-start.31) | collective-permute-done | bytes 262176 | tf_op jit(solution)/shard_map/ppermute | solution.py:465
  147.5 9.1 %collective-permute-done.32.refs_6_ = bf16[2,16,32,128]{3,2,1,0:T(8,128)(2,1)S(1)} collective-permute-done((bf16[2,16,32,128]{3,2,1,0:T(8,128)(2,1)S(1)}, bf16[2,16,32,128]{3,2,1,0:T(8,128)(2,1)S(1)}, u32[]{:S(2)}, u32[]{:S(2)}) %collective-permute-start.32) | collective-permute-done | bytes 262176 | tf_op jit(solution)/shard_map/ppermute | solution.py:465
  156.6 5.5 %collective-permute-done.33.refs_7_ = bf16[2,16,32,128]{3,2,1,0:T(8,128)(2,1)S(1)} collective-permute-done((bf16[2,16,32,128]{3,2,1,0:T(8,128)(2,1)S(1)}, bf16[2,16,32,128]{3,2,1,0:T(8,128)(2,1)S(1)}, u32[]{:S(2)}, u32[]{:S(2)}) %collective-permute-start.33) | collective-permute-done | bytes 262176 | tf_op jit(solution)/shard_map/ppermute | solution.py:465
  162.1 2.9 %finish.1 = f32[3072,128]{1,0:T(8,128)} custom-call(s32[6]{0:T(128)S(1)} %stack.27.info_ref, bf16[2,16,32,128]{3,2,1,0:T(8,128)(2,1)S(1)} %collective-permute-done.26.refs_0_, bf16[2,16,32,128]{3,2,1,0:T(8,128)(2,1)S(1)} %collective-permute-done.27.refs_1_, bf16[2,16,32,128]{3,2,1,0:T(8,128)(2,1)S(1)} %collective-permute-done.28.refs_2_, ...), custom_call_target="tpu_custom_call" | custom-call | tf_op jit(solution)/shard_map/finish/pallas_call | solution.py:352
  (47 shorter events, 2.2 us)
Async XLA Ops:
  0.0 1.1 copy-start
  2.8 6.5 %copy-start.2 = (bf16[8,32,288]{2,1,0:T(8,128)(2,1)S(1)}, bf16[8,32,288]{2,1,0:T(8,128)(2,1)}, u32[]{:S(2)}) copy-start(bf16[8,32,288]{2,1,0:T(8,128)(2,1)} %here_ref.1) | copy-start | bytes 442372
  2.8 13.9 %copy-start.1 = (f32[2,3,32,16,128]{4,3,2,1,0:T(8,128)S(1)}, f32[2,3,32,16,128]{4,3,2,1,0:T(8,128)}, u32[]{:S(2)}) copy-start(f32[2,3,32,16,128]{4,3,2,1,0:T(8,128)} %param.5) | copy-start | bytes 4718596
  3.8 9.8 %collective-permute-start = (bf16[7,4,32,128]{3,2,1,0:T(8,128)(2,1)}, bf16[7,4,32,128]{3,2,1,0:T(8,128)(2,1)S(1)}, u32[]{:S(2)}, u32[]{:S(2)}) collective-permute-start(bf16[7,4,32,128]{3,2,1,0:T(8,128)(2,1)} %maximum_bitcast_fusion), channel_id=1, source_target_pairs={{0,1},{1,2},{2,3},{4,5},{5,6},{6,7},{8,9},{9,10},{10,11},{12,13},{... | collective-permute-start | bytes 688136 | tf_op jit(solution)/shard_map/ppermute | solution.py:412
  8.0 8.6 %collective-permute-start.1 = (bf16[7,4,32,128]{3,2,1,0:T(8,128)(2,1)}, bf16[7,4,32,128]{3,2,1,0:T(8,128)(2,1)S(1)}, u32[]{:S(2)}, u32[]{:S(2)}) collective-permute-start(bf16[7,4,32,128]{3,2,1,0:T(8,128)(2,1)} %maximum_bitcast_fusion.1), channel_id=1, source_target_pairs={{1,0},{2,1},{3,2},{5,4},{6,5},{7,6},{9,8},{10,9},{11,10},{13,12},{... | collective-permute-start | bytes 688136 | tf_op jit(solution)/shard_map/ppermute | solution.py:413
  9.3 4.3 %collective-permute-start.4 = (bf16[4,32,288]{2,1,0:T(8,128)(2,1)S(1)}, bf16[4,32,288]{2,1,0:T(8,128)(2,1)S(1)}, u32[]{:S(2)}, u32[]{:S(2)}) collective-permute-start(bf16[4,32,288]{2,1,0:T(8,128)(2,1)S(1)} %slice.23), channel_id=1, source_target_pairs={{4,0},{8,4},{12,8},{16,12},{20,16},{24,20},{28,24},{32,28},{36,32}... | collective-permute-start | bytes 221192 | tf_op jit(solution)/shard_map/ppermute | solution.py:414
  12.2 13.4 %collective-permute-start.3 = (bf16[4,32,288]{2,1,0:T(8,128)(2,1)S(1)}, bf16[4,32,288]{2,1,0:T(8,128)(2,1)}, u32[]{:S(2)}, u32[]{:S(2)}) collective-permute-start(bf16[4,32,288]{2,1,0:T(8,128)(2,1)S(1)} %slice.23), channel_id=1, source_target_pairs={{0,8},{1,9},{2,10},{3,11}} | collective-permute-start | bytes 221192 | tf_op jit(solution)/shard_map/ppermute | solution.py:417
  22.9 4.1 %collective-permute-start.5 = (bf16[38,32,128]{2,1,0:T(8,128)(2,1)}, bf16[38,32,128]{2,1,0:T(8,128)(2,1)S(1)}, u32[]{:S(2)}, u32[]{:S(2)}) collective-permute-start(bf16[38,32,128]{2,1,0:T(8,128)(2,1)} %get-tuple-element.29), channel_id=1, source_target_pairs={{0,0},{4,8},{8,24},{32,32},{36,40},{40,56},{64,64},{68,72},{72,88}... | collective-permute-start | bytes 933896 | tf_op jit(solution)/shard_map/ppermute | solution.py:432
  23.6 3.4 %collective-permute-start.6 = (bf16[38,32,128]{2,1,0:T(8,128)(2,1)}, bf16[38,32,128]{2,1,0:T(8,128)(2,1)S(1)}, u32[]{:S(2)}, u32[]{:S(2)}) collective-permute-start(bf16[38,32,128]{2,1,0:T(8,128)(2,1)} %get-tuple-element.30), channel_id=1, source_target_pairs={{4,0},{8,8},{12,24},{36,32},{40,40},{44,56},{68,64},{72,72},{76,88... | collective-permute-start | bytes 933896 | tf_op jit(solution)/shard_map/ppermute | solution.py:432
  24.3 2.7 %collective-permute-start.7 = (bf16[38,32,128]{2,1,0:T(8,128)(2,1)}, bf16[38,32,128]{2,1,0:T(8,128)(2,1)S(1)}, u32[]{:S(2)}, u32[]{:S(2)}) collective-permute-start(bf16[38,32,128]{2,1,0:T(8,128)(2,1)} %get-tuple-element.31), channel_id=1, source_target_pairs={{8,0},{12,8},{0,24},{40,32},{44,40},{32,56},{72,64},{76,72},{64,88... | collective-permute-start | bytes 933896 | tf_op jit(solution)/shard_map/ppermute | solution.py:432
  24.9 2.0 %collective-permute-start.8 = (bf16[38,32,128]{2,1,0:T(8,128)(2,1)}, bf16[38,32,128]{2,1,0:T(8,128)(2,1)S(1)}, u32[]{:S(2)}, u32[]{:S(2)}) collective-permute-start(bf16[38,32,128]{2,1,0:T(8,128)(2,1)} %get-tuple-element.32), channel_id=1, source_target_pairs={{12,0},{0,8},{4,24},{44,32},{32,40},{36,56},{76,64},{64,72},{68,88... | collective-permute-start | bytes 933896 | tf_op jit(solution)/shard_map/ppermute | solution.py:432
  25.6 0.7 collective-permute-start.2
  27.2 44.2 %collective-permute-start.13 = (bf16[112,32,128]{2,1,0:T(8,128)(2,1)S(1)}, bf16[112,32,128]{2,1,0:T(8,128)(2,1)S(1)}, u32[]{:S(2)}, u32[]{:S(2)}) collective-permute-start(bf16[112,32,128]{2,1,0:T(8,128)(2,1)S(1)} %get-tuple-element.34), channel_id=1, source_target_pairs={{0,1},{1,2},{2,3},{8,9},{9,10},{10,11},{24,25},{25,26},{26,27},{32... | collective-permute-start | bytes 2752520 | tf_op jit(solution)/shard_map/ppermute | solution.py:446
  28.0 43.5 %collective-permute-start.14 = (bf16[112,32,128]{2,1,0:T(8,128)(2,1)S(1)}, bf16[112,32,128]{2,1,0:T(8,128)(2,1)S(1)}, u32[]{:S(2)}, u32[]{:S(2)}) collective-permute-start(bf16[112,32,128]{2,1,0:T(8,128)(2,1)S(1)} %get-tuple-element.35), channel_id=1, source_target_pairs={{1,0},{2,1},{3,2},{9,8},{10,9},{11,10},{25,24},{26,25},{27,26},{33... | collective-permute-start | bytes 2752520 | tf_op jit(solution)/shard_map/ppermute | solution.py:446
  28.7 26.5 %collective-permute-start.9 = (bf16[38,32,128]{2,1,0:T(8,128)(2,1)}, bf16[38,32,128]{2,1,0:T(8,128)(2,1)S(1)}, u32[]{:S(2)}, u32[]{:S(2)}) collective-permute-start(bf16[38,32,128]{2,1,0:T(8,128)(2,1)} %get-tuple-element.29), channel_id=1, source_target_pairs={{16,0},{20,8},{24,24},{48,32},{52,40},{56,56},{80,64},{84,72},{88,... | collective-permute-start | bytes 933896 | tf_op jit(solution)/shard_map/ppermute | solution.py:432
  29.4 36.3 %collective-permute-start.10 = (bf16[38,32,128]{2,1,0:T(8,128)(2,1)}, bf16[38,32,128]{2,1,0:T(8,128)(2,1)S(1)}, u32[]{:S(2)}, u32[]{:S(2)}) collective-permute-start(bf16[38,32,128]{2,1,0:T(8,128)(2,1)} %get-tuple-element.30), channel_id=1, source_target_pairs={{20,0},{24,8},{28,24},{52,32},{56,40},{60,56},{84,64},{88,72},{92,... | collective-permute-start | bytes 933896 | tf_op jit(solution)/shard_map/ppermute | solution.py:432
  53.8 11.8 %collective-permute-start.11 = (bf16[38,32,128]{2,1,0:T(8,128)(2,1)}, bf16[38,32,128]{2,1,0:T(8,128)(2,1)S(1)}, u32[]{:S(2)}, u32[]{:S(2)}) collective-permute-start(bf16[38,32,128]{2,1,0:T(8,128)(2,1)} %get-tuple-element.31), channel_id=1, source_target_pairs={{24,0},{28,8},{16,24},{56,32},{60,40},{48,56},{88,64},{92,72},{80,... | collective-permute-start | bytes 933896 | tf_op jit(solution)/shard_map/ppermute | solution.py:432
  55.2 14.6 %collective-permute-start.12 = (bf16[38,32,128]{2,1,0:T(8,128)(2,1)}, bf16[38,32,128]{2,1,0:T(8,128)(2,1)S(1)}, u32[]{:S(2)}, u32[]{:S(2)}) collective-permute-start(bf16[38,32,128]{2,1,0:T(8,128)(2,1)} %get-tuple-element.32), channel_id=1, source_target_pairs={{28,0},{16,8},{20,24},{60,32},{48,40},{52,56},{92,64},{80,72},{84,... | collective-permute-start | bytes 933896 | tf_op jit(solution)/shard_map/ppermute | solution.py:432
  69.9 1.6 collective-permute-start.15
  70.6 0.9 collective-permute-start.16
  72.0 2.1 %collective-permute-start.17 = (f32[16,32,128]{2,1,0:T(8,128)S(1)}, f32[16,32,128]{2,1,0:T(8,128)S(1)}, u32[]{:S(2)}, u32[]{:S(2)}) collective-permute-start(f32[16,32,128]{2,1,0:T(8,128)S(1)} %get-tuple-element.39), channel_id=1, source_target_pairs={{0,32},{1,33},{2,34},{3,35},{8,40},{9,41},{10,42},{11,43},{24,56},... | collective-permute-start | bytes 786440 | tf_op jit(solution)/shard_map/ppermute | solution.py:446
  72.7 1.4 collective-permute-start.19
  73.4 0.7 collective-permute-start.18
  74.8 2.1 %collective-permute-start.20 = (f32[16,32,128]{2,1,0:T(8,128)S(1)}, f32[16,32,128]{2,1,0:T(8,128)S(1)}, u32[]{:S(2)}, u32[]{:S(2)}) collective-permute-start(f32[16,32,128]{2,1,0:T(8,128)S(1)} %get-tuple-element.41), channel_id=1, source_target_pairs={{32,64},{33,65},{34,66},{35,67},{40,72},{41,73},{42,74},{43,75},{5... | collective-permute-start | bytes 786440 | tf_op jit(solution)/shard_map/ppermute | solution.py:446
  75.5 1.4 collective-permute-start.22
  76.2 0.7 collective-permute-start.21
  77.5 2.1 %collective-permute-start.23 = (f32[16,32,128]{2,1,0:T(8,128)S(1)}, f32[16,32,128]{2,1,0:T(8,128)S(1)}, u32[]{:S(2)}, u32[]{:S(2)}) collective-permute-start(f32[16,32,128]{2,1,0:T(8,128)S(1)} %get-tuple-element.43), channel_id=1, source_target_pairs={{64,96},{65,97},{66,98},{67,99},{72,104},{73,105},{74,106},{75,107... | collective-permute-start | bytes 786440 | tf_op jit(solution)/shard_map/ppermute | solution.py:446
  78.2 1.4 collective-permute-start.25
  78.8 0.7 collective-permute-start.24
  85.8 3.4 %collective-permute-start.26 = (bf16[2,16,32,128]{3,2,1,0:T(8,128)(2,1)S(1)}, bf16[2,16,32,128]{3,2,1,0:T(8,128)(2,1)S(1)}, u32[]{:S(2)}, u32[]{:S(2)}) collective-permute-start(bf16[2,16,32,128]{3,2,1,0:T(8,128)(2,1)S(1)} %get-tuple-element.45), channel_id=1, source_target_pairs={{0,0},{8,4},{24,8},{32,32},{40,36},{56,40},{64,64},{72,68},{88,72}... | collective-permute-start | bytes 786440 | tf_op jit(solution)/shard_map/ppermute | solution.py:465
  86.5 4.1 %collective-permute-start.27 = (bf16[2,16,32,128]{3,2,1,0:T(8,128)(2,1)S(1)}, bf16[2,16,32,128]{3,2,1,0:T(8,128)(2,1)S(1)}, u32[]{:S(2)}, u32[]{:S(2)}) collective-permute-start(bf16[2,16,32,128]{3,2,1,0:T(8,128)(2,1)S(1)} %get-tuple-element.46), channel_id=1, source_target_pairs={{0,4},{8,8},{24,12},{32,36},{40,40},{56,44},{64,68},{72,72},{88,76... | collective-permute-start | bytes 786440 | tf_op jit(solution)/shard_map/ppermute | solution.py:465
  87.2 4.7 %collective-permute-start.28 = (bf16[2,16,32,128]{3,2,1,0:T(8,128)(2,1)S(1)}, bf16[2,16,32,128]{3,2,1,0:T(8,128)(2,1)S(1)}, u32[]{:S(2)}, u32[]{:S(2)}) collective-permute-start(bf16[2,16,32,128]{3,2,1,0:T(8,128)(2,1)S(1)} %get-tuple-element.47), channel_id=1, source_target_pairs={{0,8},{8,12},{24,0},{32,40},{40,44},{56,32},{64,72},{72,76},{88,64... | collective-permute-start | bytes 786440 | tf_op jit(solution)/shard_map/ppermute | solution.py:465
  87.9 5.3 %collective-permute-start.29 = (bf16[2,16,32,128]{3,2,1,0:T(8,128)(2,1)S(1)}, bf16[2,16,32,128]{3,2,1,0:T(8,128)(2,1)S(1)}, u32[]{:S(2)}, u32[]{:S(2)}) collective-permute-start(bf16[2,16,32,128]{3,2,1,0:T(8,128)(2,1)S(1)} %get-tuple-element.48), channel_id=1, source_target_pairs={{0,12},{8,0},{24,4},{32,44},{40,32},{56,36},{64,76},{72,64},{88,68... | collective-permute-start | bytes 786440 | tf_op jit(solution)/shard_map/ppermute | solution.py:465
  88.6 4.6 %collective-permute-start.30 = (bf16[2,16,32,128]{3,2,1,0:T(8,128)(2,1)S(1)}, bf16[2,16,32,128]{3,2,1,0:T(8,128)(2,1)S(1)}, u32[]{:S(2)}, u32[]{:S(2)}) collective-permute-start(bf16[2,16,32,128]{3,2,1,0:T(8,128)(2,1)S(1)} %get-tuple-element.49), channel_id=1, source_target_pairs={{0,16},{8,20},{24,24},{32,48},{40,52},{56,56},{64,80},{72,84},{88,... | collective-permute-start | bytes 786440 | tf_op jit(solution)/shard_map/ppermute | solution.py:465
  89.3 58.3 %collective-permute-start.31 = (bf16[2,16,32,128]{3,2,1,0:T(8,128)(2,1)S(1)}, bf16[2,16,32,128]{3,2,1,0:T(8,128)(2,1)S(1)}, u32[]{:S(2)}, u32[]{:S(2)}) collective-permute-start(bf16[2,16,32,128]{3,2,1,0:T(8,128)(2,1)S(1)} %get-tuple-element.50), channel_id=1, source_target_pairs={{0,20},{8,24},{24,28},{32,52},{40,56},{56,60},{64,84},{72,88},{88,... | collective-permute-start | bytes 786440 | tf_op jit(solution)/shard_map/ppermute | solution.py:465
  90.6 66.0 %collective-permute-start.32 = (bf16[2,16,32,128]{3,2,1,0:T(8,128)(2,1)S(1)}, bf16[2,16,32,128]{3,2,1,0:T(8,128)(2,1)S(1)}, u32[]{:S(2)}, u32[]{:S(2)}) collective-permute-start(bf16[2,16,32,128]{3,2,1,0:T(8,128)(2,1)S(1)} %get-tuple-element.51), channel_id=1, source_target_pairs={{0,24},{8,28},{24,16},{32,56},{40,60},{56,48},{64,88},{72,92},{88,... | collective-permute-start | bytes 786440 | tf_op jit(solution)/shard_map/ppermute | solution.py:465
  91.9 70.2 %collective-permute-start.33 = (bf16[2,16,32,128]{3,2,1,0:T(8,128)(2,1)S(1)}, bf16[2,16,32,128]{3,2,1,0:T(8,128)(2,1)S(1)}, u32[]{:S(2)}, u32[]{:S(2)}) collective-permute-start(bf16[2,16,32,128]{3,2,1,0:T(8,128)(2,1)S(1)} %get-tuple-element.52), channel_id=1, source_target_pairs={{0,28},{8,16},{24,20},{32,60},{40,48},{56,52},{64,92},{72,80},{88,... | collective-permute-start | bytes 786440 | tf_op jit(solution)/shard_map/ppermute | solution.py:465

commit v4 on v3

--- a/solution.py
+++ b/solution.py
@@ -166,11 +166,11 @@
 
 def rim_kernel(half, b_ref, *refs):
     chunks, rest = refs[:FLOW], refs[FLOW:]
-    if half == 0:
+    if half == 1:
         v1_ref, up_ref, dn_ref, d_ref = rest
         v1 = v1_ref[...].astype(bf16)
-        up_ref[LEAD:] = v1
-        dn_ref[LEAD:] = v1
+        up_ref[HALO - LEAD :] = v1
+        dn_ref[HALO - LEAD :] = v1
     else:
         up_ref, dn_ref, d_ref = rest
     for k in range(FLOW):
@@ -234,9 +234,9 @@
         spread(xs, buf, row + 1, value)
 
     def begin():
-        state[:BAND] = up0_ref[LEAD:].astype(f32)
+        state[:BAND] = up1_ref[HALO - LEAD :].astype(f32)
         state[BAND : 2 * BAND] = v1_ref[...]
-        state[2 * BAND :] = dn0_ref[LEAD:].astype(f32)
+        state[2 * BAND :] = dn1_ref[HALO - LEAD :].astype(f32)
 
     def resume(own_ref, above_ref, below_ref):
         state[:BAND] = above_ref[...].astype(f32)
@@ -337,7 +337,7 @@
 
 
 def rims(half, b, *arrays):
-    total = HALO - LEAD if half else LEAD + BAND
+    total = HALO - LEAD + BAND if half else LEAD
     return pl.pallas_call(
         functools.partial(rim_kernel, half),
         out_shape=(shape(total, C, W),) * 2,
@@ -446,9 +446,10 @@
         return lax.ppermute(value, ("layer", "rows"), pairs)
 
     images = mine.astype(jnp.int32).reshape(1)
-    up, dn = rims(0, images, *received[0], v1)
-    up0, dn0 = among_sweepers(up, 0, 1, range(groups)), among_sweepers(dn, 0, -1, range(groups))
-    up, dn = rims(1, images, *received[1])
+    up, dn = rims(0, images, *received[0])
+    up0 = among_sweepers(up, 0, 1, range(groups))
+    dn0 = among_sweepers(dn, 0, -1, range(groups))
+    up, dn = rims(1, images, *received[1], v1)
     up1, dn1 = among_sweepers(up, 0, 1, range(groups)), among_sweepers(dn, 0, -1, range(groups))
     d, w = order(images, received[0] + received[1])
 

time: 166 us -> 168 us (1.012)
  starting transfers between devices: 65.4 us -> 58.4 us
  Pallas kernels: 18.3 us -> 21.8 us
  local copies, waits for them, and re-layouts: 1.59 us -> 4.78 us
  waiting for transfers between devices: 76.1 us -> 77.8 us
    ppermute x8, starting transfers between devices: 39.6 us -> 32 us  [cycle(): lax.ppermute(sends[k], 'layer', pairs(h, k))]
    unnamed x7 -> x31, local copies, waits for them, and re-layouts: 1.23 us -> 4.42 us
    ppermute x8, waiting for transfers between devices: 68.9 us -> 71.6 us  [cycle(): lax.ppermute(results[FLOW * h + k], 'layer', [(t, s) for s, t in pairs(h,...]
    pallas_call x2, Pallas kernels: 0.37 us -> 2.7 us  [rims(): pl.pallas_call(functools.partial(rim_kernel, half), out_shape=(shape(tota...]
    ppermute x8, waiting for transfers between devices: 4.12 us -> 1.85 us  [cycle(): lax.ppermute(sends[k], 'layer', pairs(h, k))]
  transfers between devices with their start and end apart: 34 -> 34, of which waited for: 5 -> 6; matrix products, arithmetic and copies ran while one was open for 0% -> 1% of each run, Pallas kernels for 4% -> 3%
where the time goes in v4:
time: 168 us
  waiting for transfers between devices  77.8 us (46%)
  starting transfers between devices  58.4 us (35%)
  Pallas kernels  21.8 us (13%)
  local copies, waits for them, and re-layouts  4.78 us (3%)
  other arithmetic  3.91 us (2%)
    ppermute x8, waiting for transfers between devices, cycle(): lax.ppermute(results[FLOW * h + k], 'layer', [(t, s) for s, t in pairs(h,...  71.6 us
    ppermute x8, starting transfers between devices, cycle(): lax.ppermute(sends[k], 'layer', pairs(h, k))  32 us
    ppermute x13, starting transfers between devices, among_sweepers(): return lax.ppermute(value, ('layer', 'rows'), pairs)  8.83 us
    pallas_call x4, Pallas kernels, sweep(): pl.pallas_call(functools.partial(sweep_kernel, stage, closing), out_shape...  8.11 us
    ppermute x8, starting transfers between devices, cycle(): lax.ppermute(results[FLOW * h + k], 'layer', [(t, s) for s, t in pairs(h,...  7.26 us
    pallas_call x1, Pallas kernels, relax(): pl.pallas_call(relax_kernel, out_shape=(shape(CHUNK, C, W),) * FLOW, in_s...  6.19 us
    unnamed x31, local copies, waits for them, and re-layouts  4.42 us
    ppermute x1, starting transfers between devices, cycle(): lax.ppermute(edge_rows(BAND - REACH), 'rows', [(i, i + 1) for i in range(...  3.54 us
  transfers between devices with their start and end apart: 34, of which 6 were waited for; matrix products, arithmetic and copies ran while one was open for 1% of the time, Pallas kernels for 3%

profile of v4, /device:TPU:31, one launch (start us, length us, event | category | flops | bytes accessed | tf_op | source)
XLA Modules:
  0.0 167.5 jit_solution(47951377413051025)
XLA Ops:
  0.0 1.1 copy-done
  1.3 1.5 convert.16
  3.1 0.7 maximum_bitcast_fusion
  3.8 3.5 %collective-permute-start = (bf16[7,4,32,128]{3,2,1,0:T(8,128)(2,1)}, bf16[7,4,32,128]{3,2,1,0:T(8,128)(2,1)S(1)}, u32[]{:S(2)}, u32[]{:S(2)}) collective-permute-start(bf16[7,4,32,128]{3,2,1,0:T(8,128)(2,1)} %maximum_bitcast_fusion), channel_id=1, source_target_pairs={{0,1},{1,2},{2,3},{4,5},{5,6},{6,7},{8,9},{9,10},{10,11},{12,13},{... | collective-permute-start | bytes 688136 | tf_op jit(solution)/shard_map/ppermute | solution.py:412
  7.3 0.7 maximum_bitcast_fusion.1
  8.0 1.3 collective-permute-start.1
  9.4 2.9 %collective-permute-start.4 = (bf16[4,32,288]{2,1,0:T(8,128)(2,1)S(1)}, bf16[4,32,288]{2,1,0:T(8,128)(2,1)S(1)}, u32[]{:S(2)}, u32[]{:S(2)}) collective-permute-start(bf16[4,32,288]{2,1,0:T(8,128)(2,1)S(1)} %slice.23), channel_id=1, source_target_pairs={{4,0},{8,4},{12,8},{16,12},{20,16},{24,20},{28,24},{32,28},{36,32}... | collective-permute-start | bytes 221192 | tf_op jit(solution)/shard_map/ppermute | solution.py:414
  12.4 0.8 collective-permute-done.4.next_ref
  13.2 3.5 %collective-permute-done.1.dn_ref = bf16[7,4,32,128]{3,2,1,0:T(8,128)(2,1)S(1)} collective-permute-done((bf16[7,4,32,128]{3,2,1,0:T(8,128)(2,1)}, bf16[7,4,32,128]{3,2,1,0:T(8,128)(2,1)S(1)}, u32[]{:S(2)}, u32[]{:S(2)}) %collective-permute-start.1) | collective-permute-done | bytes 229408 | tf_op jit(solution)/shard_map/ppermute | solution.py:413
  16.7 6.2 %relax.1 = (bf16[38,32,128]{2,1,0:T(8,128)(2,1)S(1)}, bf16[38,32,128]{2,1,0:T(8,128)(2,1)}, bf16[38,32,128]{2,1,0:T(8,128)(2,1)}, bf16[38,32,128]{2,1,0:T(8,128)(2,1)}) custom-call(s32[6]{0:T(128)S(1)} %stack.27.info_ref, f32[3072,128]{1,0:T(8,128)S(1)} %bitcast.21, bf16[7,4,32,128]{3,2,1,0:T(8,128)(2,1)S(1)} %collective-permute-done.up_ref, ...), custom_call_target="tpu_custom_call" | custom-call | tf_op jit(solution)/shard_map/relax/pallas_call | solution.py:307
  22.9 0.7 collective-permute-start.5
  23.6 0.7 collective-permute-start.6
  24.3 0.7 collective-permute-start.7
  25.0 0.7 collective-permute-start.8
  25.7 0.7 collective-permute-start.9
  26.4 1.4 shard_map.37
  27.8 0.7 collective-permute-start.13
  28.6 0.7 collective-permute-start.14
  29.3 1.3 collective-permute-start.3
  30.6 1.3 collective-permute-start.2
  31.9 24.6 %collective-permute-start.10 = (bf16[38,32,128]{2,1,0:T(8,128)(2,1)}, bf16[38,32,128]{2,1,0:T(8,128)(2,1)}, u32[]{:S(2)}, u32[]{:S(2)}) collective-permute-start(bf16[38,32,128]{2,1,0:T(8,128)(2,1)} %get-tuple-element.30), channel_id=1, source_target_pairs={{20,0},{24,8},{28,24},{52,32},{56,40},{60,56},{84,64},{88,72},{92,... | collective-permute-start | bytes 933896 | tf_op jit(solution)/shard_map/ppermute | solution.py:432
  56.5 2.0 %collective-permute-start.11 = (bf16[38,32,128]{2,1,0:T(8,128)(2,1)}, bf16[38,32,128]{2,1,0:T(8,128)(2,1)}, u32[]{:S(2)}, u32[]{:S(2)}) collective-permute-start(bf16[38,32,128]{2,1,0:T(8,128)(2,1)} %get-tuple-element.31), channel_id=1, source_target_pairs={{24,0},{28,8},{16,24},{56,32},{60,40},{48,56},{88,64},{92,72},{80,... | collective-permute-start | bytes 933896 | tf_op jit(solution)/shard_map/ppermute | solution.py:432
  58.5 0.7 copy-done.4
  59.2 2.0 %collective-permute-start.12 = (bf16[38,32,128]{2,1,0:T(8,128)(2,1)}, bf16[38,32,128]{2,1,0:T(8,128)(2,1)}, u32[]{:S(2)}, u32[]{:S(2)}) collective-permute-start(bf16[38,32,128]{2,1,0:T(8,128)(2,1)} %get-tuple-element.32), channel_id=1, source_target_pairs={{28,0},{16,8},{20,24},{60,32},{48,40},{52,56},{92,64},{80,72},{84,... | collective-permute-start | bytes 933896 | tf_op jit(solution)/shard_map/ppermute | solution.py:432
  61.2 1.0 select_select_fusion.open_ref
  62.2 0.9 copy-done.7
  63.2 0.9 copy-done.9
  65.2 1.8 %collective-permute-done.12.refs_7_.refs_3_ = bf16[38,32,128]{2,1,0:T(8,128)(2,1)} collective-permute-done((bf16[38,32,128]{2,1,0:T(8,128)(2,1)}, bf16[38,32,128]{2,1,0:T(8,128)(2,1)}, u32[]{:S(2)}, u32[]{:S(2)}) %collective-permute-start.12) | collective-permute-done | bytes 311328 | tf_op jit(solution)/shard_map/ppermute | solution.py:432
  67.1 1.3 shard_map.38
  68.4 0.7 collective-permute-start.15
  69.1 0.7 collective-permute-start.16
  69.8 1.3 order.1
  71.7 0.7 collective-permute-start.17
  73.8 0.7 sweep.5
  74.5 0.7 collective-permute-start.20
  77.2 0.7 collective-permute-start.23
  79.2 6.3 %sweep.7 = (bf16[2,16,32,128]{3,2,1,0:T(8,128)(2,1)S(1)}, bf16[2,16,32,128]{3,2,1,0:T(8,128)(2,1)S(1)}, bf16[2,16,32,128]{3,2,1,0:T(8,128)(2,1)S(1)}, bf16[2,16,...) custom-call(s32[6]{0:T(128)S(1)} %copy-done.13, ...), custom_call_target="tpu_custom_call" | custom-call | tf_op jit(solution)/shard_map/sweep/pallas_call | solution.py:386
  85.5 0.7 collective-permute-start.26
  86.2 0.7 collective-permute-start.27
  86.9 0.7 collective-permute-start.28
  87.6 0.7 collective-permute-start.29
  88.9 1.3 collective-permute-start.31
  90.2 1.3 collective-permute-start.32
  91.6 1.3 collective-permute-start.33
  92.9 57.0 %collective-permute-done.31.refs_5_ = bf16[2,16,32,128]{3,2,1,0:T(8,128)(2,1)S(1)} collective-permute-done((bf16[2,16,32,128]{3,2,1,0:T(8,128)(2,1)S(1)}, bf16[2,16,32,128]{3,2,1,0:T(8,128)(2,1)S(1)}, u32[]{:S(2)}, u32[]{:S(2)}) %collective-permute-start.31) | collective-permute-done | bytes 262176 | tf_op jit(solution)/shard_map/ppermute | solution.py:466
  149.9 9.1 %collective-permute-done.32.refs_6_ = bf16[2,16,32,128]{3,2,1,0:T(8,128)(2,1)S(1)} collective-permute-done((bf16[2,16,32,128]{3,2,1,0:T(8,128)(2,1)S(1)}, bf16[2,16,32,128]{3,2,1,0:T(8,128)(2,1)S(1)}, u32[]{:S(2)}, u32[]{:S(2)}) %collective-permute-start.32) | collective-permute-done | bytes 262176 | tf_op jit(solution)/shard_map/ppermute | solution.py:466
  158.9 5.5 %collective-permute-done.33.refs_7_ = bf16[2,16,32,128]{3,2,1,0:T(8,128)(2,1)S(1)} collective-permute-done((bf16[2,16,32,128]{3,2,1,0:T(8,128)(2,1)S(1)}, bf16[2,16,32,128]{3,2,1,0:T(8,128)(2,1)S(1)}, u32[]{:S(2)}, u32[]{:S(2)}) %collective-permute-start.33) | collective-permute-done | bytes 262176 | tf_op jit(solution)/shard_map/ppermute | solution.py:466
  164.4 2.9 %finish.1 = f32[3072,128]{1,0:T(8,128)} custom-call(s32[6]{0:T(128)S(1)} %copy-done.13, bf16[2,16,32,128]{3,2,1,0:T(8,128)(2,1)S(1)} %collective-permute-done.26.refs_0_, bf16[2,16,32,128]{3,2,1,0:T(8,128)(2,1)S(1)} %collective-permute-done.27.refs_1_, bf16[2,16,32,128]{3,2,1,0:T(8,128)(2,1)S(1)} %collective-permute-done.28.refs_2_, ...), custom_call_target="tpu_custom_call" | custom-call | tf_op jit(solution)/shard_map/finish/pallas_call | solution.py:352
  (71 shorter events, 7.5 us)
Async XLA Ops:
  0.0 1.1 copy-start
  2.8 6.5 %copy-start.10 = (bf16[8,32,288]{2,1,0:T(8,128)(2,1)S(1)}, bf16[8,32,288]{2,1,0:T(8,128)(2,1)}, u32[]{:S(2)}) copy-start(bf16[8,32,288]{2,1,0:T(8,128)(2,1)} %here_ref.1) | copy-start | bytes 442372
  2.8 13.9 %copy-start.1 = (f32[2,3,32,16,128]{4,3,2,1,0:T(8,128)S(1)}, f32[2,3,32,16,128]{4,3,2,1,0:T(8,128)}, u32[]{:S(2)}) copy-start(f32[2,3,32,16,128]{4,3,2,1,0:T(8,128)} %param.5) | copy-start | bytes 4718596
  3.8 9.4 %collective-permute-start = (bf16[7,4,32,128]{3,2,1,0:T(8,128)(2,1)}, bf16[7,4,32,128]{3,2,1,0:T(8,128)(2,1)S(1)}, u32[]{:S(2)}, u32[]{:S(2)}) collective-permute-start(bf16[7,4,32,128]{3,2,1,0:T(8,128)(2,1)} %maximum_bitcast_fusion), channel_id=1, source_target_pairs={{0,1},{1,2},{2,3},{4,5},{5,6},{6,7},{8,9},{9,10},{10,11},{12,13},{... | collective-permute-start | bytes 688136 | tf_op jit(solution)/shard_map/ppermute | solution.py:412
  8.0 8.6 %collective-permute-start.1 = (bf16[7,4,32,128]{3,2,1,0:T(8,128)(2,1)}, bf16[7,4,32,128]{3,2,1,0:T(8,128)(2,1)S(1)}, u32[]{:S(2)}, u32[]{:S(2)}) collective-permute-start(bf16[7,4,32,128]{3,2,1,0:T(8,128)(2,1)} %maximum_bitcast_fusion.1), channel_id=1, source_target_pairs={{1,0},{2,1},{3,2},{5,4},{6,5},{7,6},{9,8},{10,9},{11,10},{13,12},{... | collective-permute-start | bytes 688136 | tf_op jit(solution)/shard_map/ppermute | solution.py:413
  9.3 14.9 %copy-start.14 = (bf16[4,32,288]{2,1,0:T(8,128)(2,1)}, bf16[4,32,288]{2,1,0:T(8,128)(2,1)S(1)}, u32[]{:S(2)}) copy-start(bf16[4,32,288]{2,1,0:T(8,128)(2,1)S(1)} %slice.23) | copy-start | bytes 221188
  9.4 3.8 %collective-permute-start.4 = (bf16[4,32,288]{2,1,0:T(8,128)(2,1)S(1)}, bf16[4,32,288]{2,1,0:T(8,128)(2,1)S(1)}, u32[]{:S(2)}, u32[]{:S(2)}) collective-permute-start(bf16[4,32,288]{2,1,0:T(8,128)(2,1)S(1)} %slice.23), channel_id=1, source_target_pairs={{4,0},{8,4},{12,8},{16,12},{20,16},{24,20},{28,24},{32,28},{36,32}... | collective-permute-start | bytes 221192 | tf_op jit(solution)/shard_map/ppermute | solution.py:414
  12.4 11.9 %copy-start.11 = (s32[6]{0:T(128)}, s32[6]{0:T(128)S(1)}, u32[]{:S(2)}) copy-start(s32[6]{0:T(128)S(1)} %stack.27.info_ref) | copy-start | bytes 76
  13.2 9.7 %copy-start.6 = (bf16[7,4,32,128]{3,2,1,0:T(8,128)(2,1)}, bf16[7,4,32,128]{3,2,1,0:T(8,128)(2,1)S(1)}, u32[]{:S(2)}) copy-start(bf16[7,4,32,128]{3,2,1,0:T(8,128)(2,1)S(1)} %collective-permute-done.up_ref) | copy-start | bytes 688132
  16.7 6.2 %copy-start.8 = (bf16[7,4,32,128]{3,2,1,0:T(8,128)(2,1)}, bf16[7,4,32,128]{3,2,1,0:T(8,128)(2,1)S(1)}, u32[]{:S(2)}) copy-start(bf16[7,4,32,128]{3,2,1,0:T(8,128)(2,1)S(1)} %collective-permute-done.1.dn_ref) | copy-start | bytes 688132
  22.9 3.5 %collective-permute-start.5 = (bf16[38,32,128]{2,1,0:T(8,128)(2,1)S(1)}, bf16[38,32,128]{2,1,0:T(8,128)(2,1)S(1)}, u32[]{:S(2)}, u32[]{:S(2)}) collective-permute-start(bf16[38,32,128]{2,1,0:T(8,128)(2,1)S(1)} %get-tuple-element.29), channel_id=1, source_target_pairs={{0,0},{4,8},{8,24},{32,32},{36,40},{40,56},{64,64},{68,72},{72,88}... | collective-permute-start | bytes 933896 | tf_op jit(solution)/shard_map/ppermute | solution.py:432
  23.6 2.8 %collective-permute-start.6 = (bf16[38,32,128]{2,1,0:T(8,128)(2,1)}, bf16[38,32,128]{2,1,0:T(8,128)(2,1)S(1)}, u32[]{:S(2)}, u32[]{:S(2)}) collective-permute-start(bf16[38,32,128]{2,1,0:T(8,128)(2,1)} %get-tuple-element.30), channel_id=1, source_target_pairs={{4,0},{8,8},{12,24},{36,32},{40,40},{44,56},{68,64},{72,72},{76,88... | collective-permute-start | bytes 933896 | tf_op jit(solution)/shard_map/ppermute | solution.py:432
  24.3 2.1 %collective-permute-start.7 = (bf16[38,32,128]{2,1,0:T(8,128)(2,1)}, bf16[38,32,128]{2,1,0:T(8,128)(2,1)S(1)}, u32[]{:S(2)}, u32[]{:S(2)}) collective-permute-start(bf16[38,32,128]{2,1,0:T(8,128)(2,1)} %get-tuple-element.31), channel_id=1, source_target_pairs={{8,0},{12,8},{0,24},{40,32},{44,40},{32,56},{72,64},{76,72},{64,88... | collective-permute-start | bytes 933896 | tf_op jit(solution)/shard_map/ppermute | solution.py:432
  25.0 1.4 collective-permute-start.8
  25.7 32.8 %collective-permute-start.9 = (bf16[38,32,128]{2,1,0:T(8,128)(2,1)S(1)}, bf16[38,32,128]{2,1,0:T(8,128)(2,1)S(1)}, u32[]{:S(2)}, u32[]{:S(2)}) collective-permute-start(bf16[38,32,128]{2,1,0:T(8,128)(2,1)S(1)} %get-tuple-element.29), channel_id=1, source_target_pairs={{16,0},{20,8},{24,24},{48,32},{52,40},{56,56},{80,64},{84,72},{88,... | collective-permute-start | bytes 933896 | tf_op jit(solution)/shard_map/ppermute | solution.py:432
  26.4 2.1 %copy-start.2 = (bf16[38,32,128]{2,1,0:T(8,128)(2,1)}, bf16[38,32,128]{2,1,0:T(8,128)(2,1)S(1)}, u32[]{:S(2)}) copy-start(bf16[38,32,128]{2,1,0:T(8,128)(2,1)S(1)} %collective-permute-done.8.refs_3_) | copy-start | bytes 933892
  27.8 43.3 %collective-permute-start.13 = (bf16[96,32,128]{2,1,0:T(8,128)(2,1)}, bf16[96,32,128]{2,1,0:T(8,128)(2,1)S(1)}, u32[]{:S(2)}, u32[]{:S(2)}) collective-permute-start(bf16[96,32,128]{2,1,0:T(8,128)(2,1)} %get-tuple-element.34), channel_id=1, source_target_pairs={{0,1},{1,2},{2,3},{8,9},{9,10},{10,11},{24,25},{25,26},{26,27},{32... | collective-permute-start | bytes 2359304 | tf_op jit(solution)/shard_map/ppermute | solution.py:446
  28.6 42.6 %collective-permute-start.14 = (bf16[96,32,128]{2,1,0:T(8,128)(2,1)}, bf16[96,32,128]{2,1,0:T(8,128)(2,1)S(1)}, u32[]{:S(2)}, u32[]{:S(2)}) collective-permute-start(bf16[96,32,128]{2,1,0:T(8,128)(2,1)} %get-tuple-element.35), channel_id=1, source_target_pairs={{1,0},{2,1},{3,2},{9,8},{10,9},{11,10},{25,24},{26,25},{27,26},{33... | collective-permute-start | bytes 2359304 | tf_op jit(solution)/shard_map/ppermute | solution.py:446
  29.3 2.6 %collective-permute-start.3 = (bf16[4,32,288]{2,1,0:T(8,128)(2,1)}, bf16[4,32,288]{2,1,0:T(8,128)(2,1)}, u32[]{:S(2)}, u32[]{:S(2)}) collective-permute-start(bf16[4,32,288]{2,1,0:T(8,128)(2,1)} %copy-done.14), channel_id=1, source_target_pairs={{0,8},{1,9},{2,10},{3,11}} | collective-permute-start | bytes 221192 | tf_op jit(solution)/shard_map/ppermute | solution.py:417
  30.6 25.9 %collective-permute-start.2 = (bf16[4,32,288]{2,1,0:T(8,128)(2,1)}, bf16[4,32,288]{2,1,0:T(8,128)(2,1)}, u32[]{:S(2)}, u32[]{:S(2)}) collective-permute-start(bf16[4,32,288]{2,1,0:T(8,128)(2,1)} %copy-done.14), channel_id=1, source_target_pairs={{0,24},{1,25},{2,26},{3,27}} | collective-permute-start | bytes 221192 | tf_op jit(solution)/shard_map/ppermute | solution.py:417
  31.9 33.3 %collective-permute-start.10 = (bf16[38,32,128]{2,1,0:T(8,128)(2,1)}, bf16[38,32,128]{2,1,0:T(8,128)(2,1)}, u32[]{:S(2)}, u32[]{:S(2)}) collective-permute-start(bf16[38,32,128]{2,1,0:T(8,128)(2,1)} %get-tuple-element.30), channel_id=1, source_target_pairs={{20,0},{24,8},{28,24},{52,32},{56,40},{60,56},{84,64},{88,72},{92,... | collective-permute-start | bytes 933896 | tf_op jit(solution)/shard_map/ppermute | solution.py:432
  56.5 8.7 %collective-permute-start.11 = (bf16[38,32,128]{2,1,0:T(8,128)(2,1)}, bf16[38,32,128]{2,1,0:T(8,128)(2,1)}, u32[]{:S(2)}, u32[]{:S(2)}) collective-permute-start(bf16[38,32,128]{2,1,0:T(8,128)(2,1)} %get-tuple-element.31), channel_id=1, source_target_pairs={{24,0},{28,8},{16,24},{56,32},{60,40},{48,56},{88,64},{92,72},{80,... | collective-permute-start | bytes 933896 | tf_op jit(solution)/shard_map/ppermute | solution.py:432
  58.5 0.7 copy-start.4
  59.2 7.8 %collective-permute-start.12 = (bf16[38,32,128]{2,1,0:T(8,128)(2,1)}, bf16[38,32,128]{2,1,0:T(8,128)(2,1)}, u32[]{:S(2)}, u32[]{:S(2)}) collective-permute-start(bf16[38,32,128]{2,1,0:T(8,128)(2,1)} %get-tuple-element.32), channel_id=1, source_target_pairs={{28,0},{16,8},{20,24},{60,32},{48,40},{52,56},{92,64},{80,72},{84,... | collective-permute-start | bytes 933896 | tf_op jit(solution)/shard_map/ppermute | solution.py:432
  61.2 5.8 %copy-start.5 = (bf16[38,32,128]{2,1,0:T(8,128)(2,1)S(1)}, bf16[38,32,128]{2,1,0:T(8,128)(2,1)}, u32[]{:S(2)}) copy-start(bf16[38,32,128]{2,1,0:T(8,128)(2,1)} %copy-done.4) | copy-start | bytes 933892
  61.2 8.5 %copy-start.3 = (bf16[38,32,128]{2,1,0:T(8,128)(2,1)S(1)}, bf16[38,32,128]{2,1,0:T(8,128)(2,1)}, u32[]{:S(2)}) copy-start(bf16[38,32,128]{2,1,0:T(8,128)(2,1)} %copy-done.2) | copy-start | bytes 933892
  62.2 0.9 copy-start.7
  63.2 0.9 copy-start.9
  68.4 2.8 %copy-start.13 = (s32[6]{0:T(128)S(1)}, s32[6]{0:T(128)}, u32[]{:S(2)}) copy-start(s32[6]{0:T(128)} %copy-done.11) | copy-start | bytes 76
  68.4 2.7 %collective-permute-start.15 = (bf16[48,32,128]{2,1,0:T(8,128)(2,1)S(1)}, bf16[48,32,128]{2,1,0:T(8,128)(2,1)S(1)}, u32[]{:S(2)}, u32[]{:S(2)}) collective-permute-start(bf16[48,32,128]{2,1,0:T(8,128)(2,1)S(1)} %get-tuple-element.36), channel_id=1, source_target_pairs={{0,1},{1,2},{2,3},{8,9},{9,10},{10,11},{24,25},{25,26},{26,27},{32... | collective-permute-start | bytes 1179656 | tf_op jit(solution)/shard_map/ppermute | solution.py:446
  69.1 2.0 %collective-permute-start.16 = (bf16[48,32,128]{2,1,0:T(8,128)(2,1)S(1)}, bf16[48,32,128]{2,1,0:T(8,128)(2,1)S(1)}, u32[]{:S(2)}, u32[]{:S(2)}) collective-permute-start(bf16[48,32,128]{2,1,0:T(8,128)(2,1)S(1)} %get-tuple-element.37), channel_id=1, source_target_pairs={{1,0},{2,1},{3,2},{9,8},{10,9},{11,10},{25,24},{26,25},{27,26},{33... | collective-permute-start | bytes 1179656 | tf_op jit(solution)/shard_map/ppermute | solution.py:446
  71.7 2.1 %collective-permute-start.17 = (f32[16,32,128]{2,1,0:T(8,128)S(1)}, f32[16,32,128]{2,1,0:T(8,128)S(1)}, u32[]{:S(2)}, u32[]{:S(2)}) collective-permute-start(f32[16,32,128]{2,1,0:T(8,128)S(1)} %get-tuple-element.39), channel_id=1, source_target_pairs={{0,32},{1,33},{2,34},{3,35},{8,40},{9,41},{10,42},{11,43},{24,56},... | collective-permute-start | bytes 786440 | tf_op jit(solution)/shard_map/ppermute | solution.py:446
  72.4 1.4 collective-permute-start.19
  73.1 0.7 collective-permute-start.18
  74.5 2.1 %collective-permute-start.20 = (f32[16,32,128]{2,1,0:T(8,128)S(1)}, f32[16,32,128]{2,1,0:T(8,128)S(1)}, u32[]{:S(2)}, u32[]{:S(2)}) collective-permute-start(f32[16,32,128]{2,1,0:T(8,128)S(1)} %get-tuple-element.41), channel_id=1, source_target_pairs={{32,64},{33,65},{34,66},{35,67},{40,72},{41,73},{42,74},{43,75},{5... | collective-permute-start | bytes 786440 | tf_op jit(solution)/shard_map/ppermute | solution.py:446
  75.2 1.4 collective-permute-start.22
  75.9 0.7 collective-permute-start.21
  77.2 2.1 %collective-permute-start.23 = (f32[16,32,128]{2,1,0:T(8,128)S(1)}, f32[16,32,128]{2,1,0:T(8,128)S(1)}, u32[]{:S(2)}, u32[]{:S(2)}) collective-permute-start(f32[16,32,128]{2,1,0:T(8,128)S(1)} %get-tuple-element.43), channel_id=1, source_target_pairs={{64,96},{65,97},{66,98},{67,99},{72,104},{73,105},{74,106},{75,107... | collective-permute-start | bytes 786440 | tf_op jit(solution)/shard_map/ppermute | solution.py:446
  77.8 1.4 collective-permute-start.25
  78.5 0.7 collective-permute-start.24
  85.5 3.4 %collective-permute-start.26 = (bf16[2,16,32,128]{3,2,1,0:T(8,128)(2,1)S(1)}, bf16[2,16,32,128]{3,2,1,0:T(8,128)(2,1)S(1)}, u32[]{:S(2)}, u32[]{:S(2)}) collective-permute-start(bf16[2,16,32,128]{3,2,1,0:T(8,128)(2,1)S(1)} %get-tuple-element.45), channel_id=1, source_target_pairs={{0,0},{8,4},{24,8},{32,32},{40,36},{56,40},{64,64},{72,68},{88,72}... | collective-permute-start | bytes 786440 | tf_op jit(solution)/shard_map/ppermute | solution.py:466
  86.2 4.1 %collective-permute-start.27 = (bf16[2,16,32,128]{3,2,1,0:T(8,128)(2,1)S(1)}, bf16[2,16,32,128]{3,2,1,0:T(8,128)(2,1)S(1)}, u32[]{:S(2)}, u32[]{:S(2)}) collective-permute-start(bf16[2,16,32,128]{3,2,1,0:T(8,128)(2,1)S(1)} %get-tuple-element.46), channel_id=1, source_target_pairs={{0,4},{8,8},{24,12},{32,36},{40,40},{56,44},{64,68},{72,72},{88,76... | collective-permute-start | bytes 786440 | tf_op jit(solution)/shard_map/ppermute | solution.py:466
  86.9 4.7 %collective-permute-start.28 = (bf16[2,16,32,128]{3,2,1,0:T(8,128)(2,1)S(1)}, bf16[2,16,32,128]{3,2,1,0:T(8,128)(2,1)S(1)}, u32[]{:S(2)}, u32[]{:S(2)}) collective-permute-start(bf16[2,16,32,128]{3,2,1,0:T(8,128)(2,1)S(1)} %get-tuple-element.47), channel_id=1, source_target_pairs={{0,8},{8,12},{24,0},{32,40},{40,44},{56,32},{64,72},{72,76},{88,64... | collective-permute-start | bytes 786440 | tf_op jit(solution)/shard_map/ppermute | solution.py:466
  87.6 5.3 %collective-permute-start.29 = (bf16[2,16,32,128]{3,2,1,0:T(8,128)(2,1)S(1)}, bf16[2,16,32,128]{3,2,1,0:T(8,128)(2,1)S(1)}, u32[]{:S(2)}, u32[]{:S(2)}) collective-permute-start(bf16[2,16,32,128]{3,2,1,0:T(8,128)(2,1)S(1)} %get-tuple-element.48), channel_id=1, source_target_pairs={{0,12},{8,0},{24,4},{32,44},{40,32},{56,36},{64,76},{72,64},{88,68... | collective-permute-start | bytes 786440 | tf_op jit(solution)/shard_map/ppermute | solution.py:466
  88.2 4.6 %collective-permute-start.30 = (bf16[2,16,32,128]{3,2,1,0:T(8,128)(2,1)S(1)}, bf16[2,16,32,128]{3,2,1,0:T(8,128)(2,1)S(1)}, u32[]{:S(2)}, u32[]{:S(2)}) collective-permute-start(bf16[2,16,32,128]{3,2,1,0:T(8,128)(2,1)S(1)} %get-tuple-element.49), channel_id=1, source_target_pairs={{0,16},{8,20},{24,24},{32,48},{40,52},{56,56},{64,80},{72,84},{88,... | collective-permute-start | bytes 786440 | tf_op jit(solution)/shard_map/ppermute | solution.py:466
  88.9 60.9 %collective-permute-start.31 = (bf16[2,16,32,128]{3,2,1,0:T(8,128)(2,1)S(1)}, bf16[2,16,32,128]{3,2,1,0:T(8,128)(2,1)S(1)}, u32[]{:S(2)}, u32[]{:S(2)}) collective-permute-start(bf16[2,16,32,128]{3,2,1,0:T(8,128)(2,1)S(1)} %get-tuple-element.50), channel_id=1, source_target_pairs={{0,20},{8,24},{24,28},{32,52},{40,56},{56,60},{64,84},{72,88},{88,... | collective-permute-start | bytes 786440 | tf_op jit(solution)/shard_map/ppermute | solution.py:466
  90.2 68.7 %collective-permute-start.32 = (bf16[2,16,32,128]{3,2,1,0:T(8,128)(2,1)S(1)}, bf16[2,16,32,128]{3,2,1,0:T(8,128)(2,1)S(1)}, u32[]{:S(2)}, u32[]{:S(2)}) collective-permute-start(bf16[2,16,32,128]{3,2,1,0:T(8,128)(2,1)S(1)} %get-tuple-element.51), channel_id=1, source_target_pairs={{0,24},{8,28},{24,16},{32,56},{40,60},{56,48},{64,88},{72,92},{88,... | collective-permute-start | bytes 786440 | tf_op jit(solution)/shard_map/ppermute | solution.py:466
  91.6 72.9 %collective-permute-start.33 = (bf16[2,16,32,128]{3,2,1,0:T(8,128)(2,1)S(1)}, bf16[2,16,32,128]{3,2,1,0:T(8,128)(2,1)S(1)}, u32[]{:S(2)}, u32[]{:S(2)}) collective-permute-start(bf16[2,16,32,128]{3,2,1,0:T(8,128)(2,1)S(1)} %get-tuple-element.52), channel_id=1, source_target_pairs={{0,28},{8,16},{24,20},{32,60},{40,48},{56,52},{64,92},{72,80},{88,... | collective-permute-start | bytes 786440 | tf_op jit(solution)/shard_map/ppermute | solution.py:466
  (1 other events, 0.6 us)

commit v5 on v3

--- a/solution.py
+++ b/solution.py
@@ -110,6 +110,14 @@
     return load, layer
 
 
+def edges_kernel(info_ref, own_ref, img_ref, up_ref, dn_ref):
+    for u in range(2 * IMAGES + 1):
+        ref, at = (own_ref, u * (C * BAND)) if u < 2 * IMAGES else (img_ref, info_ref[3] * (C * BAND))
+        for r in range(REACH):
+            dn_ref[u, r] = ref[pl.ds(at + r, C, stride=BAND), :].astype(bf16)
+            up_ref[u, r] = ref[pl.ds(at + BAND - REACH + r, C, stride=BAND), :].astype(bf16)
+
+
 def tiles(ref, n):
     tail = jnp.concatenate([ref[n, :, 2 * W :], jnp.zeros((C, 3 * C), bf16)], axis=1)
     return [ref[n, :, :W], ref[n, :, W : 2 * W], tail]
@@ -156,11 +164,12 @@
     @pl.when(info_ref[2] == 1)
     def _():
         clear_rims(xs, SPAN)
-        load(0, 2 * IMAGES, up_ref, img_ref, dn_ref, 0)
+        at = info_ref[3] * (C * BAND)
+        load(0, 2 * IMAGES, up_ref, img_ref, dn_ref, at)
         for j in range(M):
             layer(0, j, banded(tiles(open_ref, j)))
         for r in range(BAND):
-            x = img_ref[pl.ds(r, C, stride=BAND), :]
+            x = img_ref[pl.ds(at + r, C, stride=BAND), :]
             v1_ref[r] = x + (state[0, REACH + r] - x.astype(bf16).astype(f32))
 
 
@@ -194,7 +203,8 @@
 
 
 def finish_kernel(info_ref, *refs):
-    arrived, (out_ref, picked, stage, sems) = refs[:SUB], refs[SUB:]
+    arrived, (out_ref, picked, stage, ready, sems, leave) = refs[:SUB], refs[SUB:]
+    writes = []
     turn, half = info_ref[1], info_ref[4]
     for b in range(IMAGES):
         want = lax.rem(turn - b + FLOW, FLOW) + FLOW * half
@@ -209,8 +219,13 @@
         for p in range(2):
             stage[b, p] = picked[b, p].astype(f32).reshape(BAND * C, W)
             for c in range(C):
-                to = ((p * IMAGES + b) * C + c) * BAND
-                out_ref[to : to + BAND] = stage[b, p, pl.ds(c, BAND, stride=C), :]
+                ready[b, p, c * BAND : (c + 1) * BAND] = stage[b, p, pl.ds(c, BAND, stride=C), :]
+            to = (p * IMAGES + b) * (C * BAND)
+            copy = pltpu.make_async_copy(ready.at[b, p], out_ref.at[to : to + C * BAND], leave.at[b, p])
+            copy.start()
+            writes.append(copy)
+    for copy in writes:
+        copy.wait()
 
 
 def sweep_kernel(
@@ -303,6 +318,17 @@
     return jax.ShapeDtypeStruct(dims, dtype)
 
 
+def edges(info, *arrays):
+    return pl.pallas_call(
+        edges_kernel,
+        out_shape=(shape(2 * IMAGES + 1, REACH, C, W),) * 2,
+        in_specs=[SM] + [VM] * len(arrays),
+        out_specs=(VM, VM),
+        compiler_params=GRANT,
+        name="edges",
+    )(info, *arrays)
+
+
 def relax(info, *arrays):
     return pl.pallas_call(
         relax_kernel,
@@ -353,11 +379,13 @@
         finish_kernel,
         out_shape=shape(2 * IMAGES * C * BAND, W, dtype=f32),
         in_specs=[SM] + [AN] * SUB,
-        out_specs=VM,
+        out_specs=AN,
         scratch_shapes=[
             pltpu.VMEM((IMAGES, 2, BAND, C, W), bf16),
             pltpu.VMEM((IMAGES, 2, BAND * C, W), f32),
+            pltpu.VMEM((IMAGES, 2, BAND * C, W), f32),
             pltpu.SemaphoreType.DMA((IMAGES,)),
+            pltpu.SemaphoreType.DMA((IMAGES, 2)),
         ],
         compiler_params=GRANT,
         name="finish",
@@ -401,24 +429,19 @@
     sub, group = lax.rem(l, SUB), l // SUB
     mine = jnp.where(sub == home(1), 1, jnp.where(sub == home(2), 2, 0))
 
-    own_image = lax.dynamic_index_in_dim(image, mine, 0, keepdims=False)
-    flat = guess.reshape(2 * IMAGES, C, BAND, W)
-
-    def edge_rows(first):
-        rim = jnp.concatenate([flat[:, :, first : first + REACH], own_image[None, :, first : first + REACH]], axis=0)
-        return rim.transpose(0, 2, 1, 3).astype(bf16)
+    lead = jnp.where(group == 0, 1, 0)
+    info = jnp.stack([z, lax.rem(sub, FLOW), lead, mine, sub // FLOW, group]).astype(jnp.int32)
+    rim_up, rim_dn = edges(info, guess.reshape(-1, W), image.reshape(-1, W))
 
     small = weights[:M]
-    up = lax.ppermute(edge_rows(BAND - REACH), "rows", [(i, i + 1) for i in range(rows - 1)])
-    dn = lax.ppermute(edge_rows(0), "rows", [(i + 1, i) for i in range(rows - 1)])
+    up = lax.ppermute(rim_up, "rows", [(i, i + 1) for i in range(rows - 1)])
+    dn = lax.ppermute(rim_dn, "rows", [(i + 1, i) for i in range(rows - 1)])
     following = lax.ppermute(small, "layer", [(i + 1, i) for i in range(layers - 1)])
     opening = small
     for b in range(1, IMAGES):
         got = lax.ppermute(small, "layer", [(0, home(b))])
         opening = jnp.where(l == home(b), got, opening)
 
-    lead = jnp.where(group == 0, 1, 0)
-    info = jnp.stack([z, lax.rem(sub, FLOW), lead, mine, sub // FLOW, group]).astype(jnp.int32)
     sends = relax(info, guess.reshape(-1, W), up, dn, weights, following)
 
     def pairs(half, k):
@@ -432,7 +455,7 @@
         [lax.ppermute(sends[k], "layer", pairs(h, k)) for k in range(FLOW)] for h in range(HALVES)
     ]
 
-    v1 = opened(info, own_image.reshape(-1, W), up, dn, opening)
+    v1 = opened(info, image.reshape(-1, W), up, dn, opening)
 
     def among_sweepers(value, ahead, by, live):
         pairs = []

time: 166 us -> 164 us (0.988)
  other arithmetic: 2.96 us -> 0.03 us
  transfers between devices with their start and end apart: 34 -> 34, of which waited for: 5 -> 6; matrix products, arithmetic and copies ran while one was open for 0% -> 0% of each run, Pallas kernels for 4% -> 4%
where the time goes in v5:
time: 164 us; the launch traced here: 163 us
  waiting for transfers between devices  76.5 us (47%)
  starting transfers between devices  64.9 us (40%)
  Pallas kernels  18.7 us (11%)
  local copies, waits for them, and re-layouts  2.65 us (2%)
    ppermute x8, waiting for transfers between devices, cycle(): lax.ppermute(results[FLOW * h + k], 'layer', [(t, s) for s, t in pairs(h,...  69 us
    ppermute x8, starting transfers between devices, cycle(): lax.ppermute(sends[k], 'layer', pairs(h, k))  39 us
    ppermute x13, starting transfers between devices, among_sweepers(): return lax.ppermute(value, ('layer', 'rows'), pairs)  8.84 us
    pallas_call x4, Pallas kernels, sweep(): pl.pallas_call(functools.partial(sweep_kernel, stage, closing), out_shape...  8.13 us
    ppermute x8, starting transfers between devices, cycle(): lax.ppermute(results[FLOW * h + k], 'layer', [(t, s) for s, t in pairs(h,...  7.26 us
    pallas_call x1, Pallas kernels, relax(): pl.pallas_call(relax_kernel, out_shape=(shape(CHUNK, C, W),) * FLOW, in_s...  6.11 us
    ppermute x8, waiting for transfers between devices, cycle(): lax.ppermute(sends[k], 'layer', pairs(h, k))  3.8 us
    ppermute x1, starting transfers between devices, cycle(): up = lax.ppermute(rim_up, 'rows', [(i, i + 1) for i in range(rows - 1)])  3.69 us
  transfers between devices with their start and end apart: 34, of which 6 were waited for; matrix products, arithmetic and copies ran while one was open for 0% of the time, Pallas kernels for 4%

profile of v5, /device:TPU:31, one launch (start us, length us, event | category | flops | bytes accessed | tf_op | source)
XLA Modules:
  0.0 163.5 jit_solution(12221479176320593710)
XLA Ops:
  0.1 1.4 copy-done
  1.5 1.1 copy-done.1
  2.6 0.8 edges.1
  3.4 3.7 %collective-permute-start = (bf16[7,4,32,128]{3,2,1,0:T(8,128)(2,1)S(1)}, bf16[7,4,32,128]{3,2,1,0:T(8,128)(2,1)S(1)}, u32[]{:S(2)}, u32[]{:S(2)}) collective-permute-start(bf16[7,4,32,128]{3,2,1,0:T(8,128)(2,1)S(1)} %get-tuple-element.31), channel_id=1, source_target_pairs={{0,1},{1,2},{2,3},{4,5},{5,6},{6,7},{8,9},{9,10},{10,11},{12,13},{... | collective-permute-start | bytes 688136 | tf_op jit(solution)/shard_map/ppermute | solution.py:437
  7.1 1.3 collective-permute-start.1
  8.5 2.9 %collective-permute-start.4 = (bf16[4,32,288]{2,1,0:T(8,128)(2,1)S(1)}, bf16[4,32,288]{2,1,0:T(8,128)(2,1)S(1)}, u32[]{:S(2)}, u32[]{:S(2)}) collective-permute-start(bf16[4,32,288]{2,1,0:T(8,128)(2,1)S(1)} %slice.3), channel_id=1, source_target_pairs={{4,0},{8,4},{12,8},{16,12},{20,16},{24,20},{28,24},{32,28},{36,32}... | collective-permute-start | bytes 221192 | tf_op jit(solution)/shard_map/ppermute | solution.py:439
  11.3 0.7 collective-permute-start.3
  12.3 3.3 %collective-permute-done.1.dn_ref = bf16[7,4,32,128]{3,2,1,0:T(8,128)(2,1)S(1)} collective-permute-done((bf16[7,4,32,128]{3,2,1,0:T(8,128)(2,1)S(1)}, bf16[7,4,32,128]{3,2,1,0:T(8,128)(2,1)S(1)}, u32[]{:S(2)}, u32[]{:S(2)}) %collective-permute-start.1) | collective-permute-done | bytes 229408 | tf_op jit(solution)/shard_map/ppermute | solution.py:438
  15.6 6.1 %relax.1 = (bf16[38,32,128]{2,1,0:T(8,128)(2,1)}, bf16[38,32,128]{2,1,0:T(8,128)(2,1)}, bf16[38,32,128]{2,1,0:T(8,128)(2,1)S(1)}, bf16[38,32,128]{2,1,0:T(8,128)(2,1)S(1)}) custom-call(s32[6]{0:T(128)S(1)} %stack.27.info_ref, f32[3072,128]{1,0:T(8,128)S(1)} %bitcast.10, bf16[7,4,32,128]{3,2,1,0:T(8,128)(2,1)S(1)} %collective-permute-done.up_ref, ...), custom_call_target="tpu_custom_call" | custom-call | tf_op jit(solution)/shard_map/relax/pallas_call | solution.py:333
  21.7 0.7 collective-permute-start.5
  22.4 0.7 collective-permute-start.6
  23.1 0.7 collective-permute-start.7
  23.8 0.7 collective-permute-start.8
  24.5 1.3 collective-permute-start.2
  26.7 0.7 collective-permute-start.13
  27.4 0.7 collective-permute-start.14
  28.1 0.7 collective-permute-start.9
  28.8 23.8 %collective-permute-start.10 = (bf16[38,32,128]{2,1,0:T(8,128)(2,1)}, bf16[38,32,128]{2,1,0:T(8,128)(2,1)S(1)}, u32[]{:S(2)}, u32[]{:S(2)}) collective-permute-start(bf16[38,32,128]{2,1,0:T(8,128)(2,1)} %get-tuple-element.34), channel_id=1, source_target_pairs={{20,0},{24,8},{28,24},{52,32},{56,40},{60,56},{84,64},{88,72},{92,... | collective-permute-start | bytes 933896 | tf_op jit(solution)/shard_map/ppermute | solution.py:455
  52.7 1.3 collective-permute-start.11
  54.0 10.5 %collective-permute-start.12 = (bf16[38,32,128]{2,1,0:T(8,128)(2,1)S(1)}, bf16[38,32,128]{2,1,0:T(8,128)(2,1)S(1)}, u32[]{:S(2)}, u32[]{:S(2)}) collective-permute-start(bf16[38,32,128]{2,1,0:T(8,128)(2,1)S(1)} %get-tuple-element.36), channel_id=1, source_target_pairs={{28,0},{16,8},{20,24},{60,32},{48,40},{52,56},{92,64},{80,72},{84,... | collective-permute-start | bytes 933896 | tf_op jit(solution)/shard_map/ppermute | solution.py:455
  64.5 3.8 %collective-permute-done.12.refs_7_.refs_3_ = bf16[38,32,128]{2,1,0:T(8,128)(2,1)S(1)} collective-permute-done((bf16[38,32,128]{2,1,0:T(8,128)(2,1)S(1)}, bf16[38,32,128]{2,1,0:T(8,128)(2,1)S(1)}, u32[]{:S(2)}, u32[]{:S(2)}) %collective-permute-start.12) | collective-permute-done | bytes 311328 | tf_op jit(solution)/shard_map/ppermute | solution.py:455
  68.4 0.7 collective-permute-start.15
  69.1 0.7 collective-permute-start.16
  70.0 0.6 sweep.4
  70.5 0.7 collective-permute-start.17
  71.2 0.7 collective-permute-start.19
  71.9 0.7 collective-permute-start.18
  72.6 0.7 sweep.5
  73.3 0.7 collective-permute-start.20
  74.0 0.7 collective-permute-start.22
  74.7 0.7 collective-permute-start.21
  75.4 0.6 sweep.6
  76.0 0.7 collective-permute-start.23
  76.7 0.7 collective-permute-start.25
  77.3 0.7 collective-permute-start.24
  78.0 6.3 %sweep.7 = (bf16[2,16,32,128]{3,2,1,0:T(8,128)(2,1)S(1)}, bf16[2,16,32,128]{3,2,1,0:T(8,128)(2,1)S(1)}, bf16[2,16,32,128]{3,2,1,0:T(8,128)(2,1)S(1)}, bf16[2,16,...) custom-call(s32[6]{0:T(128)S(1)} %stack.27.info_ref, ...), custom_call_target="tpu_custom_call" | custom-call | tf_op jit(solution)/shard_map/sweep/pallas_call | solution.py:414
  84.3 0.7 collective-permute-start.26
  85.0 0.7 collective-permute-start.27
  85.7 0.7 collective-permute-start.28
  86.4 0.7 collective-permute-start.29
  87.1 0.7 collective-permute-start.30
  87.8 1.3 collective-permute-start.31
  89.1 1.3 collective-permute-start.32
  90.4 1.3 collective-permute-start.33
  91.7 54.5 %collective-permute-done.31.refs_5_ = bf16[2,16,32,128]{3,2,1,0:T(8,128)(2,1)S(1)} collective-permute-done((bf16[2,16,32,128]{3,2,1,0:T(8,128)(2,1)S(1)}, bf16[2,16,32,128]{3,2,1,0:T(8,128)(2,1)S(1)}, u32[]{:S(2)}, u32[]{:S(2)}) %collective-permute-start.31) | collective-permute-done | bytes 262176 | tf_op jit(solution)/shard_map/ppermute | solution.py:488
  146.2 9.1 %collective-permute-done.32.refs_6_ = bf16[2,16,32,128]{3,2,1,0:T(8,128)(2,1)S(1)} collective-permute-done((bf16[2,16,32,128]{3,2,1,0:T(8,128)(2,1)S(1)}, bf16[2,16,32,128]{3,2,1,0:T(8,128)(2,1)S(1)}, u32[]{:S(2)}, u32[]{:S(2)}) %collective-permute-start.32) | collective-permute-done | bytes 262176 | tf_op jit(solution)/shard_map/ppermute | solution.py:488
  155.2 5.5 %collective-permute-done.33.refs_7_ = bf16[2,16,32,128]{3,2,1,0:T(8,128)(2,1)S(1)} collective-permute-done((bf16[2,16,32,128]{3,2,1,0:T(8,128)(2,1)S(1)}, bf16[2,16,32,128]{3,2,1,0:T(8,128)(2,1)S(1)}, u32[]{:S(2)}, u32[]{:S(2)}) %collective-permute-start.33) | collective-permute-done | bytes 262176 | tf_op jit(solution)/shard_map/ppermute | solution.py:488
  160.8 2.5 %finish.1 = f32[3072,128]{1,0:T(8,128)} custom-call(s32[6]{0:T(128)S(1)} %stack.27.info_ref, bf16[2,16,32,128]{3,2,1,0:T(8,128)(2,1)S(1)} %collective-permute-done.26.refs_0_, bf16[2,16,32,128]{3,2,1,0:T(8,128)(2,1)S(1)} %collective-permute-done.27.refs_1_, bf16[2,16,32,128]{3,2,1,0:T(8,128)(2,1)S(1)} %collective-permute-done.28.refs_2_, ...), custom_call_target="tpu_custom_call" | custom-call | tf_op jit(solution)/shard_map/finish/pallas_call | solution.py:378
  (42 shorter events, 1.5 us)
Async XLA Ops:
  0.1 1.4 copy-start
  1.5 1.1 copy-start.1
  2.6 5.8 %copy-start.3 = (bf16[8,32,288]{2,1,0:T(8,128)(2,1)S(1)}, bf16[8,32,288]{2,1,0:T(8,128)(2,1)}, u32[]{:S(2)}) copy-start(bf16[8,32,288]{2,1,0:T(8,128)(2,1)} %here_ref.1) | copy-start | bytes 442372
  3.4 22.4 %copy-start.2 = (f32[3,32,16,128]{3,2,1,0:T(8,128)S(1)}, f32[3,32,16,128]{3,2,1,0:T(8,128)}, u32[]{:S(2)}) copy-start(f32[3,32,16,128]{3,2,1,0:T(8,128)} %param.4) | copy-start | bytes 2359300
  3.4 8.8 %collective-permute-start = (bf16[7,4,32,128]{3,2,1,0:T(8,128)(2,1)S(1)}, bf16[7,4,32,128]{3,2,1,0:T(8,128)(2,1)S(1)}, u32[]{:S(2)}, u32[]{:S(2)}) collective-permute-start(bf16[7,4,32,128]{3,2,1,0:T(8,128)(2,1)S(1)} %get-tuple-element.31), channel_id=1, source_target_pairs={{0,1},{1,2},{2,3},{4,5},{5,6},{6,7},{8,9},{9,10},{10,11},{12,13},{... | collective-permute-start | bytes 688136 | tf_op jit(solution)/shard_map/ppermute | solution.py:437
  7.1 8.4 %collective-permute-start.1 = (bf16[7,4,32,128]{3,2,1,0:T(8,128)(2,1)S(1)}, bf16[7,4,32,128]{3,2,1,0:T(8,128)(2,1)S(1)}, u32[]{:S(2)}, u32[]{:S(2)}) collective-permute-start(bf16[7,4,32,128]{3,2,1,0:T(8,128)(2,1)S(1)} %get-tuple-element.32), channel_id=1, source_target_pairs={{1,0},{2,1},{3,2},{5,4},{6,5},{7,6},{9,8},{10,9},{11,10},{13,12},{... | collective-permute-start | bytes 688136 | tf_op jit(solution)/shard_map/ppermute | solution.py:438
  8.5 3.8 %collective-permute-start.4 = (bf16[4,32,288]{2,1,0:T(8,128)(2,1)S(1)}, bf16[4,32,288]{2,1,0:T(8,128)(2,1)S(1)}, u32[]{:S(2)}, u32[]{:S(2)}) collective-permute-start(bf16[4,32,288]{2,1,0:T(8,128)(2,1)S(1)} %slice.3), channel_id=1, source_target_pairs={{4,0},{8,4},{12,8},{16,12},{20,16},{24,20},{28,24},{32,28},{36,32}... | collective-permute-start | bytes 221192 | tf_op jit(solution)/shard_map/ppermute | solution.py:439
  11.3 13.1 %collective-permute-start.3 = (bf16[4,32,288]{2,1,0:T(8,128)(2,1)S(1)}, bf16[4,32,288]{2,1,0:T(8,128)(2,1)S(1)}, u32[]{:S(2)}, u32[]{:S(2)}) collective-permute-start(bf16[4,32,288]{2,1,0:T(8,128)(2,1)S(1)} %slice.3), channel_id=1, source_target_pairs={{0,8},{1,9},{2,10},{3,11}} | collective-permute-start | bytes 221192 | tf_op jit(solution)/shard_map/ppermute | solution.py:442
  21.7 4.7 %collective-permute-start.5 = (bf16[38,32,128]{2,1,0:T(8,128)(2,1)}, bf16[38,32,128]{2,1,0:T(8,128)(2,1)S(1)}, u32[]{:S(2)}, u32[]{:S(2)}) collective-permute-start(bf16[38,32,128]{2,1,0:T(8,128)(2,1)} %get-tuple-element.33), channel_id=1, source_target_pairs={{0,0},{4,8},{8,24},{32,32},{36,40},{40,56},{64,64},{68,72},{72,88}... | collective-permute-start | bytes 933896 | tf_op jit(solution)/shard_map/ppermute | solution.py:455
  22.4 4.0 %collective-permute-start.6 = (bf16[38,32,128]{2,1,0:T(8,128)(2,1)}, bf16[38,32,128]{2,1,0:T(8,128)(2,1)S(1)}, u32[]{:S(2)}, u32[]{:S(2)}) collective-permute-start(bf16[38,32,128]{2,1,0:T(8,128)(2,1)} %get-tuple-element.34), channel_id=1, source_target_pairs={{4,0},{8,8},{12,24},{36,32},{40,40},{44,56},{68,64},{72,72},{76,88... | collective-permute-start | bytes 933896 | tf_op jit(solution)/shard_map/ppermute | solution.py:455
  23.1 3.3 %collective-permute-start.7 = (bf16[38,32,128]{2,1,0:T(8,128)(2,1)S(1)}, bf16[38,32,128]{2,1,0:T(8,128)(2,1)S(1)}, u32[]{:S(2)}, u32[]{:S(2)}) collective-permute-start(bf16[38,32,128]{2,1,0:T(8,128)(2,1)S(1)} %get-tuple-element.35), channel_id=1, source_target_pairs={{8,0},{12,8},{0,24},{40,32},{44,40},{32,56},{72,64},{76,72},{64,88... | collective-permute-start | bytes 933896 | tf_op jit(solution)/shard_map/ppermute | solution.py:455
  23.8 2.6 %collective-permute-start.8 = (bf16[38,32,128]{2,1,0:T(8,128)(2,1)S(1)}, bf16[38,32,128]{2,1,0:T(8,128)(2,1)S(1)}, u32[]{:S(2)}, u32[]{:S(2)}) collective-permute-start(bf16[38,32,128]{2,1,0:T(8,128)(2,1)S(1)} %get-tuple-element.36), channel_id=1, source_target_pairs={{12,0},{0,8},{4,24},{44,32},{32,40},{36,56},{76,64},{64,72},{68,88... | collective-permute-start | bytes 933896 | tf_op jit(solution)/shard_map/ppermute | solution.py:455
  24.5 1.3 collective-permute-start.2
  26.7 43.3 %collective-permute-start.13 = (bf16[112,32,128]{2,1,0:T(8,128)(2,1)S(1)}, bf16[112,32,128]{2,1,0:T(8,128)(2,1)S(1)}, u32[]{:S(2)}, u32[]{:S(2)}) collective-permute-start(bf16[112,32,128]{2,1,0:T(8,128)(2,1)S(1)} %get-tuple-element.38), channel_id=1, source_target_pairs={{0,1},{1,2},{2,3},{8,9},{9,10},{10,11},{24,25},{25,26},{26,27},{32... | collective-permute-start | bytes 2752520 | tf_op jit(solution)/shard_map/ppermute | solution.py:469
  27.4 42.6 %collective-permute-start.14 = (bf16[112,32,128]{2,1,0:T(8,128)(2,1)S(1)}, bf16[112,32,128]{2,1,0:T(8,128)(2,1)S(1)}, u32[]{:S(2)}, u32[]{:S(2)}) collective-permute-start(bf16[112,32,128]{2,1,0:T(8,128)(2,1)S(1)} %get-tuple-element.39), channel_id=1, source_target_pairs={{1,0},{2,1},{3,2},{9,8},{10,9},{11,10},{25,24},{26,25},{27,26},{33... | collective-permute-start | bytes 2752520 | tf_op jit(solution)/shard_map/ppermute | solution.py:469
  28.1 25.9 %collective-permute-start.9 = (bf16[38,32,128]{2,1,0:T(8,128)(2,1)}, bf16[38,32,128]{2,1,0:T(8,128)(2,1)S(1)}, u32[]{:S(2)}, u32[]{:S(2)}) collective-permute-start(bf16[38,32,128]{2,1,0:T(8,128)(2,1)} %get-tuple-element.33), channel_id=1, source_target_pairs={{16,0},{20,8},{24,24},{48,32},{52,40},{56,56},{80,64},{84,72},{88,... | collective-permute-start | bytes 933896 | tf_op jit(solution)/shard_map/ppermute | solution.py:455
  28.8 35.6 %collective-permute-start.10 = (bf16[38,32,128]{2,1,0:T(8,128)(2,1)}, bf16[38,32,128]{2,1,0:T(8,128)(2,1)S(1)}, u32[]{:S(2)}, u32[]{:S(2)}) collective-permute-start(bf16[38,32,128]{2,1,0:T(8,128)(2,1)} %get-tuple-element.34), channel_id=1, source_target_pairs={{20,0},{24,8},{28,24},{52,32},{56,40},{60,56},{84,64},{88,72},{92,... | collective-permute-start | bytes 933896 | tf_op jit(solution)/shard_map/ppermute | solution.py:455
  52.7 11.8 %collective-permute-start.11 = (bf16[38,32,128]{2,1,0:T(8,128)(2,1)S(1)}, bf16[38,32,128]{2,1,0:T(8,128)(2,1)S(1)}, u32[]{:S(2)}, u32[]{:S(2)}) collective-permute-start(bf16[38,32,128]{2,1,0:T(8,128)(2,1)S(1)} %get-tuple-element.35), channel_id=1, source_target_pairs={{24,0},{28,8},{16,24},{56,32},{60,40},{48,56},{88,64},{92,72},{80,... | collective-permute-start | bytes 933896 | tf_op jit(solution)/shard_map/ppermute | solution.py:455
  54.0 14.3 %collective-permute-start.12 = (bf16[38,32,128]{2,1,0:T(8,128)(2,1)S(1)}, bf16[38,32,128]{2,1,0:T(8,128)(2,1)S(1)}, u32[]{:S(2)}, u32[]{:S(2)}) collective-permute-start(bf16[38,32,128]{2,1,0:T(8,128)(2,1)S(1)} %get-tuple-element.36), channel_id=1, source_target_pairs={{28,0},{16,8},{20,24},{60,32},{48,40},{52,56},{92,64},{80,72},{84,... | collective-permute-start | bytes 933896 | tf_op jit(solution)/shard_map/ppermute | solution.py:455
  68.4 1.6 collective-permute-start.15
  69.1 0.9 collective-permute-start.16
  70.5 2.1 %collective-permute-start.17 = (f32[16,32,128]{2,1,0:T(8,128)S(1)}, f32[16,32,128]{2,1,0:T(8,128)S(1)}, u32[]{:S(2)}, u32[]{:S(2)}) collective-permute-start(f32[16,32,128]{2,1,0:T(8,128)S(1)} %get-tuple-element.43), channel_id=1, source_target_pairs={{0,32},{1,33},{2,34},{3,35},{8,40},{9,41},{10,42},{11,43},{24,56},... | collective-permute-start | bytes 786440 | tf_op jit(solution)/shard_map/ppermute | solution.py:469
  71.2 1.4 collective-permute-start.19
  71.9 0.7 collective-permute-start.18
  73.3 2.1 %collective-permute-start.20 = (f32[16,32,128]{2,1,0:T(8,128)S(1)}, f32[16,32,128]{2,1,0:T(8,128)S(1)}, u32[]{:S(2)}, u32[]{:S(2)}) collective-permute-start(f32[16,32,128]{2,1,0:T(8,128)S(1)} %get-tuple-element.45), channel_id=1, source_target_pairs={{32,64},{33,65},{34,66},{35,67},{40,72},{41,73},{42,74},{43,75},{5... | collective-permute-start | bytes 786440 | tf_op jit(solution)/shard_map/ppermute | solution.py:469
  74.0 1.4 collective-permute-start.22
  74.7 0.7 collective-permute-start.21
  76.0 2.1 %collective-permute-start.23 = (f32[16,32,128]{2,1,0:T(8,128)S(1)}, f32[16,32,128]{2,1,0:T(8,128)S(1)}, u32[]{:S(2)}, u32[]{:S(2)}) collective-permute-start(f32[16,32,128]{2,1,0:T(8,128)S(1)} %get-tuple-element.47), channel_id=1, source_target_pairs={{64,96},{65,97},{66,98},{67,99},{72,104},{73,105},{74,106},{75,107... | collective-permute-start | bytes 786440 | tf_op jit(solution)/shard_map/ppermute | solution.py:469
  76.7 1.4 collective-permute-start.25
  77.3 0.7 collective-permute-start.24
  84.3 3.4 %collective-permute-start.26 = (bf16[2,16,32,128]{3,2,1,0:T(8,128)(2,1)S(1)}, bf16[2,16,32,128]{3,2,1,0:T(8,128)(2,1)S(1)}, u32[]{:S(2)}, u32[]{:S(2)}) collective-permute-start(bf16[2,16,32,128]{3,2,1,0:T(8,128)(2,1)S(1)} %get-tuple-element.49), channel_id=1, source_target_pairs={{0,0},{8,4},{24,8},{32,32},{40,36},{56,40},{64,64},{72,68},{88,72}... | collective-permute-start | bytes 786440 | tf_op jit(solution)/shard_map/ppermute | solution.py:488
  85.0 4.1 %collective-permute-start.27 = (bf16[2,16,32,128]{3,2,1,0:T(8,128)(2,1)S(1)}, bf16[2,16,32,128]{3,2,1,0:T(8,128)(2,1)S(1)}, u32[]{:S(2)}, u32[]{:S(2)}) collective-permute-start(bf16[2,16,32,128]{3,2,1,0:T(8,128)(2,1)S(1)} %get-tuple-element.50), channel_id=1, source_target_pairs={{0,4},{8,8},{24,12},{32,36},{40,40},{56,44},{64,68},{72,72},{88,76... | collective-permute-start | bytes 786440 | tf_op jit(solution)/shard_map/ppermute | solution.py:488
  85.7 4.7 %collective-permute-start.28 = (bf16[2,16,32,128]{3,2,1,0:T(8,128)(2,1)S(1)}, bf16[2,16,32,128]{3,2,1,0:T(8,128)(2,1)S(1)}, u32[]{:S(2)}, u32[]{:S(2)}) collective-permute-start(bf16[2,16,32,128]{3,2,1,0:T(8,128)(2,1)S(1)} %get-tuple-element.51), channel_id=1, source_target_pairs={{0,8},{8,12},{24,0},{32,40},{40,44},{56,32},{64,72},{72,76},{88,64... | collective-permute-start | bytes 786440 | tf_op jit(solution)/shard_map/ppermute | solution.py:488
  86.4 5.3 %collective-permute-start.29 = (bf16[2,16,32,128]{3,2,1,0:T(8,128)(2,1)S(1)}, bf16[2,16,32,128]{3,2,1,0:T(8,128)(2,1)S(1)}, u32[]{:S(2)}, u32[]{:S(2)}) collective-permute-start(bf16[2,16,32,128]{3,2,1,0:T(8,128)(2,1)S(1)} %get-tuple-element.52), channel_id=1, source_target_pairs={{0,12},{8,0},{24,4},{32,44},{40,32},{56,36},{64,76},{72,64},{88,68... | collective-permute-start | bytes 786440 | tf_op jit(solution)/shard_map/ppermute | solution.py:488
  87.1 4.6 %collective-permute-start.30 = (bf16[2,16,32,128]{3,2,1,0:T(8,128)(2,1)S(1)}, bf16[2,16,32,128]{3,2,1,0:T(8,128)(2,1)S(1)}, u32[]{:S(2)}, u32[]{:S(2)}) collective-permute-start(bf16[2,16,32,128]{3,2,1,0:T(8,128)(2,1)S(1)} %get-tuple-element.53), channel_id=1, source_target_pairs={{0,16},{8,20},{24,24},{32,48},{40,52},{56,56},{64,80},{72,84},{88,... | collective-permute-start | bytes 786440 | tf_op jit(solution)/shard_map/ppermute | solution.py:488
  87.8 58.4 %collective-permute-start.31 = (bf16[2,16,32,128]{3,2,1,0:T(8,128)(2,1)S(1)}, bf16[2,16,32,128]{3,2,1,0:T(8,128)(2,1)S(1)}, u32[]{:S(2)}, u32[]{:S(2)}) collective-permute-start(bf16[2,16,32,128]{3,2,1,0:T(8,128)(2,1)S(1)} %get-tuple-element.54), channel_id=1, source_target_pairs={{0,20},{8,24},{24,28},{32,52},{40,56},{56,60},{64,84},{72,88},{88,... | collective-permute-start | bytes 786440 | tf_op jit(solution)/shard_map/ppermute | solution.py:488
  89.1 66.1 %collective-permute-start.32 = (bf16[2,16,32,128]{3,2,1,0:T(8,128)(2,1)S(1)}, bf16[2,16,32,128]{3,2,1,0:T(8,128)(2,1)S(1)}, u32[]{:S(2)}, u32[]{:S(2)}) collective-permute-start(bf16[2,16,32,128]{3,2,1,0:T(8,128)(2,1)S(1)} %get-tuple-element.55), channel_id=1, source_target_pairs={{0,24},{8,28},{24,16},{32,56},{40,60},{56,48},{64,88},{72,92},{88,... | collective-permute-start | bytes 786440 | tf_op jit(solution)/shard_map/ppermute | solution.py:488
  90.4 70.3 %collective-permute-start.33 = (bf16[2,16,32,128]{3,2,1,0:T(8,128)(2,1)S(1)}, bf16[2,16,32,128]{3,2,1,0:T(8,128)(2,1)S(1)}, u32[]{:S(2)}, u32[]{:S(2)}) collective-permute-start(bf16[2,16,32,128]{3,2,1,0:T(8,128)(2,1)S(1)} %get-tuple-element.56), channel_id=1, source_target_pairs={{0,28},{8,16},{24,20},{32,60},{40,48},{56,52},{64,92},{72,80},{88,... | collective-permute-start | bytes 786440 | tf_op jit(solution)/shard_map/ppermute | solution.py:488
